TPU v7x, 32 devices: a whole 2x2x4 slice. The times are simulated.
32 devices in a mesh: parts: 2 (over y), tm: 4 (over z), space: 4 (over x, core).
Axes of the slice: x: 2, y: 2, z: 4, core: 2. Of those that a mesh axis runs over, the one named last changes fastest.
Arguments:
- rhs: float32 [8, 16, 16, 1024], P(('parts', 'tm'), None, 'space'), parts along dimension 0, may hold values from -24 to 24
- diffusivity: float32 [32, 16, 1024], P('parts', 'space'), parts along dimension 0, may hold values from 0.5 to 2
- velocity: float32 [6], P('parts'), parts along dimension 0, may hold values from -1 to 1
Outputs:
- solution: float32 [8, 16, 16, 1024], P(('parts', 'tm'), None, 'space'), parts along dimension 0
There are 2 independent parts, one for each index of `parts`. A program takes and returns all parts, laid end to end along the dimension named above; each array names one. Nothing has to cross between parts.
All inputs are finite; a program needn't handle non-finite values.
Results may differ from a plain program's by a relative error of at most 0.0002.
Values sent between devices are 32-bit elements; how exact they have to be, the bound alone decides.
No kernel may reach another device: no remote copies, remote signals or barrier semaphores. Data moves between devices by JAX's collectives and lax.ppermute only.
A program may use at most 64 MiB of HBM per device.

v0:
```python
import math

import jax
import jax.numpy as jnp
from jax import lax
from jax.sharding import PartitionSpec as P

circ_alpha = 0.1
relax_weights = (
    1.0 / (1.0 - 0.5 * math.cos(math.pi / 8.0)),
    1.0 / (1.0 - 0.5 * math.cos(3.0 * math.pi / 8.0)),
    1.0 / (1.0 - 0.5 * math.cos(5.0 * math.pi / 8.0)),
    1.0 / (1.0 - 0.5 * math.cos(7.0 * math.pi / 8.0)),
)


def padded(shard, sides, width):
    for axis, dim in sides:
        size, length = (lax.axis_size(axis), shard.shape[dim])
        up = [(i, (i + 1) % size) for i in range(size - 1)]
        down = [(j, i) for i, j in up]
        last = lax.slice_in_dim(shard, length - width, length, axis=dim)
        initial = lax.slice_in_dim(shard, 0, width, axis=dim)
        before = lax.ppermute(last, axis, up)
        after = lax.ppermute(initial, axis, down)
        shard = jnp.concatenate([before, shard, after], axis=dim)
    return shard


def stencil(extended, diffusivity, diag_re, diag_im, velocity):
    center = extended[:, :, :, 1:-1, :]
    upper_y = extended[:, :, :, 2:, :]
    lower_y = extended[:, :, :, :-2, :]
    zero_z = jnp.zeros_like(center[:, :, :1])
    upper_z = jnp.concatenate([center[:, :, 1:], zero_z], axis=2)
    lower_z = jnp.concatenate([zero_z, center[:, :, :-1]], axis=2)
    zero_x = jnp.zeros_like(center[:, :, :, :, :1])
    upper_x = jnp.concatenate([center[:, :, :, :, 1:], zero_x], axis=4)
    lower_x = jnp.concatenate([zero_x, center[:, :, :, :, :-1]], axis=4)
    coefficient = diffusivity[None, None]
    half_velocity = 0.5 * velocity
    beside = (coefficient - half_velocity[0]) * upper_z + (coefficient + half_velocity[0]) * lower_z
    beside = (
        beside
        + (coefficient - half_velocity[1]) * upper_y
        + (coefficient + half_velocity[1]) * lower_y
    )
    beside = (
        beside
        + (coefficient - half_velocity[2]) * upper_x
        + (coefficient + half_velocity[2]) * lower_x
    )
    denominator = diag_re + 6.0 * diffusivity
    center_re = center[:, 0]
    center_im = center[:, 1]
    total_re = denominator * center_re - diag_im * center_im
    total_im = denominator * center_im + diag_im * center_re
    return jnp.stack([total_re, total_im], axis=1) - beside


def divide(residual, diffusivity, diag_re, diag_im):
    denominator = diag_re + 6.0 * diffusivity
    modulus = denominator * denominator + diag_im * diag_im
    residual_re = residual[:, 0]
    residual_im = residual[:, 1]
    quotient_re = (residual_re * denominator + residual_im * diag_im) / modulus
    quotient_im = (residual_im * denominator - residual_re * diag_im) / modulus
    return jnp.stack([quotient_re, quotient_im], axis=1)


def highest(left, right):
    return jnp.dot(left, right, precision=lax.Precision.HIGHEST, preferred_element_type=jnp.float32)


def twiddle(row_index, column_index, length):
    product = row_index[:, None] * column_index[None, :] % length
    phase_table = product.astype(jnp.float32) * (2.0 * math.pi / length)
    return (jnp.cos(phase_table), jnp.sin(phase_table))


def local(rhs, diffusivity, velocity):
    local_steps, depth, rows_y, rows_x = rhs.shape
    length = local_steps * lax.axis_size("tm")
    first_step = lax.axis_index("tm") * local_steps
    own_index = first_step + jnp.arange(local_steps, dtype=jnp.int32)
    log_alpha = math.log(circ_alpha) / length
    cell_count = depth * rows_y * rows_x
    scaled = (
        rhs.reshape(local_steps, cell_count)
        * jnp.exp(own_index.astype(jnp.float32) * log_alpha)[:, None]
    )
    regrouped = lax.all_to_all(scaled, "tm", split_axis=1, concat_axis=0, tiled=True)
    full_index = jnp.arange(length, dtype=jnp.int32)
    cosine_table, sine_table = twiddle(full_index, full_index, length)
    spectrum_re = highest(cosine_table, regrouped)
    spectrum_im = -highest(sine_table, regrouped)
    source_re, source_im = (
        lax.all_to_all(spectrum_re, "tm", split_axis=0, concat_axis=1, tiled=True),
        lax.all_to_all(spectrum_im, "tm", split_axis=0, concat_axis=1, tiled=True),
    )
    source = jnp.stack([source_re, source_im], axis=1).reshape(
        local_steps, 2, depth, rows_y, rows_x
    )
    phase_angle = own_index.astype(jnp.float32) * (2.0 * math.pi / length)
    shift_factor = circ_alpha ** (1.0 / length)
    diag_re = (1.0 - shift_factor * jnp.cos(phase_angle))[:, None, None, None]
    diag_im = (shift_factor * jnp.sin(phase_angle))[:, None, None, None]
    field = relax_weights[0] * divide(source, diffusivity, diag_re, diag_im)
    for weight in relax_weights[1:]:
        extended = padded(field, (("space", 3),), 1)
        applied = stencil(extended, diffusivity, diag_re, diag_im, velocity)
        field = field + weight * divide(source - applied, diffusivity, diag_re, diag_im)
    field_re = field[:, 0].reshape(local_steps, cell_count)
    field_im = field[:, 1].reshape(local_steps, cell_count)
    mixed_re, mixed_im = (
        lax.all_to_all(field_re, "tm", split_axis=1, concat_axis=0, tiled=True),
        lax.all_to_all(field_im, "tm", split_axis=1, concat_axis=0, tiled=True),
    )
    values = (highest(cosine_table, mixed_re) - highest(sine_table, mixed_im)) / length
    restored = lax.all_to_all(values, "tm", split_axis=0, concat_axis=1, tiled=True)
    result = restored * jnp.exp(-own_index.astype(jnp.float32) * log_alpha)[:, None]
    return result.reshape(local_steps, depth, rows_y, rows_x)


def solution(mesh):
    return jax.shard_map(
        local,
        mesh=mesh,
        in_specs=(P(("parts", "tm"), None, "space", None), P("parts", "space", None), P("parts")),
        out_specs=P(("parts", "tm"), None, "space", None),
        check_vma=False,
    )
```

profile of v0, /device:TPU:1, one launch (start us, length us, event | category | flops | bytes accessed | tf_op | source)
XLA Modules:
  0.0 120.3 jit_solution(13436231676874819901)
XLA Ops:
  0.0 1.0 broadcast_multiply_fusion
  1.4 12.0 %all_to_all.84 = f32[1,4,16384]{2,0,1:T(1,128)S(1)} all-to-all(f32[1,4,16384]{2,0,1:T(1,128)S(1)} %mul.497), channel_id=1, replica_groups=mesh['parts'=2,'tm'=4,'space'=4] {'tm'}, dimensions={1} | all-to-all | bytes 524288 | tf_op jit(solution)/shard_map/all_to_all | solution.py:92
  13.4 0.7 convolution_bitcast_fusion
  14.1 1.0 copy.4
  15.1 4.3 %all-to-all-start.1 = ((f32[4,1,16384]{2,1,0:T(1,128)}), f32[4,1,16384]{2,1,0:T(1,128)S(1)}, u32[]{:S(2)}, u32[]{:S(2)}) async-start(f32[4,1,16384]{2,1,0:T(1,128)} %copy.4), calls=%async_computation.1 | async-start | bytes 524288 | tf_op jit(solution)/shard_map/all_to_all | solution.py:98
  19.4 0.7 fusion.2
  20.1 1.0 copy.5
  21.1 4.0 %all-to-all-done.1 = f32[4,1,16384]{2,1,0:T(1,128)S(1)} async-done(((f32[4,1,16384]{2,1,0:T(1,128)}), f32[4,1,16384]{2,1,0:T(1,128)S(1)}, u32[]{:S(2)}, u32[]{:S(2)}) %all-to-all-start.1) | async-done | bytes 262176 | tf_op jit(solution)/shard_map/all_to_all | solution.py:98
  25.1 4.8 %all-to-all-start.2 = ((f32[4,1,16384]{2,1,0:T(1,128)}), f32[4,1,16384]{2,1,0:T(1,128)S(1)}, u32[]{:S(2)}, u32[]{:S(2)}) async-start(f32[4,1,16384]{2,1,0:T(1,128)} %copy.5), calls=%async_computation.2 | async-start | bytes 524288 | tf_op jit(solution)/shard_map/all_to_all | solution.py:99
  30.1 0.6 copy-done.4
  30.8 0.6 fusion.83
  31.4 0.7 reduce
  32.1 0.9 stack.75
  33.3 2.3 %all-to-all-done.2 = f32[4,1,16384]{2,1,0:T(1,128)S(1)} async-done(((f32[4,1,16384]{2,1,0:T(1,128)}), f32[4,1,16384]{2,1,0:T(1,128)S(1)}, u32[]{:S(2)}, u32[]{:S(2)}) %all-to-all-start.2) | async-done | bytes 262176 | tf_op jit(solution)/shard_map/all_to_all | solution.py:99
  35.6 0.7 reduce.1
  37.4 2.3 %fusion.38 = (f32[1,1,16,4,1024]{4,3,2,1,0:T(4,128)S(1)}, f32[1,1,16,4,1024]{4,3,2,1,0:T(4,128)S(1)}, f32[16,4,1024]{2,1,0:T(4,128)S(1)}, f32[16,4,1024]{2,1,0:T...) fusion(f32[16,4,1024]{2,1,0:T(4,128)S(1)} %squeeze.67, ...), kind=kLoop, calls=%fused_computation.79 | loop fusion | flops 1179648 | bytes 2883608 | tf_op jit(solution)/shard_map/stack | solution.py:68
  39.9 0.9 fusion.82
  40.8 1.0 subtract_bitcast_fusion.2
  41.7 1.2 fusion.80
  42.9 1.3 %fusion.81 = (f32[1,2,16,4,1023]{4,3,2,1,0:T(4,128)}, f32[1,2,16,4,1023]{4,3,2,1,0:T(4,128)}) fusion(f32[1,2,16,4,1024]{4,3,2,1,0:T(4,128)S(1)} %maximum_multiply_fusion), kind=kLoop, calls=%fused_computation.131 | loop fusion | bytes 2095104 | tf_op jit(solution)/shard_map/slice | solution.py:38
  44.2 5.9 %collective-permute-start = (f32[1,2,16,1,1024]{4,3,2,1,0:T(1,128)}, f32[1,2,16,1,1024]{4,3,2,1,0:T(1,128)S(1)}, u32[]{:S(2)}, u32[]{:S(2)}) collective-permute-start(f32[1,2,16,1,1024]{4,3,2,1,0:T(1,128)} %get-tuple-element.37), channel_id=1, source_target_pairs={{1,0},{2,1},{3,2},{5,4},{6,5},{7,6},{9,8},{10,9},{11,10},{13,12},{... | collective-permute-start | bytes 393224 | tf_op jit(solution)/shard_map/ppermute | solution.py:25
  50.2 3.0 %collective-permute-start.1 = (f32[1,2,16,1,1024]{4,3,2,1,0:T(1,128)}, f32[1,2,16,1,1024]{4,3,2,1,0:T(1,128)}, u32[]{:S(2)}, u32[]{:S(2)}) collective-permute-start(f32[1,2,16,1,1024]{4,3,2,1,0:T(1,128)} %get-tuple-element.38), channel_id=1, source_target_pairs={{0,1},{1,2},{2,3},{4,5},{5,6},{6,7},{8,9},{9,10},{10,11},{12,13},{... | collective-permute-start | bytes 393224 | tf_op jit(solution)/shard_map/ppermute | solution.py:24
  53.3 1.9 %stack.76 = f32[1,1,16,4,1024]{4,3,2,1,0:T(4,128)} reshape(f32[4,16384]{1,0:T(4,128)} %copy-done.1) | data formatting | bytes 524288 | tf_op jit(solution)/shard_map/stack | solution.py:101
  55.1 1.0 constant_dynamic-update-slice_fusion
  56.2 2.8 %fusion.24 = f32[1,2,16,4,1024]{4,3,2,1,0:T(4,128)S(1)} fusion(f32[1,2,16,4,1024]{4,3,2,1,0:T(4,128)S(1)} %constant_dynamic-update-slice_fusion, f32[1,2,16,4,1024]{4,3,2,1,0:T(4,128)S(1)} %maximum_multiply_fusion, f32[1,2,16,1,1024]{4,3,2,1,0:T(1,128)} %collective-permute-done.1, f32[1,2,16,1,1024]{4,3,2,1,0:T(1,128)S(1)} %collective-permute-done, ...), kind=kLoop, calls=%fused_computation.32 | loop fusion | flops 2097152 | bytes 5962752 | tf_op jit(solution)/shard_map/sub | solution.py:112
  60.5 1.9 %collective-permute-start.2 = (f32[1,2,16,1,1024]{4,3,2,1,0:T(1,128)S(1)}, f32[1,2,16,1,1024]{4,3,2,1,0:T(1,128)S(1)}, u32[]{:S(2)}, u32[]{:S(2)}) collective-permute-start(f32[1,2,16,1,1024]{4,3,2,1,0:T(1,128)S(1)} %get-tuple-element.31), channel_id=1, source_target_pairs={{1,0},{2,1},{3,2},{5,4},{6,5},{7,6},{9,8},{10,9},{11,10},{13,12},{... | collective-permute-start | bytes 393224 | tf_op jit(solution)/shard_map/ppermute | solution.py:25
  62.4 3.8 %collective-permute-start.3 = (f32[1,2,16,1,1024]{4,3,2,1,0:T(1,128)S(1)}, f32[1,2,16,1,1024]{4,3,2,1,0:T(1,128)S(1)}, u32[]{:S(2)}, u32[]{:S(2)}) collective-permute-start(f32[1,2,16,1,1024]{4,3,2,1,0:T(1,128)S(1)} %get-tuple-element.32), channel_id=1, source_target_pairs={{0,1},{1,2},{2,3},{4,5},{5,6},{6,7},{8,9},{9,10},{10,11},{12,13},{... | collective-permute-start | bytes 393224 | tf_op jit(solution)/shard_map/ppermute | solution.py:24
  66.8 1.2 %collective-permute-done.3 = f32[1,2,16,1,1024]{4,3,2,1,0:T(1,128)S(1)} collective-permute-done((f32[1,2,16,1,1024]{4,3,2,1,0:T(1,128)S(1)}, f32[1,2,16,1,1024]{4,3,2,1,0:T(1,128)S(1)}, u32[]{:S(2)}, u32[]{:S(2)}) %collective-permute-start.3) | collective-permute-done | bytes 131104 | tf_op jit(solution)/shard_map/ppermute | solution.py:24
  68.0 1.2 %fusion.16 = f32[1,2,16,4,1024]{4,3,2,1,0:T(4,128)S(1)} fusion(f32[1,2,16,4,1024]{4,3,2,1,0:T(4,128)S(1)} %constant_dynamic-update-slice_fusion, f32[1,2,16,4,1024]{4,3,2,1,0:T(4,128)S(1)} %fusion.27, f32[1,2,16,1,1024]{4,3,2,1,0:T(1,128)S(1)} %collective-permute-done.3, f32[1,2,16,1,1024]{4,3,2,1,0:T(1,128)S(1)} %collective-permute-done.2, ...), kind=kLoop, calls=%fused_computation.22 | loop fusion | flops 2097152 | bytes 5962752 | tf_op jit(solution)/shard_map/sub | solution.py:112
  70.8 1.9 %collective-permute-start.4 = (f32[1,2,16,1,1024]{4,3,2,1,0:T(1,128)S(1)}, f32[1,2,16,1,1024]{4,3,2,1,0:T(1,128)S(1)}, u32[]{:S(2)}, u32[]{:S(2)}) collective-permute-start(f32[1,2,16,1,1024]{4,3,2,1,0:T(1,128)S(1)} %get-tuple-element.25), channel_id=1, source_target_pairs={{1,0},{2,1},{3,2},{5,4},{6,5},{7,6},{9,8},{10,9},{11,10},{13,12},{... | collective-permute-start | bytes 393224 | tf_op jit(solution)/shard_map/ppermute | solution.py:25
  72.7 4.4 %collective-permute-start.5 = (f32[1,2,16,1,1024]{4,3,2,1,0:T(1,128)S(1)}, f32[1,2,16,1,1024]{4,3,2,1,0:T(1,128)S(1)}, u32[]{:S(2)}, u32[]{:S(2)}) collective-permute-start(f32[1,2,16,1,1024]{4,3,2,1,0:T(1,128)S(1)} %get-tuple-element.26), channel_id=1, source_target_pairs={{0,1},{1,2},{2,3},{4,5},{5,6},{6,7},{8,9},{9,10},{10,11},{12,13},{... | collective-permute-start | bytes 393224 | tf_op jit(solution)/shard_map/ppermute | solution.py:24
  77.3 0.5 collective-permute-done.4
  77.8 1.2 %collective-permute-done.5 = f32[1,2,16,1,1024]{4,3,2,1,0:T(1,128)S(1)} collective-permute-done((f32[1,2,16,1,1024]{4,3,2,1,0:T(1,128)S(1)}, f32[1,2,16,1,1024]{4,3,2,1,0:T(1,128)S(1)}, u32[]{:S(2)}, u32[]{:S(2)}) %collective-permute-start.5) | collective-permute-done | bytes 131104 | tf_op jit(solution)/shard_map/ppermute | solution.py:24
  79.0 1.2 %fusion.8 = f32[1,2,16,4,1024]{4,3,2,1,0:T(4,128)S(1)} fusion(f32[1,2,16,4,1024]{4,3,2,1,0:T(4,128)S(1)} %constant_dynamic-update-slice_fusion, f32[1,2,16,4,1024]{4,3,2,1,0:T(4,128)S(1)} %fusion.28, f32[1,2,16,1,1024]{4,3,2,1,0:T(1,128)S(1)} %collective-permute-done.5, f32[1,2,16,1,1024]{4,3,2,1,0:T(1,128)S(1)} %collective-permute-done.4, ...), kind=kLoop, calls=%fused_computation.12 | loop fusion | flops 2097152 | bytes 5962752 | tf_op jit(solution)/shard_map/sub | solution.py:112
  80.5 0.6 fusion.29
  81.1 1.1 all_to_all.70
  82.2 3.4 %all-to-all-start.3 = ((f32[1,4,16384]{2,0,1:T(1,128)}), f32[1,4,16384]{2,0,1:T(1,128)S(1)}, u32[]{:S(2)}, u32[]{:S(2)}) async-start(f32[1,4,16384]{2,0,1:T(1,128)} %all_to_all.70), calls=%async_computation.3 | async-start | bytes 524288 | tf_op jit(solution)/shard_map/all_to_all | solution.py:116
  85.6 1.1 all_to_all.73
  86.7 5.9 %all-to-all-done.3 = f32[1,4,16384]{2,0,1:T(1,128)S(1)} async-done(((f32[1,4,16384]{2,0,1:T(1,128)}), f32[1,4,16384]{2,0,1:T(1,128)S(1)}, u32[]{:S(2)}, u32[]{:S(2)}) %all-to-all-start.3) | async-done | bytes 262176 | tf_op jit(solution)/shard_map/all_to_all | solution.py:116
  92.5 3.4 %all-to-all-start.4 = ((f32[1,4,16384]{2,0,1:T(1,128)}), f32[1,4,16384]{2,0,1:T(1,128)S(1)}, u32[]{:S(2)}, u32[]{:S(2)}) async-start(f32[1,4,16384]{2,0,1:T(1,128)} %all_to_all.73), calls=%async_computation.4 | async-start | bytes 524288 | tf_op jit(solution)/shard_map/all_to_all | solution.py:117
  95.9 0.7 fusion.32
  96.6 7.7 %all-to-all-done.4 = f32[1,4,16384]{2,0,1:T(1,128)S(1)} async-done(((f32[1,4,16384]{2,0,1:T(1,128)}), f32[1,4,16384]{2,0,1:T(1,128)S(1)}, u32[]{:S(2)}, u32[]{:S(2)}) %all-to-all-start.4) | async-done | bytes 262176 | tf_op jit(solution)/shard_map/all_to_all | solution.py:117
  104.3 0.7 fusion.1
  105.1 1.0 copy.6
  106.0 3.4 %all-to-all-start.5 = ((f32[4,1,16384]{2,1,0:T(1,128)}), f32[4,1,16384]{2,1,0:T(1,128)S(1)}, u32[]{:S(2)}, u32[]{:S(2)}) async-start(f32[4,1,16384]{2,1,0:T(1,128)} %copy.6), calls=%async_computation.5 | async-start | bytes 524288 | tf_op jit(solution)/shard_map/all_to_all | solution.py:120
  109.5 9.1 %all-to-all-done.5 = f32[4,1,16384]{2,1,0:T(1,128)S(1)} async-done(((f32[4,1,16384]{2,1,0:T(1,128)}), f32[4,1,16384]{2,1,0:T(1,128)S(1)}, u32[]{:S(2)}, u32[]{:S(2)}) %all-to-all-start.5) | async-done | bytes 262176 | tf_op jit(solution)/shard_map/all_to_all | solution.py:120
  118.6 0.7 multiply_reduce_fusion
  119.3 0.9 mul.572
  (32 shorter events, 5.8 us)
Async XLA Ops:
  15.1 10.0 %all-to-all-start.1 = ((f32[4,1,16384]{2,1,0:T(1,128)}), f32[4,1,16384]{2,1,0:T(1,128)S(1)}, u32[]{:S(2)}, u32[]{:S(2)}) async-start(f32[4,1,16384]{2,1,0:T(1,128)} %copy.4), calls=%async_computation.1 | async-start | bytes 524288 | tf_op jit(solution)/shard_map/all_to_all | solution.py:98
  25.1 10.4 %all-to-all-start.2 = ((f32[4,1,16384]{2,1,0:T(1,128)}), f32[4,1,16384]{2,1,0:T(1,128)S(1)}, u32[]{:S(2)}, u32[]{:S(2)}) async-start(f32[4,1,16384]{2,1,0:T(1,128)} %copy.5), calls=%async_computation.2 | async-start | bytes 524288 | tf_op jit(solution)/shard_map/all_to_all | solution.py:99
  30.1 0.7 copy-start.4
  36.3 0.7 copy-start.1
  36.3 1.0 copy-start
  42.9 10.3 %copy-start.3 = (f32[1,1,16,4,1024]{4,3,2,1,0:T(4,128)S(1)}, f32[1,1,16,4,1024]{4,3,2,1,0:T(4,128)}, u32[]{:S(2)}) copy-start(f32[1,1,16,4,1024]{4,3,2,1,0:T(4,128)} %stack.75) | copy-start | bytes 786436
  44.2 11.9 %collective-permute-start = (f32[1,2,16,1,1024]{4,3,2,1,0:T(1,128)}, f32[1,2,16,1,1024]{4,3,2,1,0:T(1,128)S(1)}, u32[]{:S(2)}, u32[]{:S(2)}) collective-permute-start(f32[1,2,16,1,1024]{4,3,2,1,0:T(1,128)} %get-tuple-element.37), channel_id=1, source_target_pairs={{1,0},{2,1},{3,2},{5,4},{6,5},{7,6},{9,8},{10,9},{11,10},{13,12},{... | collective-permute-start | bytes 393224 | tf_op jit(solution)/shard_map/ppermute | solution.py:25
  50.2 6.0 %collective-permute-start.1 = (f32[1,2,16,1,1024]{4,3,2,1,0:T(1,128)}, f32[1,2,16,1,1024]{4,3,2,1,0:T(1,128)}, u32[]{:S(2)}, u32[]{:S(2)}) collective-permute-start(f32[1,2,16,1,1024]{4,3,2,1,0:T(1,128)} %get-tuple-element.38), channel_id=1, source_target_pairs={{0,1},{1,2},{2,3},{4,5},{5,6},{6,7},{8,9},{9,10},{10,11},{12,13},{... | collective-permute-start | bytes 393224 | tf_op jit(solution)/shard_map/ppermute | solution.py:24
  55.1 1.1 copy-start.2
  60.5 6.3 %collective-permute-start.2 = (f32[1,2,16,1,1024]{4,3,2,1,0:T(1,128)S(1)}, f32[1,2,16,1,1024]{4,3,2,1,0:T(1,128)S(1)}, u32[]{:S(2)}, u32[]{:S(2)}) collective-permute-start(f32[1,2,16,1,1024]{4,3,2,1,0:T(1,128)S(1)} %get-tuple-element.31), channel_id=1, source_target_pairs={{1,0},{2,1},{3,2},{5,4},{6,5},{7,6},{9,8},{10,9},{11,10},{13,12},{... | collective-permute-start | bytes 393224 | tf_op jit(solution)/shard_map/ppermute | solution.py:25
  62.4 5.6 %collective-permute-start.3 = (f32[1,2,16,1,1024]{4,3,2,1,0:T(1,128)S(1)}, f32[1,2,16,1,1024]{4,3,2,1,0:T(1,128)S(1)}, u32[]{:S(2)}, u32[]{:S(2)}) collective-permute-start(f32[1,2,16,1,1024]{4,3,2,1,0:T(1,128)S(1)} %get-tuple-element.32), channel_id=1, source_target_pairs={{0,1},{1,2},{2,3},{4,5},{5,6},{6,7},{8,9},{9,10},{10,11},{12,13},{... | collective-permute-start | bytes 393224 | tf_op jit(solution)/shard_map/ppermute | solution.py:24
  70.8 7.0 %collective-permute-start.4 = (f32[1,2,16,1,1024]{4,3,2,1,0:T(1,128)S(1)}, f32[1,2,16,1,1024]{4,3,2,1,0:T(1,128)S(1)}, u32[]{:S(2)}, u32[]{:S(2)}) collective-permute-start(f32[1,2,16,1,1024]{4,3,2,1,0:T(1,128)S(1)} %get-tuple-element.25), channel_id=1, source_target_pairs={{1,0},{2,1},{3,2},{5,4},{6,5},{7,6},{9,8},{10,9},{11,10},{13,12},{... | collective-permute-start | bytes 393224 | tf_op jit(solution)/shard_map/ppermute | solution.py:25
  72.7 6.3 %collective-permute-start.5 = (f32[1,2,16,1,1024]{4,3,2,1,0:T(1,128)S(1)}, f32[1,2,16,1,1024]{4,3,2,1,0:T(1,128)S(1)}, u32[]{:S(2)}, u32[]{:S(2)}) collective-permute-start(f32[1,2,16,1,1024]{4,3,2,1,0:T(1,128)S(1)} %get-tuple-element.26), channel_id=1, source_target_pairs={{0,1},{1,2},{2,3},{4,5},{5,6},{6,7},{8,9},{9,10},{10,11},{12,13},{... | collective-permute-start | bytes 393224 | tf_op jit(solution)/shard_map/ppermute | solution.py:24
  82.2 10.3 %all-to-all-start.3 = ((f32[1,4,16384]{2,0,1:T(1,128)}), f32[1,4,16384]{2,0,1:T(1,128)S(1)}, u32[]{:S(2)}, u32[]{:S(2)}) async-start(f32[1,4,16384]{2,0,1:T(1,128)} %all_to_all.70), calls=%async_computation.3 | async-start | bytes 524288 | tf_op jit(solution)/shard_map/all_to_all | solution.py:116
  92.5 11.8 %all-to-all-start.4 = ((f32[1,4,16384]{2,0,1:T(1,128)}), f32[1,4,16384]{2,0,1:T(1,128)S(1)}, u32[]{:S(2)}, u32[]{:S(2)}) async-start(f32[1,4,16384]{2,0,1:T(1,128)} %all_to_all.73), calls=%async_computation.4 | async-start | bytes 524288 | tf_op jit(solution)/shard_map/all_to_all | solution.py:117
  106.0 12.6 %all-to-all-start.5 = ((f32[4,1,16384]{2,1,0:T(1,128)}), f32[4,1,16384]{2,1,0:T(1,128)S(1)}, u32[]{:S(2)}, u32[]{:S(2)}) async-start(f32[4,1,16384]{2,1,0:T(1,128)} %copy.6), calls=%async_computation.5 | async-start | bytes 524288 | tf_op jit(solution)/shard_map/all_to_all | solution.py:120
where the time goes:
time: 122 us; the launch traced here: 120 us
  starting transfers between devices  40.4 us (33%)
  waiting for transfers between devices  32.3 us (26%)
  local copies, waits for them, and re-layouts  17.9 us (15%)
  other arithmetic  14.3 us (12%)
  blocking collectives  12 us (10%)
  matrix products  2.78 us (2%)
    all_to_all x1, blocking collectives, local(): lax.all_to_all(scaled, 'tm', split_axis=1, concat_axis=0, tiled=True)  12 us
    ppermute x3, starting transfers between devices, padded(): before = lax.ppermute(last, axis, up)  11.2 us
    ppermute x3, starting transfers between devices, padded(): after = lax.ppermute(initial, axis, down)  9.81 us
    all_to_all x1, waiting for transfers between devices, local(): lax.all_to_all(values, 'tm', split_axis=0, concat_axis=1, tiled=True)  9.12 us
    all_to_all x1, waiting for transfers between devices, local(): lax.all_to_all(field_im, 'tm', split_axis=1, concat_axis=0, tiled=True)  7.73 us
    all_to_all x1, waiting for transfers between devices, local(): lax.all_to_all(field_re, 'tm', split_axis=1, concat_axis=0, tiled=True)  5.85 us
    sub x3, other arithmetic, local(): source - applied  5.27 us
    all_to_all x1, starting transfers between devices, local(): lax.all_to_all(spectrum_im, 'tm', split_axis=0, concat_axis=1, tiled=True)  4.82 us
  transfers between devices with their start and end apart: 11, of which 9 were waited for; matrix products, arithmetic and copies ran while one was open for 7% of the time, Pallas kernels for 0%

commit v1 on v0

--- a/solution.py
+++ b/solution.py
@@ -1,8 +1,11 @@
+import functools
 import math
 
 import jax
 import jax.numpy as jnp
 from jax import lax
+from jax.experimental import pallas as pl
+from jax.experimental.pallas import tpu as pltpu
 from jax.sharding import PartitionSpec as P
 
 circ_alpha = 0.1
@@ -12,6 +15,391 @@
     1.0 / (1.0 - 0.5 * math.cos(5.0 * math.pi / 8.0)),
     1.0 / (1.0 - 0.5 * math.cos(7.0 * math.pi / 8.0)),
 )
+
+
+reach = len(relax_weights) - 1
+lanes = 128
+vmem = pl.BlockSpec(memory_space=pltpu.VMEM)
+smem = pl.BlockSpec(memory_space=pltpu.SMEM)
+
+
+def call(kernel, outs, *operands, specs=None, scratch=()):
+    return pl.pallas_call(
+        kernel,
+        out_shape=[jax.ShapeDtypeStruct(o, jnp.float32) for o in outs],
+        in_specs=specs or [vmem] * len(operands),
+        out_specs=[vmem] * len(outs),
+        scratch_shapes=scratch,
+    )(*operands)
+
+
+def column_mask(left, right, shape):
+    lane = lax.broadcasted_iota(jnp.int32, shape, 1)
+    keep_right = (lane < reach).astype(jnp.float32) * right
+    keep_left = (lane >= lanes - reach).astype(jnp.float32) * left
+    return keep_right, keep_left
+
+
+def pick_block(source, write, owner, owners, depth, rows, tiles):
+    total = owners * tiles
+    left_tile = jnp.maximum(owner * tiles - 1, 0)
+    right_tile = jnp.minimum((owner + 1) * tiles, total - 1)
+    left = (owner > 0).astype(jnp.float32)
+    right = (owner < owners - 1).astype(jnp.float32)
+    keep_right, keep_left = column_mask(left, right, (depth, lanes))
+    packed = None
+
+    def tile_at(row, tile):
+        return source[:, row, pl.ds(pl.multiple_of(tile * lanes, lanes), lanes)]
+
+    for row in range(rows):
+        for tile in range(tiles):
+            write(row * tiles + tile, tile_at(row, owner * tiles + tile))
+        halo = tile_at(row, right_tile) * keep_right + tile_at(row, left_tile) * keep_left
+        if row:
+            halo = pltpu.roll(halo, row * (lanes // rows), 1)
+        packed = halo if packed is None else packed + halo
+    write(rows * tiles, packed)
+
+
+def pack_kernel(tm, log_alpha, steps, rhs, *outs):
+    me = lax.axis_index(tm)
+    depth, rows, columns = rhs.shape
+    tiles = columns // steps // lanes
+    scale = jnp.exp(jnp.full((depth, lanes), me.astype(jnp.float32) * log_alpha, jnp.float32))
+    for ahead in range(steps):
+        out = outs[ahead]
+
+        def write(index, value, out=out):
+            out[index] = value * scale
+
+        pick_block(rhs, write, lax.rem(me + ahead, steps), steps, depth, rows, tiles)
+
+
+def pack(rhs, steps):
+    depth, rows, columns = rhs.shape
+    tiles = columns // steps // lanes
+    log_alpha = math.log(circ_alpha) / steps
+    kernel = functools.partial(pack_kernel, "tm", log_alpha, steps)
+    return call(kernel, [(rows * tiles + 1, depth, lanes)] * steps, rhs)
+
+
+def halo_pieces(block, ahead, rows, tiles):
+    first = (rows - reach) * tiles if ahead else 0
+    return [first + i for i in range(reach * tiles)] + [rows * tiles]
+
+
+def halo_kernel(rows, tiles, steps, *refs):
+    blocks, (up, down) = refs[:steps], refs[steps:]
+    piece = reach * tiles + 1
+    for step, block in enumerate(blocks):
+        for out, ahead in ((up, True), (down, False)):
+            for place, index in enumerate(halo_pieces(block, ahead, rows, tiles)):
+                out[step * piece + place] = block[index]
+
+
+def halos(blocks, rows, tiles):
+    depth = blocks[0].shape[1]
+    out = (len(blocks) * (reach * tiles + 1), depth, lanes)
+    kernel = functools.partial(halo_kernel, rows, tiles, len(blocks))
+    return call(kernel, [out, out], *blocks)
+
+
+def kappa_kernel(tm, rows, tiles, steps, kappa, own, up, down):
+    me = lax.axis_index(tm)
+    held = {}
+    depth = kappa.shape[0]
+
+    def write(index, value):
+        own[index] = value
+        held[index] = value
+
+    pick_block(kappa, write, me, steps, depth, rows, tiles)
+    for out, ahead in ((up, True), (down, False)):
+        for place, index in enumerate(halo_pieces(own, ahead, rows, tiles)):
+            out[place] = held[index]
+
+
+def row_piece(own, below, above, step, row, tile, rows, tiles):
+    piece = reach * tiles + 1
+    if row < reach:
+        source, base, local_row, place = below, step * piece, rows - reach + row, row
+        packed = base + reach * tiles
+    elif row < reach + rows:
+        source, base, local_row, place = own, 0, row - reach, row - reach
+        packed = rows * tiles
+    else:
+        source, base, local_row, place = above, step * piece, row - reach - rows, row - reach - rows
+        packed = base + reach * tiles
+    if tile < tiles:
+        return source[base + place * tiles + tile]
+    value = source[packed]
+    shift = local_row * (lanes // rows)
+    return pltpu.roll(value, lanes - shift, 1) if shift else value
+
+
+def frequencies(steps):
+    return [(k, 2 * k % steps != 0) for k in range(steps // 2 + 1)]
+
+
+def coefficient_kernel(tm, space, rows, tiles, steps, own, below, above, kappa, *outs):
+    me, slab = lax.axis_index(tm), lax.axis_index(space)
+    slabs = lax.axis_size(space)
+    depth = own.shape[1]
+    keep_right, keep_left = column_mask(
+        (me > 0).astype(jnp.float32), (me < steps - 1).astype(jnp.float32), (depth, lanes)
+    )
+    halo_mask = keep_right + keep_left
+    shift_factor = circ_alpha ** (1.0 / steps)
+    for row in range(rows + 2 * reach):
+        inside = None
+        if row < reach:
+            inside = (slab > 0).astype(jnp.float32)
+        elif row >= reach + rows:
+            inside = (slab < slabs - 1).astype(jnp.float32)
+        for tile in range(tiles + 1):
+            value = row_piece(own, below, above, 0, row, tile, rows, tiles)
+            kappa[row, tile] = value
+            mask = halo_mask if tile == tiles else None
+            if inside is not None:
+                mask = mask * inside if mask is not None else jnp.full((depth, lanes), inside)
+            place = 0
+            for k, is_complex in frequencies(steps):
+                phase = 2.0 * math.pi * k / steps
+                real = (1.0 - shift_factor * math.cos(phase)) + 6.0 * value
+                if is_complex:
+                    imag = shift_factor * math.sin(phase)
+                    inverse = 1.0 / (real * real + imag * imag)
+                    pair = (real * inverse, imag * inverse)
+                else:
+                    pair = (1.0 / real,)
+                for part in pair:
+                    outs[0][place, row, tile] = part if mask is None else part * mask
+                    place += 1
+
+
+def combine(terms):
+    total = None
+    for factor, value in terms:
+        if factor == 0.0:
+            continue
+        if total is None:
+            total = value if factor == 1.0 else factor * value
+        elif factor == 1.0:
+            total = total + value
+        elif factor == -1.0:
+            total = total - value
+        else:
+            total = total + factor * value
+    return total
+
+
+def exact(value):
+    return float(round(value)) if abs(value - round(value)) < 1e-12 else value
+
+
+def cosine(product, steps):
+    return exact(math.cos(2.0 * math.pi * (product % steps) / steps))
+
+
+def sine(product, steps):
+    return exact(math.sin(2.0 * math.pi * (product % steps) / steps))
+
+
+def solve_kernel(rows, tiles, steps, *refs):
+    blocks, refs = refs[:steps], refs[steps:]
+    below, above, kappa, inverse, velocity = refs[:5]
+    outs, (source, first, second) = refs[5 : 5 + steps], refs[5 + steps :]
+    depth = blocks[0].shape[1]
+    pad = 8
+    middle = pl.ds(pad, depth)
+    lane = lax.broadcasted_iota(jnp.int32, (depth, lanes), 1)
+    at_first, at_last = lane == 0, lane == lanes - 1
+    freqs = frequencies(steps)
+    fields = sum(2 if c else 1 for _, c in freqs)
+    half = [0.5 * velocity[j] for j in range(3)]
+    extended = rows + 2 * reach
+    wide = tiles + 1
+
+    zero = jnp.zeros((8, lanes), jnp.float32)
+    for ref in (first, second):
+        for field in range(fields):
+            for row in range(extended):
+                for tile in range(wide):
+                    ref[field, row, tile, pl.ds(0, 8), :] = zero
+                    ref[field, row, tile, pl.ds(pad + depth, 8), :] = zero
+
+    def divide(values, row, tile):
+        result, place = [], 0
+        for _, is_complex in freqs:
+            if is_complex:
+                re, im = values[place], values[place + 1]
+                p, q = inverse[place, row, tile], inverse[place + 1, row, tile]
+                result += [re * p + im * q, im * p - re * q]
+                place += 2
+            else:
+                result.append(values[place] * inverse[place, row, tile])
+                place += 1
+        return result
+
+    for row in range(extended):
+        for tile in range(wide):
+            if tile == tiles and not 1 <= row < extended - 1:
+                continue
+            held = [
+                row_piece(blocks[b], below, above, b, row, tile, rows, tiles)
+                for b in range(steps)
+            ]
+            values = []
+            for k, is_complex in freqs:
+                values.append(combine((cosine(k * b, steps), held[b]) for b in range(steps)))
+                if is_complex:
+                    values.append(combine((sine(k * b, steps), held[b]) for b in range(steps)))
+            quotients = divide(values, row, tile)
+            for field in range(fields):
+                source[field, row, tile] = values[field]
+                first[field, row, tile, middle, :] = relax_weights[0] * quotients[field]
+
+    def sweep(row, old, weight, last):
+        centers = [
+            [old[field, row, tile, middle, :] for tile in range(wide)] for field in range(fields)
+        ]
+        shifted_down = [[pltpu.roll(c, 1, 1) for c in line] for line in centers]
+        shifted_up = [[pltpu.roll(c, lanes - 1, 1) for c in line] for line in centers]
+        for tile in range(tiles if last else wide):
+            values = []
+            coefficient = kappa[row, tile]
+            for field in range(fields):
+                lower_x = jnp.where(
+                    at_first, shifted_down[field][(tile - 1) % wide], shifted_down[field][tile]
+                )
+                upper_x = jnp.where(
+                    at_last, shifted_up[field][(tile + 1) % wide], shifted_up[field][tile]
+                )
+                lower_z = old[field, row, tile, pl.ds(pad - 1, depth), :]
+                upper_z = old[field, row, tile, pl.ds(pad + 1, depth), :]
+                lower_y = old[field, row - 1, tile, middle, :]
+                upper_y = old[field, row + 1, tile, middle, :]
+                around = (lower_z + upper_z) + (lower_y + upper_y) + (lower_x + upper_x)
+                slope = (
+                    half[0] * (lower_z - upper_z)
+                    + half[1] * (lower_y - upper_y)
+                    + half[2] * (lower_x - upper_x)
+                )
+                values.append(source[field, row, tile] + (coefficient * around + slope))
+            quotients = divide(values, row, tile)
+            yield tile, [
+                (1.0 - weight) * centers[field][tile] + weight * quotients[field]
+                for field in range(fields)
+            ]
+
+    def middle_level(level, old, new):
+        def step(row, carry):
+            for tile, results in sweep(row, old, relax_weights[level], False):
+                for field in range(fields):
+                    new[field, row, tile, middle, :] = results[field]
+            return carry
+
+        lax.fori_loop(level, extended - level, step, 0)
+
+    middle_level(1, first, second)
+    middle_level(2, second, first)
+
+    def last_step(row, carry):
+        for tile, results in sweep(row, first, relax_weights[reach], True):
+            for ahead in range(steps):
+                terms, place = [], 0
+                for k, is_complex in freqs:
+                    factor = (2.0 if is_complex else 1.0) / steps
+                    terms.append((factor * cosine(k * ahead, steps), results[place]))
+                    place += 1
+                    if is_complex:
+                        terms.append((-factor * sine(k * ahead, steps), results[place]))
+                        place += 1
+                outs[ahead][(row - reach) * tiles + tile] = combine(terms)
+        return carry
+
+    lax.fori_loop(reach, reach + rows, last_step, 0)
+
+
+def unpack_kernel(tm, log_alpha, steps, *refs):
+    blocks, out = refs[:steps], refs[steps]
+    me = lax.axis_index(tm)
+    depth, rows, columns = out.shape
+    tiles = columns // steps // lanes
+    scale = jnp.exp(jnp.full((depth, lanes), me.astype(jnp.float32) * -log_alpha, jnp.float32))
+    for behind in range(steps):
+        owner = lax.rem(me - behind + steps, steps)
+        for row in range(rows):
+            for tile in range(tiles):
+                place = pl.multiple_of((owner * tiles + tile) * lanes, lanes)
+                out[:, row, pl.ds(place, lanes)] = blocks[behind][row * tiles + tile] * scale
+
+
+def exchange(blocks, steps):
+    moved = [
+        lax.ppermute(blocks[d], "tm", [(i, (i + d) % steps) for i in range(steps)])
+        for d in range(1, steps)
+    ]
+    return [blocks[0]] + moved
+
+
+def neighbours(up, down):
+    size = lax.axis_size("space")
+    ahead = [(i, i + 1) for i in range(size - 1)]
+    return (
+        lax.ppermute(up, "space", ahead),
+        lax.ppermute(down, "space", [(j, i) for i, j in ahead]),
+    )
+
+
+def fast_local(rhs, diffusivity, velocity):
+    _, depth, rows, columns = rhs.shape
+    steps = lax.axis_size("tm")
+    tiles = columns // steps // lanes
+    log_alpha = math.log(circ_alpha) / steps
+    extended, wide = rows + 2 * reach, tiles + 1
+    fields = steps
+    blocks = exchange(pack(rhs[0], steps), steps)
+    piece = (reach * tiles + 1, depth, lanes)
+    kappa_own, kappa_up, kappa_down = call(
+        functools.partial(kappa_kernel, "tm", rows, tiles, steps),
+        [(rows * tiles + 1, depth, lanes), piece, piece],
+        diffusivity,
+    )
+    kappa_below, kappa_above = neighbours(kappa_up, kappa_down)
+    kappa, inverse = call(
+        functools.partial(coefficient_kernel, "tm", "space", rows, tiles, steps),
+        [(extended, wide, depth, lanes), (fields, extended, wide, depth, lanes)],
+        kappa_own,
+        kappa_below,
+        kappa_above,
+    )
+    below, above = neighbours(*halos(blocks, rows, tiles))
+    padded = pltpu.VMEM((fields, extended, wide, depth + 16, lanes), jnp.float32)
+    results = call(
+        functools.partial(solve_kernel, rows, tiles, steps),
+        [(rows * tiles, depth, lanes)] * steps,
+        *blocks,
+        below,
+        above,
+        kappa,
+        inverse,
+        velocity,
+        specs=[vmem] * (steps + 4) + [smem],
+        scratch=[
+            pltpu.VMEM((fields, extended, wide, depth, lanes), jnp.float32),
+            padded,
+            padded,
+        ],
+    )
+    returned = exchange(results, steps)
+    (result,) = call(
+        functools.partial(unpack_kernel, "tm", log_alpha, steps),
+        [(depth, rows, columns)],
+        *returned,
+    )
+    return result[None]
 
 
 def padded(shard, sides, width):
@@ -78,7 +466,7 @@
     return (jnp.cos(phase_table), jnp.sin(phase_table))
 
 
-def local(rhs, diffusivity, velocity):
+def general_local(rhs, diffusivity, velocity):
     local_steps, depth, rows_y, rows_x = rhs.shape
     length = local_steps * lax.axis_size("tm")
     first_step = lax.axis_index("tm") * local_steps
@@ -122,6 +510,14 @@
     return result.reshape(local_steps, depth, rows_y, rows_x)
 
 
+def local(rhs, diffusivity, velocity):
+    steps = lax.axis_size("tm")
+    local_steps, depth, rows, columns = rhs.shape
+    if local_steps == 1 and rows >= reach and lanes % rows == 0 and columns % (steps * lanes) == 0:
+        return fast_local(rhs, diffusivity, velocity)
+    return general_local(rhs, diffusivity, velocity)
+
+
 def solution(mesh):
     return jax.shard_map(
         local,

time: 122 us -> 51 us (0.42)
  starting transfers between devices: 40.4 us -> 20.4 us
  waiting for transfers between devices: 32.3 us -> 12.3 us
  local copies, waits for them, and re-layouts: 17.9 us -> 2.7 us
  Pallas kernels: 0 us -> 14.8 us
  other arithmetic: 14.3 us -> 0 us
  blocking collectives: 12 us -> 0 us
  matrix products: 2.78 us -> 0 us
    all_to_all x5 -> x0, waiting for transfers between devices: 29 us -> none  [the longest x1 9.12 us: local(): lax.all_to_all(values, 'tm', split_axis=0, concat_axis=1, tiled=True)]
    all_to_all x5 -> x0, starting transfers between devices: 19.4 us -> none  [the longest x1 4.82 us: local(): lax.all_to_all(spectrum_im, 'tm', split_axis=0, concat_axis=1, tiled=True)]
    pallas_call x0 -> x6, Pallas kernels: none -> 14.8 us  [call(): pl.pallas_call(kernel, out_shape=[jax.ShapeDtypeStruct(o, jnp.float32) fo...]
    all_to_all x1 -> x0, blocking collectives: 12 us -> none  [local(): lax.all_to_all(scaled, 'tm', split_axis=1, concat_axis=0, tiled=True)]
    ppermute x6 -> x10, waiting for transfers between devices: 3.31 us -> 12.3 us  [the longest x6 8.53 us: exchange(): lax.ppermute(blocks[d], 'tm', [(i, (i + d) % steps) for i in range(steps)])]
    slice x11 -> x0, local copies, waits for them, and re-layouts: 5.72 us -> none  [the longest x3 2 us: stencil(): upper_x = jnp.concatenate([center[:, :, :, :, 1:], zero_x], axis=4)]
    sub x3 -> x0, other arithmetic: 5.27 us -> none  [local(): source - applied]
    all_to_all x5 -> x0, local copies, waits for them, and re-layouts: 5.04 us -> none  [the longest x1 1.06 us: local(): lax.all_to_all(field_im, 'tm', split_axis=1, concat_axis=0, tiled=True)]
  transfers between devices with their start and end apart: 11 -> 10, of which waited for: 9 -> 6; matrix products, arithmetic and copies ran while one was open for 7% -> 0% of each run, Pallas kernels for 0% -> 8%
where the time goes in v1:
time: 51 us; the launch traced here: 50.3 us
  starting transfers between devices  20.4 us (40%)
  Pallas kernels  14.8 us (29%)
  waiting for transfers between devices  12.3 us (24%)
  local copies, waits for them, and re-layouts  2.7 us (5%)
    pallas_call x6, Pallas kernels, call(): pl.pallas_call(kernel, out_shape=[jax.ShapeDtypeStruct(o, jnp.float32) fo...  14.8 us
    ppermute x6, starting transfers between devices, exchange(): lax.ppermute(blocks[d], 'tm', [(i, (i + d) % steps) for i in range(steps)])  9.15 us
    ppermute x6, waiting for transfers between devices, exchange(): lax.ppermute(blocks[d], 'tm', [(i, (i + d) % steps) for i in range(steps)])  8.53 us
    ppermute x2, starting transfers between devices, neighbours(): lax.ppermute(up, 'space', ahead)  7.43 us
    ppermute x2, starting transfers between devices, neighbours(): lax.ppermute(down, 'space', [(j, i) for i, j in ahead])  3.84 us
    ppermute x2, waiting for transfers between devices, neighbours(): lax.ppermute(down, 'space', [(j, i) for i, j in ahead])  3.76 us
    unnamed x20, local copies, waits for them, and re-layouts  2.7 us
  transfers between devices with their start and end apart: 10, of which 6 were waited for; matrix products, arithmetic and copies ran while one was open for 0% of the time, Pallas kernels for 8%

profile of v1, /device:TPU:1, one launch (start us, length us, event | category | flops | bytes accessed | tf_op | source)
XLA Modules:
  0.0 50.3 jit_solution(4831775970574033803)
XLA Ops:
  0.0 2.0 %shard_map.37 = (f32[9,16,128]{2,1,0:T(8,128)}, f32[9,16,128]{2,1,0:T(8,128)}, f32[9,16,128]{2,1,0:T(8,128)}, f32[9,16,128]{2,1,0:T(8,128)}) custom-call(f32[16,4,1024]{2,1,0:T(4,128)} %bitcast.2), custom_call_target="tpu_custom_call" | custom-call | tf_op jit(solution)/shard_map/pallas_call | solution.py:27
  2.0 2.1 %collective-permute-start = (f32[9,16,128]{2,1,0:T(8,128)}, f32[9,16,128]{2,1,0:T(8,128)S(1)}, u32[]{:S(2)}, u32[]{:S(2)}) collective-permute-start(f32[9,16,128]{2,1,0:T(8,128)} %get-tuple-element.21), channel_id=1, source_target_pairs={{0,4},{4,8},{8,12},{12,0},{1,5},{5,9},{9,13},{13,1},{2,6},{6,10},{... | collective-permute-start | bytes 221192 | tf_op jit(solution)/shard_map/ppermute | solution.py:341
  4.1 2.3 %collective-permute-start.1 = (f32[9,16,128]{2,1,0:T(8,128)}, f32[9,16,128]{2,1,0:T(8,128)S(1)}, u32[]{:S(2)}, u32[]{:S(2)}) collective-permute-start(f32[9,16,128]{2,1,0:T(8,128)} %get-tuple-element.22), channel_id=1, source_target_pairs={{0,8},{4,12},{8,0},{12,4},{1,9},{5,13},{9,1},{13,5},{2,10},{6,14},... | collective-permute-start | bytes 221192 | tf_op jit(solution)/shard_map/ppermute | solution.py:341
  6.5 1.1 %collective-permute-start.2 = (f32[9,16,128]{2,1,0:T(8,128)}, f32[9,16,128]{2,1,0:T(8,128)S(1)}, u32[]{:S(2)}, u32[]{:S(2)}) collective-permute-start(f32[9,16,128]{2,1,0:T(8,128)} %get-tuple-element.23), channel_id=1, source_target_pairs={{0,12},{4,0},{8,4},{12,8},{1,13},{5,1},{9,5},{13,9},{2,14},{6,2},{... | collective-permute-start | bytes 221192 | tf_op jit(solution)/shard_map/ppermute | solution.py:341
  7.5 0.6 %collective-permute-done.refs_1_ = f32[9,16,128]{2,1,0:T(8,128)S(1)} collective-permute-done((f32[9,16,128]{2,1,0:T(8,128)}, f32[9,16,128]{2,1,0:T(8,128)S(1)}, u32[]{:S(2)}, u32[]{:S(2)}) %collective-permute-start) | collective-permute-done | bytes 73760 | tf_op jit(solution)/shard_map/ppermute | solution.py:341
  8.2 0.0 copy-start
  8.2 4.1 %collective-permute-done.1.refs_2_ = f32[9,16,128]{2,1,0:T(8,128)S(1)} collective-permute-done((f32[9,16,128]{2,1,0:T(8,128)}, f32[9,16,128]{2,1,0:T(8,128)S(1)}, u32[]{:S(2)}, u32[]{:S(2)}) %collective-permute-start.1) | collective-permute-done | bytes 73760 | tf_op jit(solution)/shard_map/ppermute | solution.py:341
  12.3 0.0 copy-start.1
  12.3 0.0 collective-permute-done.2.refs_3_
  12.3 0.0 copy-start.2
  12.3 0.0 copy-done
  12.3 0.6 %copy-done.1 = f32[9,16,128]{2,1,0:T(8,128)} copy-done((f32[9,16,128]{2,1,0:T(8,128)}, f32[9,16,128]{2,1,0:T(8,128)S(1)}, u32[]{:S(2)}) %copy-start.1) | copy-done | bytes 73752
  12.9 0.0 copy-done.2
  12.9 1.8 %shard_map.38 = (f32[28,16,128]{2,1,0:T(8,128)}, f32[28,16,128]{2,1,0:T(8,128)}) custom-call(f32[9,16,128]{2,1,0:T(8,128)} %get-tuple-element.20.refs_0_, f32[9,16,128]{2,1,0:T(8,128)} %copy-done, f32[9,16,128]{2,1,0:T(8,128)} %copy-done.1, f32[9,16,128]{2,1,0:T(8,128)} %copy-done.2), custom_call_target="tpu_custom_call" | custom-call | tf_op jit(solution)/shard_map/pallas_call | solution.py:27
  14.8 3.8 %collective-permute-start.3 = (f32[28,16,128]{2,1,0:T(8,128)}, f32[28,16,128]{2,1,0:T(8,128)S(1)}, u32[]{:S(2)}, u32[]{:S(2)}) collective-permute-start(f32[28,16,128]{2,1,0:T(8,128)} %get-tuple-element.24), channel_id=1, source_target_pairs={{0,1},{1,2},{2,3},{4,5},{5,6},{6,7},{8,9},{9,10},{10,11},{12,13},{... | collective-permute-start | bytes 688136 | tf_op jit(solution)/shard_map/ppermute | solution.py:351
  18.6 1.9 %collective-permute-start.4 = (f32[28,16,128]{2,1,0:T(8,128)}, f32[28,16,128]{2,1,0:T(8,128)S(1)}, u32[]{:S(2)}, u32[]{:S(2)}) collective-permute-start(f32[28,16,128]{2,1,0:T(8,128)} %get-tuple-element.25), channel_id=1, source_target_pairs={{1,0},{2,1},{3,2},{5,4},{6,5},{7,6},{9,8},{10,9},{11,10},{13,12},{... | collective-permute-start | bytes 688136 | tf_op jit(solution)/shard_map/ppermute | solution.py:352
  20.5 1.7 %shard_map.39 = (f32[9,16,128]{2,1,0:T(8,128)}, f32[7,16,128]{2,1,0:T(8,128)}, f32[7,16,128]{2,1,0:T(8,128)}) custom-call(f32[16,4,1024]{2,1,0:T(4,128)} %kappa.1), custom_call_target="tpu_custom_call" | custom-call | tf_op jit(solution)/shard_map/pallas_call | solution.py:27
  22.2 3.6 %collective-permute-start.5 = (f32[7,16,128]{2,1,0:T(8,128)}, f32[7,16,128]{2,1,0:T(8,128)S(1)}, u32[]{:S(2)}, u32[]{:S(2)}) collective-permute-start(f32[7,16,128]{2,1,0:T(8,128)} %get-tuple-element.27), channel_id=1, source_target_pairs={{0,1},{1,2},{2,3},{4,5},{5,6},{6,7},{8,9},{9,10},{10,11},{12,13},{... | collective-permute-start | bytes 172040 | tf_op jit(solution)/shard_map/ppermute | solution.py:351
  25.9 1.9 %collective-permute-start.6 = (f32[7,16,128]{2,1,0:T(8,128)}, f32[7,16,128]{2,1,0:T(8,128)S(1)}, u32[]{:S(2)}, u32[]{:S(2)}) collective-permute-start(f32[7,16,128]{2,1,0:T(8,128)} %get-tuple-element.28), channel_id=1, source_target_pairs={{1,0},{2,1},{3,2},{5,4},{6,5},{7,6},{9,8},{10,9},{11,10},{13,12},{... | collective-permute-start | bytes 172040 | tf_op jit(solution)/shard_map/ppermute | solution.py:352
  27.8 0.0 collective-permute-done.5.below
  27.8 0.0 copy-start.8
  27.8 3.8 %collective-permute-done.6.above = f32[7,16,128]{2,1,0:T(8,128)S(1)} collective-permute-done((f32[7,16,128]{2,1,0:T(8,128)}, f32[7,16,128]{2,1,0:T(8,128)S(1)}, u32[]{:S(2)}, u32[]{:S(2)}) %collective-permute-start.6) | collective-permute-done | bytes 57376 | tf_op jit(solution)/shard_map/ppermute | solution.py:352
  31.6 0.0 copy-start.9
  31.6 0.0 copy-done.8
  31.6 0.6 %copy-done.9 = f32[7,16,128]{2,1,0:T(8,128)} copy-done((f32[7,16,128]{2,1,0:T(8,128)}, f32[7,16,128]{2,1,0:T(8,128)S(1)}, u32[]{:S(2)}) %copy-start.9) | copy-done | bytes 57368
  32.2 2.1 %shard_map.40 = (f32[10,3,16,128]{3,2,1,0:T(8,128)}, f32[4,10,3,16,128]{4,3,2,1,0:T(8,128)}) custom-call(f32[9,16,128]{2,1,0:T(8,128)} %get-tuple-element.26.own, f32[7,16,128]{2,1,0:T(8,128)} %copy-done.8, f32[7,16,128]{2,1,0:T(8,128)} %copy-done.9), custom_call_target="tpu_custom_call" | custom-call | tf_op jit(solution)/shard_map/pallas_call | solution.py:27
  34.2 0.0 collective-permute-done.3.refs_4_
  34.2 0.0 copy-start.3
  34.2 0.0 collective-permute-done.4.refs_5_
  34.3 0.0 copy-start.4
  34.3 0.7 %copy-done.3 = f32[28,16,128]{2,1,0:T(8,128)} copy-done((f32[28,16,128]{2,1,0:T(8,128)}, f32[28,16,128]{2,1,0:T(8,128)S(1)}, u32[]{:S(2)}) %copy-start.3) | copy-done | bytes 229400
  34.9 0.1 copy-done.4
  35.1 5.2 %shard_map.41 = (f32[8,16,128]{2,1,0:T(8,128)}, f32[8,16,128]{2,1,0:T(8,128)}, f32[8,16,128]{2,1,0:T(8,128)}, f32[8,16,128]{2,1,0:T(8,128)}) custom-call(f32[9,16,128]{2,1,0:T(8,128)} %get-tuple-element.20.refs_0_, f32[9,16,128]{2,1,0:T(8,128)} %copy-done, f32[9,16,128]{2,1,0:T(8,128)} %copy-done.1, f32[9,16,128]{2,1,0:T(8,128)} %copy-done.2, ...), custom_call_target="tpu_custom_call" | custom-call | tf_op jit(solution)/shard_map/pallas_call | solution.py:27
  40.3 1.5 %collective-permute-start.7 = (f32[8,16,128]{2,1,0:T(8,128)}, f32[8,16,128]{2,1,0:T(8,128)S(1)}, u32[]{:S(2)}, u32[]{:S(2)}) collective-permute-start(f32[8,16,128]{2,1,0:T(8,128)} %get-tuple-element.32), channel_id=1, source_target_pairs={{0,4},{4,8},{8,12},{12,0},{1,5},{5,9},{9,13},{13,1},{2,6},{6,10},{... | collective-permute-start | bytes 196616 | tf_op jit(solution)/shard_map/ppermute | solution.py:341
  41.8 1.6 %collective-permute-start.8 = (f32[8,16,128]{2,1,0:T(8,128)}, f32[8,16,128]{2,1,0:T(8,128)S(1)}, u32[]{:S(2)}, u32[]{:S(2)}) collective-permute-start(f32[8,16,128]{2,1,0:T(8,128)} %get-tuple-element.33), channel_id=1, source_target_pairs={{0,8},{4,12},{8,0},{12,4},{1,9},{5,13},{9,1},{13,5},{2,10},{6,14},... | collective-permute-start | bytes 196616 | tf_op jit(solution)/shard_map/ppermute | solution.py:341
  43.4 0.5 %collective-permute-start.9 = (f32[8,16,128]{2,1,0:T(8,128)}, f32[8,16,128]{2,1,0:T(8,128)S(1)}, u32[]{:S(2)}, u32[]{:S(2)}) collective-permute-start(f32[8,16,128]{2,1,0:T(8,128)} %get-tuple-element.34), channel_id=1, source_target_pairs={{0,12},{4,0},{8,4},{12,8},{1,13},{5,1},{9,5},{13,9},{2,14},{6,2},{... | collective-permute-start | bytes 196616 | tf_op jit(solution)/shard_map/ppermute | solution.py:341
  43.9 1.8 %collective-permute-done.7.refs_1_ = f32[8,16,128]{2,1,0:T(8,128)S(1)} collective-permute-done((f32[8,16,128]{2,1,0:T(8,128)}, f32[8,16,128]{2,1,0:T(8,128)S(1)}, u32[]{:S(2)}, u32[]{:S(2)}) %collective-permute-start.7) | collective-permute-done | bytes 65568 | tf_op jit(solution)/shard_map/ppermute | solution.py:341
  45.7 0.0 copy-start.5
  45.7 1.9 %collective-permute-done.8.refs_2_ = f32[8,16,128]{2,1,0:T(8,128)S(1)} collective-permute-done((f32[8,16,128]{2,1,0:T(8,128)}, f32[8,16,128]{2,1,0:T(8,128)S(1)}, u32[]{:S(2)}, u32[]{:S(2)}) %collective-permute-start.8) | collective-permute-done | bytes 65568 | tf_op jit(solution)/shard_map/ppermute | solution.py:341
  47.6 0.0 copy-start.6
  47.6 0.1 collective-permute-done.9.refs_3_
  47.7 0.0 copy-start.7
  47.7 0.0 copy-done.5
  47.7 0.5 copy-done.6
  48.2 0.2 copy-done.7
  48.3 1.9 %shard_map.42 = f32[16,4,1024]{2,1,0:T(4,128)} custom-call(f32[8,16,128]{2,1,0:T(8,128)} %get-tuple-element.31.refs_0_, f32[8,16,128]{2,1,0:T(8,128)} %copy-done.5, f32[8,16,128]{2,1,0:T(8,128)} %copy-done.6, f32[8,16,128]{2,1,0:T(8,128)} %copy-done.7), custom_call_target="tpu_custom_call" | custom-call | tf_op jit(solution)/shard_map/pallas_call | solution.py:27
Async XLA Ops:
  2.0 6.1 %collective-permute-start = (f32[9,16,128]{2,1,0:T(8,128)}, f32[9,16,128]{2,1,0:T(8,128)S(1)}, u32[]{:S(2)}, u32[]{:S(2)}) collective-permute-start(f32[9,16,128]{2,1,0:T(8,128)} %get-tuple-element.21), channel_id=1, source_target_pairs={{0,4},{4,8},{8,12},{12,0},{1,5},{5,9},{9,13},{13,1},{2,6},{6,10},{... | collective-permute-start | bytes 221192 | tf_op jit(solution)/shard_map/ppermute | solution.py:341
  4.1 8.1 %collective-permute-start.1 = (f32[9,16,128]{2,1,0:T(8,128)}, f32[9,16,128]{2,1,0:T(8,128)S(1)}, u32[]{:S(2)}, u32[]{:S(2)}) collective-permute-start(f32[9,16,128]{2,1,0:T(8,128)} %get-tuple-element.22), channel_id=1, source_target_pairs={{0,8},{4,12},{8,0},{12,4},{1,9},{5,13},{9,1},{13,5},{2,10},{6,14},... | collective-permute-start | bytes 221192 | tf_op jit(solution)/shard_map/ppermute | solution.py:341
  6.5 5.8 %collective-permute-start.2 = (f32[9,16,128]{2,1,0:T(8,128)}, f32[9,16,128]{2,1,0:T(8,128)S(1)}, u32[]{:S(2)}, u32[]{:S(2)}) collective-permute-start(f32[9,16,128]{2,1,0:T(8,128)} %get-tuple-element.23), channel_id=1, source_target_pairs={{0,12},{4,0},{8,4},{12,8},{1,13},{5,1},{9,5},{13,9},{2,14},{6,2},{... | collective-permute-start | bytes 221192 | tf_op jit(solution)/shard_map/ppermute | solution.py:341
  8.2 4.1 %copy-start = (f32[9,16,128]{2,1,0:T(8,128)}, f32[9,16,128]{2,1,0:T(8,128)S(1)}, u32[]{:S(2)}) copy-start(f32[9,16,128]{2,1,0:T(8,128)S(1)} %collective-permute-done.refs_1_) | copy-start | bytes 221188
  12.3 0.6 %copy-start.1 = (f32[9,16,128]{2,1,0:T(8,128)}, f32[9,16,128]{2,1,0:T(8,128)S(1)}, u32[]{:S(2)}) copy-start(f32[9,16,128]{2,1,0:T(8,128)S(1)} %collective-permute-done.1.refs_2_) | copy-start | bytes 221188
  12.3 0.7 %copy-start.2 = (f32[9,16,128]{2,1,0:T(8,128)}, f32[9,16,128]{2,1,0:T(8,128)S(1)}, u32[]{:S(2)}) copy-start(f32[9,16,128]{2,1,0:T(8,128)S(1)} %collective-permute-done.2.refs_3_) | copy-start | bytes 221188
  14.8 19.5 %collective-permute-start.3 = (f32[28,16,128]{2,1,0:T(8,128)}, f32[28,16,128]{2,1,0:T(8,128)S(1)}, u32[]{:S(2)}, u32[]{:S(2)}) collective-permute-start(f32[28,16,128]{2,1,0:T(8,128)} %get-tuple-element.24), channel_id=1, source_target_pairs={{0,1},{1,2},{2,3},{4,5},{5,6},{6,7},{8,9},{9,10},{10,11},{12,13},{... | collective-permute-start | bytes 688136 | tf_op jit(solution)/shard_map/ppermute | solution.py:351
  18.6 15.7 %collective-permute-start.4 = (f32[28,16,128]{2,1,0:T(8,128)}, f32[28,16,128]{2,1,0:T(8,128)S(1)}, u32[]{:S(2)}, u32[]{:S(2)}) collective-permute-start(f32[28,16,128]{2,1,0:T(8,128)} %get-tuple-element.25), channel_id=1, source_target_pairs={{1,0},{2,1},{3,2},{5,4},{6,5},{7,6},{9,8},{10,9},{11,10},{13,12},{... | collective-permute-start | bytes 688136 | tf_op jit(solution)/shard_map/ppermute | solution.py:352
  22.2 5.6 %collective-permute-start.5 = (f32[7,16,128]{2,1,0:T(8,128)}, f32[7,16,128]{2,1,0:T(8,128)S(1)}, u32[]{:S(2)}, u32[]{:S(2)}) collective-permute-start(f32[7,16,128]{2,1,0:T(8,128)} %get-tuple-element.27), channel_id=1, source_target_pairs={{0,1},{1,2},{2,3},{4,5},{5,6},{6,7},{8,9},{9,10},{10,11},{12,13},{... | collective-permute-start | bytes 172040 | tf_op jit(solution)/shard_map/ppermute | solution.py:351
  25.9 5.7 %collective-permute-start.6 = (f32[7,16,128]{2,1,0:T(8,128)}, f32[7,16,128]{2,1,0:T(8,128)S(1)}, u32[]{:S(2)}, u32[]{:S(2)}) collective-permute-start(f32[7,16,128]{2,1,0:T(8,128)} %get-tuple-element.28), channel_id=1, source_target_pairs={{1,0},{2,1},{3,2},{5,4},{6,5},{7,6},{9,8},{10,9},{11,10},{13,12},{... | collective-permute-start | bytes 172040 | tf_op jit(solution)/shard_map/ppermute | solution.py:352
  27.8 3.8 %copy-start.8 = (f32[7,16,128]{2,1,0:T(8,128)}, f32[7,16,128]{2,1,0:T(8,128)S(1)}, u32[]{:S(2)}) copy-start(f32[7,16,128]{2,1,0:T(8,128)S(1)} %collective-permute-done.5.below) | copy-start | bytes 172036
  31.6 0.6 %copy-start.9 = (f32[7,16,128]{2,1,0:T(8,128)}, f32[7,16,128]{2,1,0:T(8,128)S(1)}, u32[]{:S(2)}) copy-start(f32[7,16,128]{2,1,0:T(8,128)S(1)} %collective-permute-done.6.above) | copy-start | bytes 172036
  34.2 0.7 %copy-start.3 = (f32[28,16,128]{2,1,0:T(8,128)}, f32[28,16,128]{2,1,0:T(8,128)S(1)}, u32[]{:S(2)}) copy-start(f32[28,16,128]{2,1,0:T(8,128)S(1)} %collective-permute-done.3.refs_4_) | copy-start | bytes 688132
  34.3 0.8 %copy-start.4 = (f32[28,16,128]{2,1,0:T(8,128)}, f32[28,16,128]{2,1,0:T(8,128)S(1)}, u32[]{:S(2)}) copy-start(f32[28,16,128]{2,1,0:T(8,128)S(1)} %collective-permute-done.4.refs_5_) | copy-start | bytes 688132
  40.3 5.4 %collective-permute-start.7 = (f32[8,16,128]{2,1,0:T(8,128)}, f32[8,16,128]{2,1,0:T(8,128)S(1)}, u32[]{:S(2)}, u32[]{:S(2)}) collective-permute-start(f32[8,16,128]{2,1,0:T(8,128)} %get-tuple-element.32), channel_id=1, source_target_pairs={{0,4},{4,8},{8,12},{12,0},{1,5},{5,9},{9,13},{13,1},{2,6},{6,10},{... | collective-permute-start | bytes 196616 | tf_op jit(solution)/shard_map/ppermute | solution.py:341
  41.8 5.8 %collective-permute-start.8 = (f32[8,16,128]{2,1,0:T(8,128)}, f32[8,16,128]{2,1,0:T(8,128)S(1)}, u32[]{:S(2)}, u32[]{:S(2)}) collective-permute-start(f32[8,16,128]{2,1,0:T(8,128)} %get-tuple-element.33), channel_id=1, source_target_pairs={{0,8},{4,12},{8,0},{12,4},{1,9},{5,13},{9,1},{13,5},{2,10},{6,14},... | collective-permute-start | bytes 196616 | tf_op jit(solution)/shard_map/ppermute | solution.py:341
  43.4 4.3 %collective-permute-start.9 = (f32[8,16,128]{2,1,0:T(8,128)}, f32[8,16,128]{2,1,0:T(8,128)S(1)}, u32[]{:S(2)}, u32[]{:S(2)}) collective-permute-start(f32[8,16,128]{2,1,0:T(8,128)} %get-tuple-element.34), channel_id=1, source_target_pairs={{0,12},{4,0},{8,4},{12,8},{1,13},{5,1},{9,5},{13,9},{2,14},{6,2},{... | collective-permute-start | bytes 196616 | tf_op jit(solution)/shard_map/ppermute | solution.py:341
  45.7 2.0 %copy-start.5 = (f32[8,16,128]{2,1,0:T(8,128)}, f32[8,16,128]{2,1,0:T(8,128)S(1)}, u32[]{:S(2)}) copy-start(f32[8,16,128]{2,1,0:T(8,128)S(1)} %collective-permute-done.7.refs_1_) | copy-start | bytes 196612
  47.6 0.6 %copy-start.6 = (f32[8,16,128]{2,1,0:T(8,128)}, f32[8,16,128]{2,1,0:T(8,128)S(1)}, u32[]{:S(2)}) copy-start(f32[8,16,128]{2,1,0:T(8,128)S(1)} %collective-permute-done.8.refs_2_) | copy-start | bytes 196612
  47.7 0.6 %copy-start.7 = (f32[8,16,128]{2,1,0:T(8,128)}, f32[8,16,128]{2,1,0:T(8,128)S(1)}, u32[]{:S(2)}) copy-start(f32[8,16,128]{2,1,0:T(8,128)S(1)} %collective-permute-done.9.refs_3_) | copy-start | bytes 196612

commit v2 on v1

--- a/solution.py
+++ b/solution.py
@@ -23,14 +23,19 @@
 smem = pl.BlockSpec(memory_space=pltpu.SMEM)
 
 
-def call(kernel, outs, *operands, specs=None, scratch=()):
+def call(kernel, outs, *operands, from_hbm=0, kept=True, scratch=()):
+    on_chip = [
+        x if i < from_hbm or x.ndim == 1 else pltpu.with_memory_space_constraint(x, pltpu.VMEM)
+        for i, x in enumerate(operands)
+    ]
+    make = pltpu.VMEM if kept else jax.ShapeDtypeStruct
     return pl.pallas_call(
         kernel,
-        out_shape=[jax.ShapeDtypeStruct(o, jnp.float32) for o in outs],
-        in_specs=specs or [vmem] * len(operands),
+        out_shape=[make(o, jnp.float32) for o in outs],
+        in_specs=[smem if x.ndim == 1 else vmem for x in operands],
         out_specs=[vmem] * len(outs),
         scratch_shapes=scratch,
-    )(*operands)
+    )(*on_chip)
 
 
 def column_mask(left, right, shape):
@@ -81,7 +86,7 @@
     tiles = columns // steps // lanes
     log_alpha = math.log(circ_alpha) / steps
     kernel = functools.partial(pack_kernel, "tm", log_alpha, steps)
-    return call(kernel, [(rows * tiles + 1, depth, lanes)] * steps, rhs)
+    return call(kernel, [(rows * tiles + 1, depth, lanes)] * steps, rhs, from_hbm=1)
 
 
 def halo_pieces(block, ahead, rows, tiles):
@@ -90,7 +95,7 @@
 
 
 def halo_kernel(rows, tiles, steps, *refs):
-    blocks, (up, down) = refs[:steps], refs[steps:]
+    blocks, (_, up, down) = refs[:steps], refs[steps:]
     piece = reach * tiles + 1
     for step, block in enumerate(blocks):
         for out, ahead in ((up, True), (down, False)):
@@ -98,11 +103,11 @@
                 out[step * piece + place] = block[index]
 
 
-def halos(blocks, rows, tiles):
+def halos(blocks, ready, rows, tiles):
     depth = blocks[0].shape[1]
     out = (len(blocks) * (reach * tiles + 1), depth, lanes)
     kernel = functools.partial(halo_kernel, rows, tiles, len(blocks))
-    return call(kernel, [out, out], *blocks)
+    return call(kernel, [out, out], *blocks, ready)
 
 
 def kappa_kernel(tm, rows, tiles, steps, kappa, own, up, down):
@@ -366,6 +371,7 @@
         functools.partial(kappa_kernel, "tm", rows, tiles, steps),
         [(rows * tiles + 1, depth, lanes), piece, piece],
         diffusivity,
+        from_hbm=1,
     )
     kappa_below, kappa_above = neighbours(kappa_up, kappa_down)
     kappa, inverse = call(
@@ -375,7 +381,7 @@
         kappa_below,
         kappa_above,
     )
-    below, above = neighbours(*halos(blocks, rows, tiles))
+    below, above = neighbours(*halos(blocks, kappa, rows, tiles))
     padded = pltpu.VMEM((fields, extended, wide, depth + 16, lanes), jnp.float32)
     results = call(
         functools.partial(solve_kernel, rows, tiles, steps),
@@ -386,7 +392,6 @@
         kappa,
         inverse,
         velocity,
-        specs=[vmem] * (steps + 4) + [smem],
         scratch=[
             pltpu.VMEM((fields, extended, wide, depth, lanes), jnp.float32),
             padded,
@@ -398,6 +403,7 @@
         functools.partial(unpack_kernel, "tm", log_alpha, steps),
         [(depth, rows, columns)],
         *returned,
+        kept=False,
     )
     return result[None]
 

time: 51 us -> 38.4 us (0.75)
  Pallas kernels: 14.8 us -> 7.13 us
  local copies, waits for them, and re-layouts: 2.7 us -> 0 us
  waiting for transfers between devices: 12.3 us -> 11.3 us
  starting transfers between devices: 20.4 us -> 19.6 us
    pallas_call x6, Pallas kernels: 14.8 us -> 7.13 us  [call(): pl.pallas_call(kernel, out_shape=[make(o, jnp.float32) for o in outs], in...]
    ppermute x6, waiting for transfers between devices: 8.53 us -> 2.8 us  [exchange(): lax.ppermute(blocks[d], 'tm', [(i, (i + d) % steps) for i in range(steps)])]
    ppermute x2, waiting for transfers between devices: 3.76 us -> 7.95 us  [neighbours(): lax.ppermute(down, 'space', [(j, i) for i, j in ahead])]
    unnamed x20 -> x0, local copies, waits for them, and re-layouts: 2.7 us -> none
    ppermute x2, starting transfers between devices: 7.43 us -> 6.44 us  [neighbours(): lax.ppermute(up, 'space', ahead)]
    ppermute x2, waiting for transfers between devices: 0.01 us -> 0.52 us  [neighbours(): lax.ppermute(up, 'space', ahead)]
  transfers between devices with their start and end apart: 10 -> 10, of which waited for: 6 -> 5; matrix products, arithmetic and copies ran while one was open for 0% -> 0% of each run, Pallas kernels for 8% -> 3%
where the time goes in v2:
time: 38.4 us; the launch traced here: 38.1 us
  starting transfers between devices  19.6 us (51%)
  waiting for transfers between devices  11.3 us (29%)
  Pallas kernels  7.13 us (19%)
    ppermute x6, starting transfers between devices, exchange(): lax.ppermute(blocks[d], 'tm', [(i, (i + d) % steps) for i in range(steps)])  8.86 us
    ppermute x2, waiting for transfers between devices, neighbours(): lax.ppermute(down, 'space', [(j, i) for i, j in ahead])  7.95 us
    pallas_call x6, Pallas kernels, call(): pl.pallas_call(kernel, out_shape=[make(o, jnp.float32) for o in outs], in...  7.13 us
    ppermute x2, starting transfers between devices, neighbours(): lax.ppermute(up, 'space', ahead)  6.44 us
    ppermute x2, starting transfers between devices, neighbours(): lax.ppermute(down, 'space', [(j, i) for i, j in ahead])  4.34 us
    ppermute x6, waiting for transfers between devices, exchange(): lax.ppermute(blocks[d], 'tm', [(i, (i + d) % steps) for i in range(steps)])  2.8 us
  transfers between devices with their start and end apart: 10, of which 5 were waited for; matrix products, arithmetic and copies ran while one was open for 0% of the time, Pallas kernels for 3%

profile of v2, /device:TPU:1, one launch (start us, length us, event | category | flops | bytes accessed | tf_op | source)
XLA Modules:
  0.0 38.1 jit_solution(6134020446623908949)
XLA Ops:
  0.0 1.4 %shard_map.37 = (f32[9,16,128]{2,1,0:T(8,128)S(1)}, f32[9,16,128]{2,1,0:T(8,128)S(1)}, f32[9,16,128]{2,1,0:T(8,128)S(1)}, f32[9,16,128]{2,1,0:T(8,128)S(1)}) custom-call(f32[16,4,1024]{2,1,0:T(4,128)} %bitcast.2), custom_call_target="tpu_custom_call" | custom-call | tf_op jit(solution)/shard_map/pallas_call | solution.py:32
  1.4 2.2 %collective-permute-start = (f32[9,16,128]{2,1,0:T(8,128)S(1)}, f32[9,16,128]{2,1,0:T(8,128)S(1)}, u32[]{:S(2)}, u32[]{:S(2)}) collective-permute-start(f32[9,16,128]{2,1,0:T(8,128)S(1)} %get-tuple-element.21), channel_id=1, source_target_pairs={{0,4},{4,8},{8,12},{12,0},{1,5},{5,9},{9,13},{13,1},{2,6},{6,10},{... | collective-permute-start | bytes 221192 | tf_op jit(solution)/shard_map/ppermute | solution.py:346
  3.6 2.3 %collective-permute-start.1 = (f32[9,16,128]{2,1,0:T(8,128)S(1)}, f32[9,16,128]{2,1,0:T(8,128)S(1)}, u32[]{:S(2)}, u32[]{:S(2)}) collective-permute-start(f32[9,16,128]{2,1,0:T(8,128)S(1)} %get-tuple-element.22), channel_id=1, source_target_pairs={{0,8},{4,12},{8,0},{12,4},{1,9},{5,13},{9,1},{13,5},{2,10},{6,14},... | collective-permute-start | bytes 221192 | tf_op jit(solution)/shard_map/ppermute | solution.py:346
  5.9 1.1 %collective-permute-start.2 = (f32[9,16,128]{2,1,0:T(8,128)S(1)}, f32[9,16,128]{2,1,0:T(8,128)S(1)}, u32[]{:S(2)}, u32[]{:S(2)}) collective-permute-start(f32[9,16,128]{2,1,0:T(8,128)S(1)} %get-tuple-element.23), channel_id=1, source_target_pairs={{0,12},{4,0},{8,4},{12,8},{1,13},{5,1},{9,5},{13,9},{2,14},{6,2},{... | collective-permute-start | bytes 221192 | tf_op jit(solution)/shard_map/ppermute | solution.py:346
  7.0 1.1 %shard_map.38 = (f32[9,16,128]{2,1,0:T(8,128)S(1)}, f32[7,16,128]{2,1,0:T(8,128)S(1)}, f32[7,16,128]{2,1,0:T(8,128)S(1)}) custom-call(f32[16,4,1024]{2,1,0:T(4,128)} %kappa.1), custom_call_target="tpu_custom_call" | custom-call | tf_op jit(solution)/shard_map/pallas_call | solution.py:32
  8.0 4.5 %collective-permute-start.3 = (f32[7,16,128]{2,1,0:T(8,128)S(1)}, f32[7,16,128]{2,1,0:T(8,128)S(1)}, u32[]{:S(2)}, u32[]{:S(2)}) collective-permute-start(f32[7,16,128]{2,1,0:T(8,128)S(1)} %get-tuple-element.25), channel_id=1, source_target_pairs={{0,1},{1,2},{2,3},{4,5},{5,6},{6,7},{8,9},{9,10},{10,11},{12,13},{... | collective-permute-start | bytes 172040 | tf_op jit(solution)/shard_map/ppermute | solution.py:356
  12.5 1.9 %collective-permute-start.4 = (f32[7,16,128]{2,1,0:T(8,128)S(1)}, f32[7,16,128]{2,1,0:T(8,128)S(1)}, u32[]{:S(2)}, u32[]{:S(2)}) collective-permute-start(f32[7,16,128]{2,1,0:T(8,128)S(1)} %get-tuple-element.26), channel_id=1, source_target_pairs={{1,0},{2,1},{3,2},{5,4},{6,5},{7,6},{9,8},{10,9},{11,10},{13,12},{... | collective-permute-start | bytes 172040 | tf_op jit(solution)/shard_map/ppermute | solution.py:357
  14.5 0.0 collective-permute-done.3.below
  14.5 3.6 %collective-permute-done.4.above = f32[7,16,128]{2,1,0:T(8,128)S(1)} collective-permute-done((f32[7,16,128]{2,1,0:T(8,128)S(1)}, f32[7,16,128]{2,1,0:T(8,128)S(1)}, u32[]{:S(2)}, u32[]{:S(2)}) %collective-permute-start.4) | collective-permute-done | bytes 57376 | tf_op jit(solution)/shard_map/ppermute | solution.py:357
  18.0 0.1 shard_map.39
  18.2 0.0 collective-permute-done.refs_1_
  18.2 0.0 collective-permute-done.1.refs_2_
  18.2 0.0 collective-permute-done.2.refs_3_
  18.2 1.9 %collective-permute-start.5 = (f32[28,16,128]{2,1,0:T(8,128)S(1)}, f32[28,16,128]{2,1,0:T(8,128)S(1)}, u32[]{:S(2)}, u32[]{:S(2)}) collective-permute-start(f32[28,16,128]{2,1,0:T(8,128)S(1)} %get-tuple-element.28), channel_id=1, source_target_pairs={{0,1},{1,2},{2,3},{4,5},{5,6},{6,7},{8,9},{9,10},{10,11},{12,13},{... | collective-permute-start | bytes 688136 | tf_op jit(solution)/shard_map/ppermute | solution.py:356
  20.2 2.4 %collective-permute-start.6 = (f32[28,16,128]{2,1,0:T(8,128)S(1)}, f32[28,16,128]{2,1,0:T(8,128)S(1)}, u32[]{:S(2)}, u32[]{:S(2)}) collective-permute-start(f32[28,16,128]{2,1,0:T(8,128)S(1)} %get-tuple-element.29), channel_id=1, source_target_pairs={{1,0},{2,1},{3,2},{5,4},{6,5},{7,6},{9,8},{10,9},{11,10},{13,12},{... | collective-permute-start | bytes 688136 | tf_op jit(solution)/shard_map/ppermute | solution.py:357
  22.6 0.5 %collective-permute-done.5.refs_4_ = f32[28,16,128]{2,1,0:T(8,128)S(1)} collective-permute-done((f32[28,16,128]{2,1,0:T(8,128)S(1)}, f32[28,16,128]{2,1,0:T(8,128)S(1)}, u32[]{:S(2)}, u32[]{:S(2)}) %collective-permute-start.5) | collective-permute-done | bytes 229408 | tf_op jit(solution)/shard_map/ppermute | solution.py:356
  23.1 4.4 %collective-permute-done.6.refs_5_ = f32[28,16,128]{2,1,0:T(8,128)S(1)} collective-permute-done((f32[28,16,128]{2,1,0:T(8,128)S(1)}, f32[28,16,128]{2,1,0:T(8,128)S(1)}, u32[]{:S(2)}, u32[]{:S(2)}) %collective-permute-start.6) | collective-permute-done | bytes 229408 | tf_op jit(solution)/shard_map/ppermute | solution.py:357
  27.5 3.5 %shard_map.41 = (f32[8,16,128]{2,1,0:T(8,128)S(1)}, f32[8,16,128]{2,1,0:T(8,128)S(1)}, f32[8,16,128]{2,1,0:T(8,128)S(1)}, f32[8,16,128]{2,1,0:T(8,128)S(1)}) custom-call(f32[9,16,128]{2,1,0:T(8,128)S(1)} %get-tuple-element.20.refs_0_, f32[9,16,128]{2,1,0:T(8,128)S(1)} %collective-permute-done.refs_1_, f32[9,16,128]{2,1,0:T(8,128)S(1)} %collective-permute-done.1.refs_2_, ...), custom_call_target="tpu_custom_call" | custom-call | tf_op jit(solution)/shard_map/pallas_call | solution.py:32
  31.0 0.5 %collective-permute-start.7 = (f32[8,16,128]{2,1,0:T(8,128)S(1)}, f32[8,16,128]{2,1,0:T(8,128)S(1)}, u32[]{:S(2)}, u32[]{:S(2)}) collective-permute-start(f32[8,16,128]{2,1,0:T(8,128)S(1)} %get-tuple-element.32), channel_id=1, source_target_pairs={{0,4},{4,8},{8,12},{12,0},{1,5},{5,9},{9,13},{13,1},{2,6},{6,10},{... | collective-permute-start | bytes 196616 | tf_op jit(solution)/shard_map/ppermute | solution.py:346
  31.5 0.1 collective-permute-start.8
  31.5 2.8 %collective-permute-start.9 = (f32[8,16,128]{2,1,0:T(8,128)S(1)}, f32[8,16,128]{2,1,0:T(8,128)S(1)}, u32[]{:S(2)}, u32[]{:S(2)}) collective-permute-start(f32[8,16,128]{2,1,0:T(8,128)S(1)} %get-tuple-element.34), channel_id=1, source_target_pairs={{0,12},{4,0},{8,4},{12,8},{1,13},{5,1},{9,5},{13,9},{2,14},{6,2},{... | collective-permute-start | bytes 196616 | tf_op jit(solution)/shard_map/ppermute | solution.py:346
  34.4 1.8 %collective-permute-done.7.refs_1_ = f32[8,16,128]{2,1,0:T(8,128)S(1)} collective-permute-done((f32[8,16,128]{2,1,0:T(8,128)S(1)}, f32[8,16,128]{2,1,0:T(8,128)S(1)}, u32[]{:S(2)}, u32[]{:S(2)}) %collective-permute-start.7) | collective-permute-done | bytes 65568 | tf_op jit(solution)/shard_map/ppermute | solution.py:346
  36.2 1.0 %collective-permute-done.8.refs_2_ = f32[8,16,128]{2,1,0:T(8,128)S(1)} collective-permute-done((f32[8,16,128]{2,1,0:T(8,128)S(1)}, f32[8,16,128]{2,1,0:T(8,128)S(1)}, u32[]{:S(2)}, u32[]{:S(2)}) %collective-permute-start.8) | collective-permute-done | bytes 65568 | tf_op jit(solution)/shard_map/ppermute | solution.py:346
  37.1 0.0 collective-permute-done.9.refs_3_
  37.1 1.0 %shard_map.42 = f32[16,4,1024]{2,1,0:T(4,128)} custom-call(f32[8,16,128]{2,1,0:T(8,128)S(1)} %get-tuple-element.31.refs_0_, f32[8,16,128]{2,1,0:T(8,128)S(1)} %collective-permute-done.7.refs_1_, f32[8,16,128]{2,1,0:T(8,128)S(1)} %collective-permute-done.8.refs_2_, f32[8,16,128]{2,1,0:T(8,128)S(1)} %collective-permute-done.9.refs_3_), custom_call_target="tpu_custom_call" | custom-call | tf_op jit(solution)/shard_map/pallas_call | solution.py:32
  (1 shorter events, 0.0 us)
Async XLA Ops:
  1.4 16.8 %collective-permute-start = (f32[9,16,128]{2,1,0:T(8,128)S(1)}, f32[9,16,128]{2,1,0:T(8,128)S(1)}, u32[]{:S(2)}, u32[]{:S(2)}) collective-permute-start(f32[9,16,128]{2,1,0:T(8,128)S(1)} %get-tuple-element.21), channel_id=1, source_target_pairs={{0,4},{4,8},{8,12},{12,0},{1,5},{5,9},{9,13},{13,1},{2,6},{6,10},{... | collective-permute-start | bytes 221192 | tf_op jit(solution)/shard_map/ppermute | solution.py:346
  3.6 14.6 %collective-permute-start.1 = (f32[9,16,128]{2,1,0:T(8,128)S(1)}, f32[9,16,128]{2,1,0:T(8,128)S(1)}, u32[]{:S(2)}, u32[]{:S(2)}) collective-permute-start(f32[9,16,128]{2,1,0:T(8,128)S(1)} %get-tuple-element.22), channel_id=1, source_target_pairs={{0,8},{4,12},{8,0},{12,4},{1,9},{5,13},{9,1},{13,5},{2,10},{6,14},... | collective-permute-start | bytes 221192 | tf_op jit(solution)/shard_map/ppermute | solution.py:346
  5.9 12.3 %collective-permute-start.2 = (f32[9,16,128]{2,1,0:T(8,128)S(1)}, f32[9,16,128]{2,1,0:T(8,128)S(1)}, u32[]{:S(2)}, u32[]{:S(2)}) collective-permute-start(f32[9,16,128]{2,1,0:T(8,128)S(1)} %get-tuple-element.23), channel_id=1, source_target_pairs={{0,12},{4,0},{8,4},{12,8},{1,13},{5,1},{9,5},{13,9},{2,14},{6,2},{... | collective-permute-start | bytes 221192 | tf_op jit(solution)/shard_map/ppermute | solution.py:346
  8.0 6.5 %collective-permute-start.3 = (f32[7,16,128]{2,1,0:T(8,128)S(1)}, f32[7,16,128]{2,1,0:T(8,128)S(1)}, u32[]{:S(2)}, u32[]{:S(2)}) collective-permute-start(f32[7,16,128]{2,1,0:T(8,128)S(1)} %get-tuple-element.25), channel_id=1, source_target_pairs={{0,1},{1,2},{2,3},{4,5},{5,6},{6,7},{8,9},{9,10},{10,11},{12,13},{... | collective-permute-start | bytes 172040 | tf_op jit(solution)/shard_map/ppermute | solution.py:356
  12.5 5.5 %collective-permute-start.4 = (f32[7,16,128]{2,1,0:T(8,128)S(1)}, f32[7,16,128]{2,1,0:T(8,128)S(1)}, u32[]{:S(2)}, u32[]{:S(2)}) collective-permute-start(f32[7,16,128]{2,1,0:T(8,128)S(1)} %get-tuple-element.26), channel_id=1, source_target_pairs={{1,0},{2,1},{3,2},{5,4},{6,5},{7,6},{9,8},{10,9},{11,10},{13,12},{... | collective-permute-start | bytes 172040 | tf_op jit(solution)/shard_map/ppermute | solution.py:357
  18.2 4.9 %collective-permute-start.5 = (f32[28,16,128]{2,1,0:T(8,128)S(1)}, f32[28,16,128]{2,1,0:T(8,128)S(1)}, u32[]{:S(2)}, u32[]{:S(2)}) collective-permute-start(f32[28,16,128]{2,1,0:T(8,128)S(1)} %get-tuple-element.28), channel_id=1, source_target_pairs={{0,1},{1,2},{2,3},{4,5},{5,6},{6,7},{8,9},{9,10},{10,11},{12,13},{... | collective-permute-start | bytes 688136 | tf_op jit(solution)/shard_map/ppermute | solution.py:356
  20.2 7.3 %collective-permute-start.6 = (f32[28,16,128]{2,1,0:T(8,128)S(1)}, f32[28,16,128]{2,1,0:T(8,128)S(1)}, u32[]{:S(2)}, u32[]{:S(2)}) collective-permute-start(f32[28,16,128]{2,1,0:T(8,128)S(1)} %get-tuple-element.29), channel_id=1, source_target_pairs={{1,0},{2,1},{3,2},{5,4},{6,5},{7,6},{9,8},{10,9},{11,10},{13,12},{... | collective-permute-start | bytes 688136 | tf_op jit(solution)/shard_map/ppermute | solution.py:357
  31.0 5.1 %collective-permute-start.7 = (f32[8,16,128]{2,1,0:T(8,128)S(1)}, f32[8,16,128]{2,1,0:T(8,128)S(1)}, u32[]{:S(2)}, u32[]{:S(2)}) collective-permute-start(f32[8,16,128]{2,1,0:T(8,128)S(1)} %get-tuple-element.32), channel_id=1, source_target_pairs={{0,4},{4,8},{8,12},{12,0},{1,5},{5,9},{9,13},{13,1},{2,6},{6,10},{... | collective-permute-start | bytes 196616 | tf_op jit(solution)/shard_map/ppermute | solution.py:346
  31.5 5.7 %collective-permute-start.8 = (f32[8,16,128]{2,1,0:T(8,128)S(1)}, f32[8,16,128]{2,1,0:T(8,128)S(1)}, u32[]{:S(2)}, u32[]{:S(2)}) collective-permute-start(f32[8,16,128]{2,1,0:T(8,128)S(1)} %get-tuple-element.33), channel_id=1, source_target_pairs={{0,8},{4,12},{8,0},{12,4},{1,9},{5,13},{9,1},{13,5},{2,10},{6,14},... | collective-permute-start | bytes 196616 | tf_op jit(solution)/shard_map/ppermute | solution.py:346
  31.5 5.6 %collective-permute-start.9 = (f32[8,16,128]{2,1,0:T(8,128)S(1)}, f32[8,16,128]{2,1,0:T(8,128)S(1)}, u32[]{:S(2)}, u32[]{:S(2)}) collective-permute-start(f32[8,16,128]{2,1,0:T(8,128)S(1)} %get-tuple-element.34), channel_id=1, source_target_pairs={{0,12},{4,0},{8,4},{12,8},{1,13},{5,1},{9,5},{13,9},{2,14},{6,2},{... | collective-permute-start | bytes 196616 | tf_op jit(solution)/shard_map/ppermute | solution.py:346

commit v3 on v2

--- a/solution.py
+++ b/solution.py
@@ -23,7 +23,7 @@
 smem = pl.BlockSpec(memory_space=pltpu.SMEM)
 
 
-def call(kernel, outs, *operands, from_hbm=0, kept=True, scratch=()):
+def call(kernel, outs, *operands, from_hbm=0, kept=True, aliases=None):
     on_chip = [
         x if i < from_hbm or x.ndim == 1 else pltpu.with_memory_space_constraint(x, pltpu.VMEM)
         for i, x in enumerate(operands)
@@ -34,7 +34,8 @@
         out_shape=[make(o, jnp.float32) for o in outs],
         in_specs=[smem if x.ndim == 1 else vmem for x in operands],
         out_specs=[vmem] * len(outs),
-        scratch_shapes=scratch,
+        input_output_aliases=aliases or {},
+        compiler_params=pltpu.CompilerParams(vmem_limit_bytes=16 << 20),
     )(*on_chip)
 
 
@@ -45,8 +46,18 @@
     return keep_right, keep_left
 
 
-def pick_block(source, write, owner, owners, depth, rows, tiles):
-    total = owners * tiles
+def upwards(space):
+    return lax.rem(lax.axis_index(space), 2)
+
+
+def row_of(y, rows, up):
+    return up * y + (1 - up) * (rows - 1 - y)
+
+
+def pick_block(source, write, owner, owners, up):
+    depth, rows, columns = source.shape
+    total = columns // lanes
+    tiles = total // owners
     left_tile = jnp.maximum(owner * tiles - 1, 0)
     right_tile = jnp.minimum((owner + 1) * tiles, total - 1)
     left = (owner > 0).astype(jnp.float32)
@@ -54,23 +65,22 @@
     keep_right, keep_left = column_mask(left, right, (depth, lanes))
     packed = None
 
-    def tile_at(row, tile):
-        return source[:, row, pl.ds(pl.multiple_of(tile * lanes, lanes), lanes)]
-
-    for row in range(rows):
+    def tile_at(y, tile):
+        return source[:, y, pl.ds(pl.multiple_of(tile * lanes, lanes), lanes)]
+
+    for y in range(rows):
+        row = row_of(y, rows, up)
         for tile in range(tiles):
-            write(row * tiles + tile, tile_at(row, owner * tiles + tile))
-        halo = tile_at(row, right_tile) * keep_right + tile_at(row, left_tile) * keep_left
-        if row:
-            halo = pltpu.roll(halo, row * (lanes // rows), 1)
+            write(row * tiles + tile, tile_at(y, owner * tiles + tile))
+        halo = tile_at(y, right_tile) * keep_right + tile_at(y, left_tile) * keep_left
+        halo = pltpu.roll(halo, row * (lanes // rows), 1)
         packed = halo if packed is None else packed + halo
     write(rows * tiles, packed)
 
 
-def pack_kernel(tm, log_alpha, steps, rhs, *outs):
-    me = lax.axis_index(tm)
-    depth, rows, columns = rhs.shape
-    tiles = columns // steps // lanes
+def pack_kernel(tm, space, log_alpha, steps, rhs, *outs):
+    me, up = lax.axis_index(tm), upwards(space)
+    depth = rhs.shape[0]
     scale = jnp.exp(jnp.full((depth, lanes), me.astype(jnp.float32) * log_alpha, jnp.float32))
     for ahead in range(steps):
         out = outs[ahead]
@@ -78,29 +88,30 @@
         def write(index, value, out=out):
             out[index] = value * scale
 
-        pick_block(rhs, write, lax.rem(me + ahead, steps), steps, depth, rows, tiles)
+        pick_block(rhs, write, lax.rem(me + ahead, steps), steps, up)
 
 
 def pack(rhs, steps):
     depth, rows, columns = rhs.shape
     tiles = columns // steps // lanes
     log_alpha = math.log(circ_alpha) / steps
-    kernel = functools.partial(pack_kernel, "tm", log_alpha, steps)
+    kernel = functools.partial(pack_kernel, "tm", "space", log_alpha, steps)
     return call(kernel, [(rows * tiles + 1, depth, lanes)] * steps, rhs, from_hbm=1)
 
 
-def halo_pieces(block, ahead, rows, tiles):
-    first = (rows - reach) * tiles if ahead else 0
-    return [first + i for i in range(reach * tiles)] + [rows * tiles]
+def first_row(near, rows):
+    return 0 if near else rows - reach
 
 
 def halo_kernel(rows, tiles, steps, *refs):
-    blocks, (_, up, down) = refs[:steps], refs[steps:]
+    blocks, (_, near, far) = refs[:steps], refs[steps:]
     piece = reach * tiles + 1
     for step, block in enumerate(blocks):
-        for out, ahead in ((up, True), (down, False)):
-            for place, index in enumerate(halo_pieces(block, ahead, rows, tiles)):
-                out[step * piece + place] = block[index]
+        for out, is_near in ((near, True), (far, False)):
+            start = first_row(is_near, rows) * tiles
+            for place in range(reach * tiles):
+                out[step * piece + place] = block[start + place]
+            out[step * piece + reach * tiles] = block[rows * tiles]
 
 
 def halos(blocks, ready, rows, tiles):
@@ -110,36 +121,36 @@
     return call(kernel, [out, out], *blocks, ready)
 
 
-def kappa_kernel(tm, rows, tiles, steps, kappa, own, up, down):
-    me = lax.axis_index(tm)
-    held = {}
-    depth = kappa.shape[0]
+def kappa_kernel(tm, space, rows, tiles, steps, kappa, own, near, far):
+    me, up = lax.axis_index(tm), upwards(space)
 
     def write(index, value):
         own[index] = value
-        held[index] = value
-
-    pick_block(kappa, write, me, steps, depth, rows, tiles)
-    for out, ahead in ((up, True), (down, False)):
-        for place, index in enumerate(halo_pieces(own, ahead, rows, tiles)):
-            out[place] = held[index]
-
-
-def row_piece(own, below, above, step, row, tile, rows, tiles):
+
+    pick_block(kappa, write, me, steps, up)
+    for out, is_near in ((near, True), (far, False)):
+        start = first_row(is_near, rows) * tiles
+        for place in range(reach * tiles):
+            out[place] = own[start + place]
+        out[reach * tiles] = own[rows * tiles]
+
+
+def row_piece(own, near, far, step, row, tile, rows, tiles):
     piece = reach * tiles + 1
     if row < reach:
-        source, base, local_row, place = below, step * piece, rows - reach + row, row
+        source, base, there, start = near, step * piece, reach - 1 - row, 0
         packed = base + reach * tiles
     elif row < reach + rows:
-        source, base, local_row, place = own, 0, row - reach, row - reach
+        source, base, there, start = own, 0, row - reach, 0
         packed = rows * tiles
     else:
-        source, base, local_row, place = above, step * piece, row - reach - rows, row - reach - rows
+        source, base, there = far, step * piece, 2 * rows + reach - 1 - row
+        start = rows - reach
         packed = base + reach * tiles
     if tile < tiles:
-        return source[base + place * tiles + tile]
+        return source[base + (there - start) * tiles + tile]
     value = source[packed]
-    shift = local_row * (lanes // rows)
+    shift = there * (lanes // rows)
     return pltpu.roll(value, lanes - shift, 1) if shift else value
 
 
@@ -147,8 +158,8 @@
     return [(k, 2 * k % steps != 0) for k in range(steps // 2 + 1)]
 
 
-def coefficient_kernel(tm, space, rows, tiles, steps, own, below, above, kappa, *outs):
-    me, slab = lax.axis_index(tm), lax.axis_index(space)
+def coefficient_kernel(tm, space, rows, tiles, steps, own, near, far, kappa, inverse):
+    me, slab, up = lax.axis_index(tm), lax.axis_index(space), upwards(space)
     slabs = lax.axis_size(space)
     depth = own.shape[1]
     keep_right, keep_left = column_mask(
@@ -156,14 +167,13 @@
     )
     halo_mask = keep_right + keep_left
     shift_factor = circ_alpha ** (1.0 / steps)
+    has_lower, has_upper = slab > 0, slab < slabs - 1
+    has_near = jnp.where(up == 1, has_lower, has_upper).astype(jnp.float32)
+    has_far = jnp.where(up == 1, has_upper, has_lower).astype(jnp.float32)
     for row in range(rows + 2 * reach):
-        inside = None
-        if row < reach:
-            inside = (slab > 0).astype(jnp.float32)
-        elif row >= reach + rows:
-            inside = (slab < slabs - 1).astype(jnp.float32)
+        inside = has_near if row < reach else has_far if row >= reach + rows else None
         for tile in range(tiles + 1):
-            value = row_piece(own, below, above, 0, row, tile, rows, tiles)
+            value = row_piece(own, near, far, 0, row, tile, rows, tiles)
             kappa[row, tile] = value
             mask = halo_mask if tile == tiles else None
             if inside is not None:
@@ -174,12 +184,12 @@
                 real = (1.0 - shift_factor * math.cos(phase)) + 6.0 * value
                 if is_complex:
                     imag = shift_factor * math.sin(phase)
-                    inverse = 1.0 / (real * real + imag * imag)
-                    pair = (real * inverse, imag * inverse)
+                    reciprocal = 1.0 / (real * real + imag * imag)
+                    pair = (real * reciprocal, imag * reciprocal)
                 else:
                     pair = (1.0 / real,)
                 for part in pair:
-                    outs[0][place, row, tile] = part if mask is None else part * mask
+                    inverse[place, row, tile] = part if mask is None else part * mask
                     place += 1
 
 
@@ -211,28 +221,44 @@
     return exact(math.sin(2.0 * math.pi * (product % steps) / steps))
 
 
-def solve_kernel(rows, tiles, steps, *refs):
-    blocks, refs = refs[:steps], refs[steps:]
-    below, above, kappa, inverse, velocity = refs[:5]
-    outs, (source, first, second) = refs[5 : 5 + steps], refs[5 + steps :]
-    depth = blocks[0].shape[1]
+def solve_kernel(space, rows, tiles, steps, second_half, *refs):
+    freqs = frequencies(steps)
+    fields = sum(2 if c else 1 for _, c in freqs)
+    levels = reach
+    if second_half:
+        far, kappa, inverse, velocity = refs[:4]
+        refs = refs[5 + levels + steps :]
+        source, *iterates = refs[: 1 + levels]
+        outs = refs[1 + levels :]
+        blocks, near = [None] * steps, None
+    else:
+        blocks, (near, kappa, inverse, velocity) = refs[:steps], refs[steps : steps + 4]
+        source, *iterates = refs[steps + 4 : steps + 5 + levels]
+        outs = refs[steps + 5 + levels :]
+        far = None
+    depth = kappa.shape[2]
     pad = 8
     middle = pl.ds(pad, depth)
     lane = lax.broadcasted_iota(jnp.int32, (depth, lanes), 1)
     at_first, at_last = lane == 0, lane == lanes - 1
-    freqs = frequencies(steps)
-    fields = sum(2 if c else 1 for _, c in freqs)
-    half = [0.5 * velocity[j] for j in range(3)]
-    extended = rows + 2 * reach
+    direction = (2 * upwards(space) - 1).astype(jnp.float32)
+    half = [0.5 * velocity[0], 0.5 * direction * velocity[1], 0.5 * velocity[2]]
+    known = reach + rows
+    extended = known + reach
     wide = tiles + 1
 
-    zero = jnp.zeros((8, lanes), jnp.float32)
-    for ref in (first, second):
-        for field in range(fields):
-            for row in range(extended):
-                for tile in range(wide):
-                    ref[field, row, tile, pl.ds(0, 8), :] = zero
-                    ref[field, row, tile, pl.ds(pad + depth, 8), :] = zero
+    def rows_of(level):
+        split = known - level
+        return (split, extended - level) if second_half else (level, split)
+
+    if not second_half:
+        zero = jnp.zeros((8, lanes), jnp.float32)
+        for level, ref in enumerate(iterates):
+            for field in range(fields):
+                for row in range(level, extended - level):
+                    for tile in range(wide):
+                        ref[field, row, tile, pl.ds(0, 8), :] = zero
+                        ref[field, row, tile, pl.ds(pad + depth, 8), :] = zero
 
     def divide(values, row, tile):
         result, place = [], 0
@@ -247,13 +273,12 @@
                 place += 1
         return result
 
-    for row in range(extended):
+    for row in range(*rows_of(0)):
         for tile in range(wide):
             if tile == tiles and not 1 <= row < extended - 1:
                 continue
             held = [
-                row_piece(blocks[b], below, above, b, row, tile, rows, tiles)
-                for b in range(steps)
+                row_piece(blocks[b], near, far, b, row, tile, rows, tiles) for b in range(steps)
             ]
             values = []
             for k, is_complex in freqs:
@@ -263,7 +288,7 @@
             quotients = divide(values, row, tile)
             for field in range(fields):
                 source[field, row, tile] = values[field]
-                first[field, row, tile, middle, :] = relax_weights[0] * quotients[field]
+                iterates[0][field, row, tile, middle, :] = relax_weights[0] * quotients[field]
 
     def sweep(row, old, weight, last):
         centers = [
@@ -298,20 +323,18 @@
                 for field in range(fields)
             ]
 
-    def middle_level(level, old, new):
-        def step(row, carry):
-            for tile, results in sweep(row, old, relax_weights[level], False):
+    for level in range(1, levels):
+
+        def step(row, carry, level=level):
+            for tile, results in sweep(row, iterates[level - 1], relax_weights[level], False):
                 for field in range(fields):
-                    new[field, row, tile, middle, :] = results[field]
+                    iterates[level][field, row, tile, middle, :] = results[field]
             return carry
 
-        lax.fori_loop(level, extended - level, step, 0)
-
-    middle_level(1, first, second)
-    middle_level(2, second, first)
+        lax.fori_loop(*rows_of(level), step, 0)
 
     def last_step(row, carry):
-        for tile, results in sweep(row, first, relax_weights[reach], True):
+        for tile, results in sweep(row, iterates[levels - 1], relax_weights[levels], True):
             for ahead in range(steps):
                 terms, place = [], 0
                 for k, is_complex in freqs:
@@ -324,21 +347,22 @@
                 outs[ahead][(row - reach) * tiles + tile] = combine(terms)
         return carry
 
-    lax.fori_loop(reach, reach + rows, last_step, 0)
-
-
-def unpack_kernel(tm, log_alpha, steps, *refs):
+    lax.fori_loop(*rows_of(levels), last_step, 0)
+
+
+def unpack_kernel(tm, space, log_alpha, steps, *refs):
     blocks, out = refs[:steps], refs[steps]
-    me = lax.axis_index(tm)
+    me, up = lax.axis_index(tm), upwards(space)
     depth, rows, columns = out.shape
     tiles = columns // steps // lanes
     scale = jnp.exp(jnp.full((depth, lanes), me.astype(jnp.float32) * -log_alpha, jnp.float32))
     for behind in range(steps):
         owner = lax.rem(me - behind + steps, steps)
-        for row in range(rows):
+        for y in range(rows):
+            row = row_of(y, rows, up)
             for tile in range(tiles):
                 place = pl.multiple_of((owner * tiles + tile) * lanes, lanes)
-                out[:, row, pl.ds(place, lanes)] = blocks[behind][row * tiles + tile] * scale
+                out[:, y, pl.ds(place, lanes)] = blocks[behind][row * tiles + tile] * scale
 
 
 def exchange(blocks, steps):
@@ -349,13 +373,13 @@
     return [blocks[0]] + moved
 
 
-def neighbours(up, down):
+def swap(value, first):
     size = lax.axis_size("space")
-    ahead = [(i, i + 1) for i in range(size - 1)]
-    return (
-        lax.ppermute(up, "space", ahead),
-        lax.ppermute(down, "space", [(j, i) for i, j in ahead]),
-    )
+    pairs = []
+    for slab in range(size):
+        partner = slab + 1 if (slab - first) % 2 == 0 else slab - 1
+        pairs.append((slab, partner if 0 <= partner < size else slab))
+    return lax.ppermute(value, "space", pairs)
 
 
 def fast_local(rhs, diffusivity, velocity):
@@ -367,40 +391,41 @@
     fields = steps
     blocks = exchange(pack(rhs[0], steps), steps)
     piece = (reach * tiles + 1, depth, lanes)
-    kappa_own, kappa_up, kappa_down = call(
-        functools.partial(kappa_kernel, "tm", rows, tiles, steps),
+    kappa_own, kappa_near, kappa_far = call(
+        functools.partial(kappa_kernel, "tm", "space", rows, tiles, steps),
         [(rows * tiles + 1, depth, lanes), piece, piece],
         diffusivity,
         from_hbm=1,
     )
-    kappa_below, kappa_above = neighbours(kappa_up, kappa_down)
     kappa, inverse = call(
         functools.partial(coefficient_kernel, "tm", "space", rows, tiles, steps),
         [(extended, wide, depth, lanes), (fields, extended, wide, depth, lanes)],
         kappa_own,
-        kappa_below,
-        kappa_above,
-    )
-    below, above = neighbours(*halos(blocks, kappa, rows, tiles))
-    padded = pltpu.VMEM((fields, extended, wide, depth + 16, lanes), jnp.float32)
-    results = call(
-        functools.partial(solve_kernel, rows, tiles, steps),
-        [(rows * tiles, depth, lanes)] * steps,
-        *blocks,
-        below,
-        above,
+        swap(kappa_near, 0),
+        swap(kappa_far, 1),
+    )
+    near, far = halos(blocks, kappa, rows, tiles)
+    far, near = swap(far, 1), swap(near, 0)
+    state = [(fields, extended, wide, depth, lanes)]
+    state += [(fields, extended, wide, depth + 16, lanes)] * reach
+    state += [(rows * tiles, depth, lanes)] * steps
+    solve = functools.partial(solve_kernel, "space", rows, tiles, steps)
+    held = call(
+        functools.partial(solve, False), state, *blocks, near, kappa, inverse, velocity
+    )
+    held = call(
+        functools.partial(solve, True),
+        state,
+        far,
         kappa,
         inverse,
         velocity,
-        scratch=[
-            pltpu.VMEM((fields, extended, wide, depth, lanes), jnp.float32),
-            padded,
-            padded,
-        ],
-    )
-    returned = exchange(results, steps)
+        *held,
+        aliases={4 + i: i for i in range(len(state))},
+    )
+    returned = exchange(held[1 + reach :], steps)
     (result,) = call(
-        functools.partial(unpack_kernel, "tm", log_alpha, steps),
+        functools.partial(unpack_kernel, "tm", "space", log_alpha, steps),
         [(depth, rows, columns)],
         *returned,
         kept=False,

time: 38.4 us -> 32.3 us (0.84)
  waiting for transfers between devices: 11.3 us -> 7.18 us
  starting transfers between devices: 19.6 us -> 16.6 us
  local copies, waits for them, and re-layouts: 0 us -> 2.55 us
  Pallas kernels: 7.13 us -> 5.74 us
    ppermute x4, waiting for transfers between devices: 8.48 us -> 3.97 us  [swap(): return lax.ppermute(value, 'space', pairs)]
    ppermute x4, starting transfers between devices: 10.8 us -> 7.69 us  [swap(): return lax.ppermute(value, 'space', pairs)]
    unnamed x0 -> x6, local copies, waits for them, and re-layouts: none -> 2.55 us
    pallas_call x6 -> x7, Pallas kernels: 7.13 us -> 5.74 us  [call(): pl.pallas_call(kernel, out_shape=[make(o, jnp.float32) for o in outs], in...]
    ppermute x6, waiting for transfers between devices: 2.8 us -> 3.21 us  [exchange(): lax.ppermute(blocks[d], 'tm', [(i, (i + d) % steps) for i in range(steps)])]
  transfers between devices with their start and end apart: 10 -> 10, of which waited for: 5 -> 4; matrix products, arithmetic and copies ran while one was open for 0% -> 0% of each run, Pallas kernels for 3% -> 7%
where the time goes in v3:
time: 32.3 us; the launch traced here: 32.1 us
  starting transfers between devices  16.6 us (51%)
  waiting for transfers between devices  7.18 us (22%)
  Pallas kernels  5.74 us (18%)
  local copies, waits for them, and re-layouts  2.55 us (8%)
    ppermute x6, starting transfers between devices, exchange(): lax.ppermute(blocks[d], 'tm', [(i, (i + d) % steps) for i in range(steps)])  8.86 us
    ppermute x4, starting transfers between devices, swap(): return lax.ppermute(value, 'space', pairs)  7.69 us
    pallas_call x7, Pallas kernels, call(): pl.pallas_call(kernel, out_shape=[make(o, jnp.float32) for o in outs], in...  5.74 us
    ppermute x4, waiting for transfers between devices, swap(): return lax.ppermute(value, 'space', pairs)  3.97 us
    ppermute x6, waiting for transfers between devices, exchange(): lax.ppermute(blocks[d], 'tm', [(i, (i + d) % steps) for i in range(steps)])  3.21 us
    unnamed x6, local copies, waits for them, and re-layouts  2.55 us
  transfers between devices with their start and end apart: 10, of which 4 were waited for; matrix products, arithmetic and copies ran while one was open for 0% of the time, Pallas kernels for 7%

profile of v3, /device:TPU:1, one launch (start us, length us, event | category | flops | bytes accessed | tf_op | source)
XLA Modules:
  0.0 32.1 jit_solution(1475953226882657094)
XLA Ops:
  0.0 0.0 copy-start
  0.0 0.9 %copy-done = f32[1,16,4,1024]{3,2,1,0:T(4,128)S(1)} copy-done((f32[1,16,4,1024]{3,2,1,0:T(4,128)S(1)}, f32[1,16,4,1024]{3,2,1,0:T(4,128)}, u32[]{:S(2)}) %copy-start) | copy-done | bytes 262168
  1.0 0.4 %shard_map.37 = (f32[9,16,128]{2,1,0:T(8,128)S(1)}, f32[9,16,128]{2,1,0:T(8,128)S(1)}, f32[9,16,128]{2,1,0:T(8,128)S(1)}, f32[9,16,128]{2,1,0:T(8,128)S(1)}) custom-call(f32[16,4,1024]{2,1,0:T(4,128)S(1)} %bitcast.2), custom_call_target="tpu_custom_call" | custom-call | tf_op jit(solution)/shard_map/pallas_call | solution.py:32
  1.4 2.2 %collective-permute-start = (f32[9,16,128]{2,1,0:T(8,128)S(1)}, f32[9,16,128]{2,1,0:T(8,128)S(1)}, u32[]{:S(2)}, u32[]{:S(2)}) collective-permute-start(f32[9,16,128]{2,1,0:T(8,128)S(1)} %get-tuple-element.29), channel_id=1, source_target_pairs={{0,4},{4,8},{8,12},{12,0},{1,5},{5,9},{9,13},{13,1},{2,6},{6,10},{... | collective-permute-start | bytes 221192 | tf_op jit(solution)/shard_map/ppermute | solution.py:370
  3.6 2.3 %collective-permute-start.1 = (f32[9,16,128]{2,1,0:T(8,128)S(1)}, f32[9,16,128]{2,1,0:T(8,128)S(1)}, u32[]{:S(2)}, u32[]{:S(2)}) collective-permute-start(f32[9,16,128]{2,1,0:T(8,128)S(1)} %get-tuple-element.30), channel_id=1, source_target_pairs={{0,8},{4,12},{8,0},{12,4},{1,9},{5,13},{9,1},{13,5},{2,10},{6,14},... | collective-permute-start | bytes 221192 | tf_op jit(solution)/shard_map/ppermute | solution.py:370
  5.9 1.1 %collective-permute-start.2 = (f32[9,16,128]{2,1,0:T(8,128)S(1)}, f32[9,16,128]{2,1,0:T(8,128)S(1)}, u32[]{:S(2)}, u32[]{:S(2)}) collective-permute-start(f32[9,16,128]{2,1,0:T(8,128)S(1)} %get-tuple-element.31), channel_id=1, source_target_pairs={{0,12},{4,0},{8,4},{12,8},{1,13},{5,1},{9,5},{13,9},{2,14},{6,2},{... | collective-permute-start | bytes 221192 | tf_op jit(solution)/shard_map/ppermute | solution.py:370
  6.9 0.0 copy-start.1
  6.9 0.9 %copy-done.1 = f32[16,4,1024]{2,1,0:T(4,128)S(1)} copy-done((f32[16,4,1024]{2,1,0:T(4,128)S(1)}, f32[16,4,1024]{2,1,0:T(4,128)}, u32[]{:S(2)}) %copy-start.1) | copy-done | bytes 262168
  7.9 0.1 shard_map.38
  8.0 1.6 %collective-permute-start.3 = (f32[7,16,128]{2,1,0:T(8,128)S(1)}, f32[7,16,128]{2,1,0:T(8,128)S(1)}, u32[]{:S(2)}, u32[]{:S(2)}) collective-permute-start(f32[7,16,128]{2,1,0:T(8,128)S(1)} %get-tuple-element.33), channel_id=1, source_target_pairs={{0,1},{1,0},{2,3},{3,2},{4,5},{5,4},{6,7},{7,6},{8,9},{9,8},{10,11... | collective-permute-start | bytes 172040 | tf_op jit(solution)/shard_map/ppermute | solution.py:382
  9.6 3.0 %collective-permute-start.4 = (f32[7,16,128]{2,1,0:T(8,128)S(1)}, f32[7,16,128]{2,1,0:T(8,128)S(1)}, u32[]{:S(2)}, u32[]{:S(2)}) collective-permute-start(f32[7,16,128]{2,1,0:T(8,128)S(1)} %get-tuple-element.34), channel_id=1, source_target_pairs={{0,0},{1,2},{2,1},{3,3},{4,4},{5,6},{6,5},{7,7},{8,8},{9,10},{10,9... | collective-permute-start | bytes 172040 | tf_op jit(solution)/shard_map/ppermute | solution.py:382
  12.6 0.0 collective-permute-done.3.near
  12.6 2.4 %collective-permute-done.4.far = f32[7,16,128]{2,1,0:T(8,128)S(1)} collective-permute-done((f32[7,16,128]{2,1,0:T(8,128)S(1)}, f32[7,16,128]{2,1,0:T(8,128)S(1)}, u32[]{:S(2)}, u32[]{:S(2)}) %collective-permute-start.4) | collective-permute-done | bytes 57376 | tf_op jit(solution)/shard_map/ppermute | solution.py:382
  15.1 0.1 shard_map.39
  15.2 0.0 collective-permute-done.refs_1_
  15.2 0.0 collective-permute-done.1.refs_2_
  15.2 0.0 collective-permute-done.2.refs_3_
  15.3 0.1 collective-permute-start.6
  15.4 3.0 %collective-permute-start.5 = (f32[28,16,128]{2,1,0:T(8,128)S(1)}, f32[28,16,128]{2,1,0:T(8,128)S(1)}, u32[]{:S(2)}, u32[]{:S(2)}) collective-permute-start(f32[28,16,128]{2,1,0:T(8,128)S(1)} %get-tuple-element.36), channel_id=1, source_target_pairs={{0,0},{1,2},{2,1},{3,3},{4,4},{5,6},{6,5},{7,7},{8,8},{9,10},{10,9... | collective-permute-start | bytes 688136 | tf_op jit(solution)/shard_map/ppermute | solution.py:382
  18.4 0.0 collective-permute-done.6.refs_4_
  18.4 0.0 copy-start.2
  18.4 0.6 %copy-done.2 = f32[3]{0:T(128)S(1)} copy-done((f32[3]{0:T(128)S(1)}, f32[3]{0:T(128)}, u32[]{:S(2)}) %copy-start.2) | copy-done | bytes 36
  19.1 2.1 %shard_map.41 = (f32[4,10,3,16,128]{4,3,2,1,0:T(8,128)S(1)}, f32[4,10,3,32,128]{4,3,2,1,0:T(8,128)S(1)}, f32[4,10,3,32,128]{4,3,2,1,0:T(8,128)S(1)}, f32[4,10,3,...) custom-call(f32[9,16,128]{2,1,0:T(8,128)S(1)} %get-tuple-element.28., ...), custom_call_target="tpu_custom_call" | custom-call | tf_op jit(solution)/shard_map/pallas_call | solution.py:32
  21.2 1.5 %collective-permute-done.5.refs_0_ = f32[28,16,128]{2,1,0:T(8,128)S(1)} collective-permute-done((f32[28,16,128]{2,1,0:T(8,128)S(1)}, f32[28,16,128]{2,1,0:T(8,128)S(1)}, u32[]{:S(2)}, u32[]{:S(2)}) %collective-permute-start.5) | collective-permute-done | bytes 229408 | tf_op jit(solution)/shard_map/ppermute | solution.py:382
  22.7 1.9 %shard_map.42 = (f32[4,10,3,16,128]{4,3,2,1,0:T(8,128)S(1)}, f32[4,10,3,32,128]{4,3,2,1,0:T(8,128)S(1)}, f32[4,10,3,32,128]{4,3,2,1,0:T(8,128)S(1)}, f32[4,10,3,...) custom-call(f32[28,16,128]{2,1,0:T(8,128)S(1)} %collective-permute-d, ...), custom_call_target="tpu_custom_call", output_to_operand_aliasing={{0}: (4, {}), {1}: (5, {}), {2}: (6, {}), {3}: (7, {}), {4}... | custom-call | tf_op jit(solution)/shard_map/pallas_call | solution.py:32
  24.6 0.5 %collective-permute-start.7 = (f32[8,16,128]{2,1,0:T(8,128)S(1)}, f32[8,16,128]{2,1,0:T(8,128)S(1)}, u32[]{:S(2)}, u32[]{:S(2)}) collective-permute-start(f32[8,16,128]{2,1,0:T(8,128)S(1)} %get-tuple-element.48), channel_id=1, source_target_pairs={{0,4},{4,8},{8,12},{12,0},{1,5},{5,9},{9,13},{13,1},{2,6},{6,10},{... | collective-permute-start | bytes 196616 | tf_op jit(solution)/shard_map/ppermute | solution.py:370
  25.1 0.1 collective-permute-start.8
  25.1 2.8 %collective-permute-start.9 = (f32[8,16,128]{2,1,0:T(8,128)S(1)}, f32[8,16,128]{2,1,0:T(8,128)S(1)}, u32[]{:S(2)}, u32[]{:S(2)}) collective-permute-start(f32[8,16,128]{2,1,0:T(8,128)S(1)} %get-tuple-element.50), channel_id=1, source_target_pairs={{0,12},{4,0},{8,4},{12,8},{1,13},{5,1},{9,5},{13,9},{2,14},{6,2},{... | collective-permute-start | bytes 196616 | tf_op jit(solution)/shard_map/ppermute | solution.py:370
  27.9 1.8 %collective-permute-done.7.refs_1_ = f32[8,16,128]{2,1,0:T(8,128)S(1)} collective-permute-done((f32[8,16,128]{2,1,0:T(8,128)S(1)}, f32[8,16,128]{2,1,0:T(8,128)S(1)}, u32[]{:S(2)}, u32[]{:S(2)}) %collective-permute-start.7) | collective-permute-done | bytes 65568 | tf_op jit(solution)/shard_map/ppermute | solution.py:370
  29.7 1.4 %collective-permute-done.8.refs_2_ = f32[8,16,128]{2,1,0:T(8,128)S(1)} collective-permute-done((f32[8,16,128]{2,1,0:T(8,128)S(1)}, f32[8,16,128]{2,1,0:T(8,128)S(1)}, u32[]{:S(2)}, u32[]{:S(2)}) %collective-permute-start.8) | collective-permute-done | bytes 65568 | tf_op jit(solution)/shard_map/ppermute | solution.py:370
  31.1 0.0 collective-permute-done.9.refs_3_
  31.1 1.0 %shard_map.43 = f32[16,4,1024]{2,1,0:T(4,128)} custom-call(f32[8,16,128]{2,1,0:T(8,128)S(1)} %get-tuple-element.47.refs_0_, f32[8,16,128]{2,1,0:T(8,128)S(1)} %collective-permute-done.7.refs_1_, f32[8,16,128]{2,1,0:T(8,128)S(1)} %collective-permute-done.8.refs_2_, f32[8,16,128]{2,1,0:T(8,128)S(1)} %collective-permute-done.9.refs_3_), custom_call_target="tpu_custom_call" | custom-call | tf_op jit(solution)/shard_map/pallas_call | solution.py:32
  (1 shorter events, 0.0 us)
Async XLA Ops:
  0.0 0.9 %copy-start = (f32[1,16,4,1024]{3,2,1,0:T(4,128)S(1)}, f32[1,16,4,1024]{3,2,1,0:T(4,128)}, u32[]{:S(2)}) copy-start(f32[1,16,4,1024]{3,2,1,0:T(4,128)} %param.3) | copy-start | bytes 786436
  1.4 13.8 %collective-permute-start = (f32[9,16,128]{2,1,0:T(8,128)S(1)}, f32[9,16,128]{2,1,0:T(8,128)S(1)}, u32[]{:S(2)}, u32[]{:S(2)}) collective-permute-start(f32[9,16,128]{2,1,0:T(8,128)S(1)} %get-tuple-element.29), channel_id=1, source_target_pairs={{0,4},{4,8},{8,12},{12,0},{1,5},{5,9},{9,13},{13,1},{2,6},{6,10},{... | collective-permute-start | bytes 221192 | tf_op jit(solution)/shard_map/ppermute | solution.py:370
  3.6 11.7 %collective-permute-start.1 = (f32[9,16,128]{2,1,0:T(8,128)S(1)}, f32[9,16,128]{2,1,0:T(8,128)S(1)}, u32[]{:S(2)}, u32[]{:S(2)}) collective-permute-start(f32[9,16,128]{2,1,0:T(8,128)S(1)} %get-tuple-element.30), channel_id=1, source_target_pairs={{0,8},{4,12},{8,0},{12,4},{1,9},{5,13},{9,1},{13,5},{2,10},{6,14},... | collective-permute-start | bytes 221192 | tf_op jit(solution)/shard_map/ppermute | solution.py:370
  5.9 9.4 %collective-permute-start.2 = (f32[9,16,128]{2,1,0:T(8,128)S(1)}, f32[9,16,128]{2,1,0:T(8,128)S(1)}, u32[]{:S(2)}, u32[]{:S(2)}) collective-permute-start(f32[9,16,128]{2,1,0:T(8,128)S(1)} %get-tuple-element.31), channel_id=1, source_target_pairs={{0,12},{4,0},{8,4},{12,8},{1,13},{5,1},{9,5},{13,9},{2,14},{6,2},{... | collective-permute-start | bytes 221192 | tf_op jit(solution)/shard_map/ppermute | solution.py:370
  6.9 0.9 %copy-start.1 = (f32[16,4,1024]{2,1,0:T(4,128)S(1)}, f32[16,4,1024]{2,1,0:T(4,128)}, u32[]{:S(2)}) copy-start(f32[16,4,1024]{2,1,0:T(4,128)} %kappa.1) | copy-start | bytes 786436
  8.0 4.6 %collective-permute-start.3 = (f32[7,16,128]{2,1,0:T(8,128)S(1)}, f32[7,16,128]{2,1,0:T(8,128)S(1)}, u32[]{:S(2)}, u32[]{:S(2)}) collective-permute-start(f32[7,16,128]{2,1,0:T(8,128)S(1)} %get-tuple-element.33), channel_id=1, source_target_pairs={{0,1},{1,0},{2,3},{3,2},{4,5},{5,4},{6,7},{7,6},{8,9},{9,8},{10,11... | collective-permute-start | bytes 172040 | tf_op jit(solution)/shard_map/ppermute | solution.py:382
  9.6 5.5 %collective-permute-start.4 = (f32[7,16,128]{2,1,0:T(8,128)S(1)}, f32[7,16,128]{2,1,0:T(8,128)S(1)}, u32[]{:S(2)}, u32[]{:S(2)}) collective-permute-start(f32[7,16,128]{2,1,0:T(8,128)S(1)} %get-tuple-element.34), channel_id=1, source_target_pairs={{0,0},{1,2},{2,1},{3,3},{4,4},{5,6},{6,5},{7,7},{8,8},{9,10},{10,9... | collective-permute-start | bytes 172040 | tf_op jit(solution)/shard_map/ppermute | solution.py:382
  15.3 3.1 %collective-permute-start.6 = (f32[28,16,128]{2,1,0:T(8,128)S(1)}, f32[28,16,128]{2,1,0:T(8,128)S(1)}, u32[]{:S(2)}, u32[]{:S(2)}) collective-permute-start(f32[28,16,128]{2,1,0:T(8,128)S(1)} %get-tuple-element.38), channel_id=1, source_target_pairs={{0,1},{1,0},{2,3},{3,2},{4,5},{5,4},{6,7},{7,6},{8,9},{9,8},{10,11... | collective-permute-start | bytes 688136 | tf_op jit(solution)/shard_map/ppermute | solution.py:382
  15.4 7.3 %collective-permute-start.5 = (f32[28,16,128]{2,1,0:T(8,128)S(1)}, f32[28,16,128]{2,1,0:T(8,128)S(1)}, u32[]{:S(2)}, u32[]{:S(2)}) collective-permute-start(f32[28,16,128]{2,1,0:T(8,128)S(1)} %get-tuple-element.36), channel_id=1, source_target_pairs={{0,0},{1,2},{2,1},{3,3},{4,4},{5,6},{6,5},{7,7},{8,8},{9,10},{10,9... | collective-permute-start | bytes 688136 | tf_op jit(solution)/shard_map/ppermute | solution.py:382
  18.4 0.7 %copy-start.2 = (f32[3]{0:T(128)S(1)}, f32[3]{0:T(128)}, u32[]{:S(2)}) copy-start(f32[3]{0:T(128)} %refs_3_.1) | copy-start | bytes 40
  24.6 5.1 %collective-permute-start.7 = (f32[8,16,128]{2,1,0:T(8,128)S(1)}, f32[8,16,128]{2,1,0:T(8,128)S(1)}, u32[]{:S(2)}, u32[]{:S(2)}) collective-permute-start(f32[8,16,128]{2,1,0:T(8,128)S(1)} %get-tuple-element.48), channel_id=1, source_target_pairs={{0,4},{4,8},{8,12},{12,0},{1,5},{5,9},{9,13},{13,1},{2,6},{6,10},{... | collective-permute-start | bytes 196616 | tf_op jit(solution)/shard_map/ppermute | solution.py:370
  25.1 6.1 %collective-permute-start.8 = (f32[8,16,128]{2,1,0:T(8,128)S(1)}, f32[8,16,128]{2,1,0:T(8,128)S(1)}, u32[]{:S(2)}, u32[]{:S(2)}) collective-permute-start(f32[8,16,128]{2,1,0:T(8,128)S(1)} %get-tuple-element.49), channel_id=1, source_target_pairs={{0,8},{4,12},{8,0},{12,4},{1,9},{5,13},{9,1},{13,5},{2,10},{6,14},... | collective-permute-start | bytes 196616 | tf_op jit(solution)/shard_map/ppermute | solution.py:370
  25.1 6.0 %collective-permute-start.9 = (f32[8,16,128]{2,1,0:T(8,128)S(1)}, f32[8,16,128]{2,1,0:T(8,128)S(1)}, u32[]{:S(2)}, u32[]{:S(2)}) collective-permute-start(f32[8,16,128]{2,1,0:T(8,128)S(1)} %get-tuple-element.50), channel_id=1, source_target_pairs={{0,12},{4,0},{8,4},{12,8},{1,13},{5,1},{9,5},{13,9},{2,14},{6,2},{... | collective-permute-start | bytes 196616 | tf_op jit(solution)/shard_map/ppermute | solution.py:370

commit v4 on v3

--- a/solution.py
+++ b/solution.py
@@ -21,19 +21,24 @@
 lanes = 128
 vmem = pl.BlockSpec(memory_space=pltpu.VMEM)
 smem = pl.BlockSpec(memory_space=pltpu.SMEM)
-
-
-def call(kernel, outs, *operands, from_hbm=0, kept=True, aliases=None):
+hbm = pl.BlockSpec(memory_space=pltpu.HBM)
+
+
+def call(kernel, outs, *operands, specs=None, kept=True, aliases=None, scratch=()):
+    specs = specs or {}
     on_chip = [
-        x if i < from_hbm or x.ndim == 1 else pltpu.with_memory_space_constraint(x, pltpu.VMEM)
+        x
+        if specs.get(i) is smem
+        else pltpu.with_memory_space_constraint(x, pltpu.HBM if i in specs else pltpu.VMEM)
         for i, x in enumerate(operands)
     ]
     make = pltpu.VMEM if kept else jax.ShapeDtypeStruct
     return pl.pallas_call(
         kernel,
         out_shape=[make(o, jnp.float32) for o in outs],
-        in_specs=[smem if x.ndim == 1 else vmem for x in operands],
-        out_specs=[vmem] * len(outs),
+        in_specs=[specs.get(i, vmem) for i in range(len(operands))],
+        out_specs=[vmem if kept else hbm] * len(outs),
+        scratch_shapes=scratch,
         input_output_aliases=aliases or {},
         compiler_params=pltpu.CompilerParams(vmem_limit_bytes=16 << 20),
     )(*on_chip)
@@ -78,9 +83,26 @@
     write(rows * tiles, packed)
 
 
-def pack_kernel(tm, space, log_alpha, steps, rhs, *outs):
+def fetch(source, target, semaphores):
+    pieces = semaphores.shape[0]
+    size = source.shape[0] // pieces
+    copies = [
+        pltpu.make_async_copy(
+            source.at[pl.ds(i * size, size)], target.at[pl.ds(i * size, size)], semaphores.at[i]
+        )
+        for i in range(pieces)
+    ]
+    for copy in copies:
+        copy.start()
+    for copy in copies:
+        copy.wait()
+
+
+def pack_kernel(tm, space, log_alpha, steps, rhs, *refs):
+    outs, (held, semaphores) = refs[:steps], refs[steps:]
     me, up = lax.axis_index(tm), upwards(space)
     depth = rhs.shape[0]
+    fetch(rhs, held, semaphores)
     scale = jnp.exp(jnp.full((depth, lanes), me.astype(jnp.float32) * log_alpha, jnp.float32))
     for ahead in range(steps):
         out = outs[ahead]
@@ -88,7 +110,12 @@
         def write(index, value, out=out):
             out[index] = value * scale
 
-        pick_block(rhs, write, lax.rem(me + ahead, steps), steps, up)
+        pick_block(held, write, lax.rem(me + ahead, steps), steps, up)
+
+
+def staging(shape):
+    pieces = math.gcd(shape[0], 4)
+    return [pltpu.VMEM(shape, jnp.float32), pltpu.SemaphoreType.DMA((pieces,))]
 
 
 def pack(rhs, steps):
@@ -96,15 +123,16 @@
     tiles = columns // steps // lanes
     log_alpha = math.log(circ_alpha) / steps
     kernel = functools.partial(pack_kernel, "tm", "space", log_alpha, steps)
-    return call(kernel, [(rows * tiles + 1, depth, lanes)] * steps, rhs, from_hbm=1)
+    out = (rows * tiles + 1, depth, lanes)
+    return call(kernel, [out] * steps, rhs, specs={0: hbm}, scratch=staging(rhs.shape))
 
 
 def first_row(near, rows):
     return 0 if near else rows - reach
 
 
-def halo_kernel(rows, tiles, steps, *refs):
-    blocks, (_, near, far) = refs[:steps], refs[steps:]
+def halo_kernel(rows, tiles, count, *refs):
+    blocks, (near, far) = refs[:count], refs[count:]
     piece = reach * tiles + 1
     for step, block in enumerate(blocks):
         for out, is_near in ((near, True), (far, False)):
@@ -114,25 +142,11 @@
             out[step * piece + reach * tiles] = block[rows * tiles]
 
 
-def halos(blocks, ready, rows, tiles):
+def halos(blocks, rows, tiles):
     depth = blocks[0].shape[1]
     out = (len(blocks) * (reach * tiles + 1), depth, lanes)
     kernel = functools.partial(halo_kernel, rows, tiles, len(blocks))
-    return call(kernel, [out, out], *blocks, ready)
-
-
-def kappa_kernel(tm, space, rows, tiles, steps, kappa, own, near, far):
-    me, up = lax.axis_index(tm), upwards(space)
-
-    def write(index, value):
-        own[index] = value
-
-    pick_block(kappa, write, me, steps, up)
-    for out, is_near in ((near, True), (far, False)):
-        start = first_row(is_near, rows) * tiles
-        for place in range(reach * tiles):
-            out[place] = own[start + place]
-        out[reach * tiles] = own[rows * tiles]
+    return call(kernel, [out, out], *blocks)
 
 
 def row_piece(own, near, far, step, row, tile, rows, tiles):
@@ -158,39 +172,61 @@
     return [(k, 2 * k % steps != 0) for k in range(steps // 2 + 1)]
 
 
-def coefficient_kernel(tm, space, rows, tiles, steps, own, near, far, kappa, inverse):
-    me, slab, up = lax.axis_index(tm), lax.axis_index(space), upwards(space)
-    slabs = lax.axis_size(space)
-    depth = own.shape[1]
+def write_coefficients(row, tile, value, mask, steps, kappa, inverse):
+    shift_factor = circ_alpha ** (1.0 / steps)
+    kappa[row, tile] = value
+    place = 0
+    for k, is_complex in frequencies(steps):
+        phase = 2.0 * math.pi * k / steps
+        real = (1.0 - shift_factor * math.cos(phase)) + 6.0 * value
+        if is_complex:
+            imag = shift_factor * math.sin(phase)
+            reciprocal = 1.0 / (real * real + imag * imag)
+            pair = (real * reciprocal, imag * reciprocal)
+        else:
+            pair = (1.0 / real,)
+        for part in pair:
+            inverse[place, row, tile] = part if mask is None else part * mask
+            place += 1
+
+
+def side_mask(tm, steps, depth):
+    me = lax.axis_index(tm)
     keep_right, keep_left = column_mask(
         (me > 0).astype(jnp.float32), (me < steps - 1).astype(jnp.float32), (depth, lanes)
     )
-    halo_mask = keep_right + keep_left
-    shift_factor = circ_alpha ** (1.0 / steps)
-    has_lower, has_upper = slab > 0, slab < slabs - 1
-    has_near = jnp.where(up == 1, has_lower, has_upper).astype(jnp.float32)
-    has_far = jnp.where(up == 1, has_upper, has_lower).astype(jnp.float32)
-    for row in range(rows + 2 * reach):
-        inside = has_near if row < reach else has_far if row >= reach + rows else None
+    return keep_right + keep_left
+
+
+def prepare_kernel(tm, space, rows, tiles, steps, diffusivity, velocity, *refs):
+    own, kappa, inverse, drift, *iterates = refs[:-2]
+    held, semaphores = refs[-2:]
+    up = upwards(space)
+    depth = diffusivity.shape[0]
+    direction = (2 * up - 1).astype(jnp.float32)
+    for j in range(3):
+        speed = 0.5 * velocity[j]
+        drift[j] = jnp.full((depth, lanes), speed * direction if j == 1 else speed, jnp.float32)
+    zero = jnp.zeros((8, lanes), jnp.float32)
+    for level, ref in enumerate(iterates):
+        fields, extended, wide = ref.shape[:3]
+        for field in range(fields):
+            for row in range(level, extended - level):
+                for tile in range(wide):
+                    ref[field, row, tile, pl.ds(0, 8), :] = zero
+                    ref[field, row, tile, pl.ds(8 + depth, 8), :] = zero
+    fetch(diffusivity, held, semaphores)
+
+    def write(index, value):
+        own[index] = value
+
+    pick_block(held, write, lax.axis_index(tm), steps, up)
+    halo_mask = side_mask(tm, steps, depth)
+    for row in range(reach, reach + rows):
         for tile in range(tiles + 1):
-            value = row_piece(own, near, far, 0, row, tile, rows, tiles)
-            kappa[row, tile] = value
+            value = row_piece(own, None, None, 0, row, tile, rows, tiles)
             mask = halo_mask if tile == tiles else None
-            if inside is not None:
-                mask = mask * inside if mask is not None else jnp.full((depth, lanes), inside)
-            place = 0
-            for k, is_complex in frequencies(steps):
-                phase = 2.0 * math.pi * k / steps
-                real = (1.0 - shift_factor * math.cos(phase)) + 6.0 * value
-                if is_complex:
-                    imag = shift_factor * math.sin(phase)
-                    reciprocal = 1.0 / (real * real + imag * imag)
-                    pair = (real * reciprocal, imag * reciprocal)
-                else:
-                    pair = (1.0 / real,)
-                for part in pair:
-                    inverse[place, row, tile] = part if mask is None else part * mask
-                    place += 1
+            write_coefficients(row, tile, value, mask, steps, kappa, inverse)
 
 
 def combine(terms):
@@ -221,28 +257,27 @@
     return exact(math.sin(2.0 * math.pi * (product % steps) / steps))
 
 
-def solve_kernel(space, rows, tiles, steps, second_half, *refs):
+def solve_kernel(tm, space, rows, tiles, steps, second_half, *refs):
     freqs = frequencies(steps)
     fields = sum(2 if c else 1 for _, c in freqs)
     levels = reach
+    made = 2 + levels
     if second_half:
-        far, kappa, inverse, velocity = refs[:4]
-        refs = refs[5 + levels + steps :]
-        source, *iterates = refs[: 1 + levels]
-        outs = refs[1 + levels :]
+        far, drift = refs[:2]
+        kappa, inverse, *iterates = refs[2 + made + 1 + steps :][:made]
+        source, *outs = refs[2 + made + 1 + steps + made :]
         blocks, near = [None] * steps, None
     else:
-        blocks, (near, kappa, inverse, velocity) = refs[:steps], refs[steps : steps + 4]
-        source, *iterates = refs[steps + 4 : steps + 5 + levels]
-        outs = refs[steps + 5 + levels :]
+        blocks, (near, drift) = refs[:steps], refs[steps : steps + 2]
+        kappa, inverse, *iterates = refs[steps + 2 + made :][:made]
+        source, *outs = refs[steps + 2 + made + made :]
         far = None
     depth = kappa.shape[2]
     pad = 8
     middle = pl.ds(pad, depth)
     lane = lax.broadcasted_iota(jnp.int32, (depth, lanes), 1)
     at_first, at_last = lane == 0, lane == lanes - 1
-    direction = (2 * upwards(space) - 1).astype(jnp.float32)
-    half = [0.5 * velocity[0], 0.5 * direction * velocity[1], 0.5 * velocity[2]]
+    half = [drift[j] for j in range(3)]
     known = reach + rows
     extended = known + reach
     wide = tiles + 1
@@ -251,14 +286,17 @@
         split = known - level
         return (split, extended - level) if second_half else (level, split)
 
-    if not second_half:
-        zero = jnp.zeros((8, lanes), jnp.float32)
-        for level, ref in enumerate(iterates):
-            for field in range(fields):
-                for row in range(level, extended - level):
-                    for tile in range(wide):
-                        ref[field, row, tile, pl.ds(0, 8), :] = zero
-                        ref[field, row, tile, pl.ds(pad + depth, 8), :] = zero
+    slab, slabs, up = lax.axis_index(space), lax.axis_size(space), upwards(space)
+    beyond = slab < slabs - 1 if second_half else slab > 0
+    before = slab > 0 if second_half else slab < slabs - 1
+    inside = jnp.where(up == 1, beyond, before).astype(jnp.float32)
+    halo_mask = side_mask(tm, steps, depth) * inside
+    row_mask = jnp.full((depth, lanes), inside, jnp.float32)
+    for row in range(known, extended) if second_half else range(reach):
+        for tile in range(wide):
+            value = row_piece(None, near, far, steps, row, tile, rows, tiles)
+            mask = halo_mask if tile == tiles else row_mask
+            write_coefficients(row, tile, value, mask, steps, kappa, inverse)
 
     def divide(values, row, tile):
         result, place = [], 0
@@ -351,18 +389,29 @@
 
 
 def unpack_kernel(tm, space, log_alpha, steps, *refs):
-    blocks, out = refs[:steps], refs[steps]
+    blocks, (out, held, semaphores) = refs[:steps], refs[steps:]
     me, up = lax.axis_index(tm), upwards(space)
     depth, rows, columns = out.shape
-    tiles = columns // steps // lanes
+    width = columns // steps
+    tiles = width // lanes
     scale = jnp.exp(jnp.full((depth, lanes), me.astype(jnp.float32) * -log_alpha, jnp.float32))
+    copies = []
     for behind in range(steps):
         owner = lax.rem(me - behind + steps, steps)
         for y in range(rows):
             row = row_of(y, rows, up)
             for tile in range(tiles):
                 place = pl.multiple_of((owner * tiles + tile) * lanes, lanes)
-                out[:, y, pl.ds(place, lanes)] = blocks[behind][row * tiles + tile] * scale
+                held[:, y, pl.ds(place, lanes)] = blocks[behind][row * tiles + tile] * scale
+        part = pl.ds(pl.multiple_of(owner * width, lanes), width)
+        copies.append(
+            pltpu.make_async_copy(
+                held.at[:, :, part], out.at[:, :, part], semaphores.at[behind]
+            )
+        )
+        copies[-1].start()
+    for copy in copies:
+        copy.wait()
 
 
 def exchange(blocks, steps):
@@ -374,12 +423,15 @@
 
 
 def swap(value, first):
-    size = lax.axis_size("space")
+    size, steps = lax.axis_size("space"), lax.axis_size("tm")
     pairs = []
-    for slab in range(size):
-        partner = slab + 1 if (slab - first) % 2 == 0 else slab - 1
-        pairs.append((slab, partner if 0 <= partner < size else slab))
-    return lax.ppermute(value, "space", pairs)
+    for step in range(steps):
+        beside = step ^ 1 if steps % 2 == 0 else (step + 1) % steps
+        for slab in range(size):
+            partner = slab + 1 if (slab - first) % 2 == 0 else slab - 1
+            target = (step, partner) if 0 <= partner < size else (beside, slab)
+            pairs.append((step * size + slab, target[0] * size + target[1]))
+    return lax.ppermute(value, ("tm", "space"), pairs)
 
 
 def fast_local(rhs, diffusivity, velocity):
@@ -390,45 +442,48 @@
     extended, wide = rows + 2 * reach, tiles + 1
     fields = steps
     blocks = exchange(pack(rhs[0], steps), steps)
-    piece = (reach * tiles + 1, depth, lanes)
-    kappa_own, kappa_near, kappa_far = call(
-        functools.partial(kappa_kernel, "tm", "space", rows, tiles, steps),
-        [(rows * tiles + 1, depth, lanes), piece, piece],
+    made = [(extended, wide, depth, lanes), (fields, extended, wide, depth, lanes)]
+    iterates = [(fields, extended, wide, depth + 16, lanes)] * reach
+    own, kappa, inverse, drift, *margins = call(
+        functools.partial(prepare_kernel, "tm", "space", rows, tiles, steps),
+        [(rows * tiles + 1, depth, lanes), *made, (3, depth, lanes), *iterates],
         diffusivity,
-        from_hbm=1,
-    )
-    kappa, inverse = call(
-        functools.partial(coefficient_kernel, "tm", "space", rows, tiles, steps),
-        [(extended, wide, depth, lanes), (fields, extended, wide, depth, lanes)],
-        kappa_own,
-        swap(kappa_near, 0),
-        swap(kappa_far, 1),
-    )
-    near, far = halos(blocks, kappa, rows, tiles)
+        velocity,
+        specs={0: hbm, 1: smem},
+        scratch=staging(diffusivity.shape),
+    )
+    near, far = halos([*blocks, own], rows, tiles)
     far, near = swap(far, 1), swap(near, 0)
-    state = [(fields, extended, wide, depth, lanes)]
-    state += [(fields, extended, wide, depth + 16, lanes)] * reach
-    state += [(rows * tiles, depth, lanes)] * steps
-    solve = functools.partial(solve_kernel, "space", rows, tiles, steps)
+    state = [*made, *iterates, made[1]] + [(rows * tiles, depth, lanes)] * steps
+    solve = functools.partial(solve_kernel, "tm", "space", rows, tiles, steps)
+    kept = [kappa, inverse, *margins]
     held = call(
-        functools.partial(solve, False), state, *blocks, near, kappa, inverse, velocity
+        functools.partial(solve, False),
+        state,
+        *blocks,
+        near,
+        drift,
+        *kept,
+        aliases={steps + 2 + i: i for i in range(len(kept))},
     )
     held = call(
         functools.partial(solve, True),
         state,
         far,
-        kappa,
-        inverse,
-        velocity,
+        drift,
         *held,
-        aliases={4 + i: i for i in range(len(state))},
-    )
-    returned = exchange(held[1 + reach :], steps)
+        aliases={2 + i: i for i in range(len(state))},
+    )
+    returned = exchange(held[len(kept) + 1 :], steps)
     (result,) = call(
         functools.partial(unpack_kernel, "tm", "space", log_alpha, steps),
         [(depth, rows, columns)],
         *returned,
         kept=False,
+        scratch=[
+            pltpu.VMEM((depth, rows, columns), jnp.float32),
+            pltpu.SemaphoreType.DMA((steps,)),
+        ],
     )
     return result[None]
 

time: 32.3 us -> 30.8 us (0.954)
  the two profiles are of different devices: /device:TPU:1 before, /device:TPU:0 now
where the time goes in v4:
time: 30.8 us; the launch traced here: 30.6 us
  starting transfers between devices  13.7 us (44%)
  waiting for transfers between devices  9.06 us (29%)
  Pallas kernels  7.16 us (23%)
  local copies, waits for them, and re-layouts  0.65 us (2%)
    ppermute x6, starting transfers between devices, exchange(): lax.ppermute(blocks[d], 'tm', [(i, (i + d) % steps) for i in range(steps)])  11.7 us
    pallas_call x6, Pallas kernels, call(): pl.pallas_call(kernel, out_shape=[make(o, jnp.float32) for o in outs], in...  7.16 us
    ppermute x6, waiting for transfers between devices, exchange(): lax.ppermute(blocks[d], 'tm', [(i, (i + d) % steps) for i in range(steps)])  5.74 us
    ppermute x2, waiting for transfers between devices, swap(): return lax.ppermute(value, ('tm', 'space'), pairs)  3.32 us
    ppermute x2, starting transfers between devices, swap(): return lax.ppermute(value, ('tm', 'space'), pairs)  1.94 us
    unnamed x2, local copies, waits for them, and re-layouts  0.65 us
  transfers between devices with their start and end apart: 8, of which 6 were waited for; matrix products, arithmetic and copies ran while one was open for 0% of the time, Pallas kernels for 11%

profile of v4, /device:TPU:0, one launch (start us, length us, event | category | flops | bytes accessed | tf_op | source)
XLA Modules:
  0.0 30.6 jit_solution(13094231078405898460)
XLA Ops:
  0.0 1.4 %shard_map.37 = (f32[9,16,128]{2,1,0:T(8,128)S(1)}, f32[9,16,128]{2,1,0:T(8,128)S(1)}, f32[9,16,128]{2,1,0:T(8,128)S(1)}, f32[9,16,128]{2,1,0:T(8,128)S(1)}) custom-call(f32[16,4,1024]{2,1,0:T(4,128)} %bitcast.2), custom_call_target="tpu_custom_call" | custom-call | tf_op jit(solution)/shard_map/pallas_call | solution.py:36
  1.4 3.1 %collective-permute-start = (f32[9,16,128]{2,1,0:T(8,128)S(1)}, f32[9,16,128]{2,1,0:T(8,128)S(1)}, u32[]{:S(2)}, u32[]{:S(2)}) collective-permute-start(f32[9,16,128]{2,1,0:T(8,128)S(1)} %get-tuple-element.33), channel_id=1, source_target_pairs={{0,4},{4,8},{8,12},{12,0},{1,5},{5,9},{9,13},{13,1},{2,6},{6,10},{... | collective-permute-start | bytes 221192 | tf_op jit(solution)/shard_map/ppermute | solution.py:419
  4.5 2.6 %collective-permute-start.1 = (f32[9,16,128]{2,1,0:T(8,128)S(1)}, f32[9,16,128]{2,1,0:T(8,128)S(1)}, u32[]{:S(2)}, u32[]{:S(2)}) collective-permute-start(f32[9,16,128]{2,1,0:T(8,128)S(1)} %get-tuple-element.34), channel_id=1, source_target_pairs={{0,8},{4,12},{8,0},{12,4},{1,9},{5,13},{9,1},{13,5},{2,10},{6,14},... | collective-permute-start | bytes 221192 | tf_op jit(solution)/shard_map/ppermute | solution.py:419
  7.1 1.3 %collective-permute-start.2 = (f32[9,16,128]{2,1,0:T(8,128)S(1)}, f32[9,16,128]{2,1,0:T(8,128)S(1)}, u32[]{:S(2)}, u32[]{:S(2)}) collective-permute-start(f32[9,16,128]{2,1,0:T(8,128)S(1)} %get-tuple-element.35), channel_id=1, source_target_pairs={{0,12},{4,0},{8,4},{12,8},{1,13},{5,1},{9,5},{13,9},{2,14},{6,2},{... | collective-permute-start | bytes 221192 | tf_op jit(solution)/shard_map/ppermute | solution.py:419
  8.5 0.0 copy-start
  8.5 0.7 %copy-done = f32[3]{0:T(128)S(1)} copy-done((f32[3]{0:T(128)S(1)}, f32[3]{0:T(128)}, u32[]{:S(2)}) %copy-start) | copy-done | bytes 36
  9.1 1.9 %shard_map.38 = (f32[9,16,128]{2,1,0:T(8,128)S(1)}, f32[10,3,16,128]{3,2,1,0:T(8,128)S(1)}, f32[4,10,3,16,128]{4,3,2,1,0:T(8,128)S(1)}, f32[3,16,128]{2,1,0:T(8,...) custom-call(f32[16,4,1024]{2,1,0:T(4,128)} %diffusivity.1, ...), custom_call_target="tpu_custom_call" | custom-call | tf_op jit(solution)/shard_map/pallas_call | solution.py:36
  11.0 0.0 collective-permute-done.refs_1_
  11.0 1.0 %collective-permute-done.1.refs_2_ = f32[9,16,128]{2,1,0:T(8,128)S(1)} collective-permute-done((f32[9,16,128]{2,1,0:T(8,128)S(1)}, f32[9,16,128]{2,1,0:T(8,128)S(1)}, u32[]{:S(2)}, u32[]{:S(2)}) %collective-permute-start.1) | collective-permute-done | bytes 73760 | tf_op jit(solution)/shard_map/ppermute | solution.py:419
  12.1 0.2 collective-permute-done.2.refs_3_
  12.4 0.1 collective-permute-start.4
  12.4 1.9 %collective-permute-start.3 = (f32[35,16,128]{2,1,0:T(8,128)S(1)}, f32[35,16,128]{2,1,0:T(8,128)S(1)}, u32[]{:S(2)}, u32[]{:S(2)}) collective-permute-start(f32[35,16,128]{2,1,0:T(8,128)S(1)} %get-tuple-element.37), channel_id=1, source_target_pairs={{0,4},{1,2},{2,1},{3,7},{4,0},{5,6},{6,5},{7,3},{8,12},{9,10},{10,... | collective-permute-start | bytes 860168 | tf_op jit(solution)/shard_map/ppermute | solution.py:434
  14.3 0.0 collective-permute-done.4.refs_4_
  14.3 1.5 %shard_map.40 = (f32[10,3,16,128]{3,2,1,0:T(8,128)S(1)}, f32[4,10,3,16,128]{4,3,2,1,0:T(8,128)S(1)}, f32[4,10,3,32,128]{4,3,2,1,0:T(8,128)S(1)}, f32[4,10,3,32,1...) custom-call(f32[9,16,128]{2,1,0:T(8,128)S(1)} %get-tuple-element.32., ...), custom_call_target="tpu_custom_call", output_to_operand_aliasing={{0}: (6, {}), {1}: (7, {}), {2}: (8, {}), {3}: (9, {}), {4}... | custom-call | tf_op jit(solution)/shard_map/pallas_call | solution.py:36
  15.8 3.3 %collective-permute-done.3.refs_0_ = f32[35,16,128]{2,1,0:T(8,128)S(1)} collective-permute-done((f32[35,16,128]{2,1,0:T(8,128)S(1)}, f32[35,16,128]{2,1,0:T(8,128)S(1)}, u32[]{:S(2)}, u32[]{:S(2)}) %collective-permute-start.3) | collective-permute-done | bytes 286752 | tf_op jit(solution)/shard_map/ppermute | solution.py:434
  19.1 1.4 %shard_map.41 = (f32[10,3,16,128]{3,2,1,0:T(8,128)S(1)}, f32[4,10,3,16,128]{4,3,2,1,0:T(8,128)S(1)}, f32[4,10,3,32,128]{4,3,2,1,0:T(8,128)S(1)}, f32[4,10,3,32,1...) custom-call(f32[35,16,128]{2,1,0:T(8,128)S(1)} %collective-permute-d, ...), custom_call_target="tpu_custom_call", output_to_operand_aliasing={{0}: (2, {}), {1}: (3, {}), {2}: (4, {}), {3}: (5, {}), {4}... | custom-call | tf_op jit(solution)/shard_map/pallas_call | solution.py:36
  20.5 1.9 %collective-permute-start.5 = (f32[8,16,128]{2,1,0:T(8,128)S(1)}, f32[8,16,128]{2,1,0:T(8,128)S(1)}, u32[]{:S(2)}, u32[]{:S(2)}) collective-permute-start(f32[8,16,128]{2,1,0:T(8,128)S(1)} %get-tuple-element.56), channel_id=1, source_target_pairs={{0,4},{4,8},{8,12},{12,0},{1,5},{5,9},{9,13},{13,1},{2,6},{6,10},{... | collective-permute-start | bytes 196616 | tf_op jit(solution)/shard_map/ppermute | solution.py:419
  22.4 1.9 %collective-permute-start.6 = (f32[8,16,128]{2,1,0:T(8,128)S(1)}, f32[8,16,128]{2,1,0:T(8,128)S(1)}, u32[]{:S(2)}, u32[]{:S(2)}) collective-permute-start(f32[8,16,128]{2,1,0:T(8,128)S(1)} %get-tuple-element.57), channel_id=1, source_target_pairs={{0,8},{4,12},{8,0},{12,4},{1,9},{5,13},{9,1},{13,5},{2,10},{6,14},... | collective-permute-start | bytes 196616 | tf_op jit(solution)/shard_map/ppermute | solution.py:419
  24.3 0.9 %collective-permute-start.7 = (f32[8,16,128]{2,1,0:T(8,128)S(1)}, f32[8,16,128]{2,1,0:T(8,128)S(1)}, u32[]{:S(2)}, u32[]{:S(2)}) collective-permute-start(f32[8,16,128]{2,1,0:T(8,128)S(1)} %get-tuple-element.58), channel_id=1, source_target_pairs={{0,12},{4,0},{8,4},{12,8},{1,13},{5,1},{9,5},{13,9},{2,14},{6,2},{... | collective-permute-start | bytes 196616 | tf_op jit(solution)/shard_map/ppermute | solution.py:419
  25.2 2.1 %collective-permute-done.5.refs_1_ = f32[8,16,128]{2,1,0:T(8,128)S(1)} collective-permute-done((f32[8,16,128]{2,1,0:T(8,128)S(1)}, f32[8,16,128]{2,1,0:T(8,128)S(1)}, u32[]{:S(2)}, u32[]{:S(2)}) %collective-permute-start.5) | collective-permute-done | bytes 65568 | tf_op jit(solution)/shard_map/ppermute | solution.py:419
  27.3 2.1 %collective-permute-done.6.refs_2_ = f32[8,16,128]{2,1,0:T(8,128)S(1)} collective-permute-done((f32[8,16,128]{2,1,0:T(8,128)S(1)}, f32[8,16,128]{2,1,0:T(8,128)S(1)}, u32[]{:S(2)}, u32[]{:S(2)}) %collective-permute-start.6) | collective-permute-done | bytes 65568 | tf_op jit(solution)/shard_map/ppermute | solution.py:419
  29.4 0.3 collective-permute-done.7.refs_3_
  29.7 0.9 %shard_map.42 = f32[16,4,1024]{2,1,0:T(4,128)} custom-call(f32[8,16,128]{2,1,0:T(8,128)S(1)} %get-tuple-element.55.refs_0_, f32[8,16,128]{2,1,0:T(8,128)S(1)} %collective-permute-done.5.refs_1_, f32[8,16,128]{2,1,0:T(8,128)S(1)} %collective-permute-done.6.refs_2_, f32[8,16,128]{2,1,0:T(8,128)S(1)} %collective-permute-done.7.refs_3_), custom_call_target="tpu_custom_call" | custom-call | tf_op jit(solution)/shard_map/pallas_call | solution.py:36
  (1 shorter events, 0.0 us)
Async XLA Ops:
  1.4 9.6 %collective-permute-start = (f32[9,16,128]{2,1,0:T(8,128)S(1)}, f32[9,16,128]{2,1,0:T(8,128)S(1)}, u32[]{:S(2)}, u32[]{:S(2)}) collective-permute-start(f32[9,16,128]{2,1,0:T(8,128)S(1)} %get-tuple-element.33), channel_id=1, source_target_pairs={{0,4},{4,8},{8,12},{12,0},{1,5},{5,9},{9,13},{13,1},{2,6},{6,10},{... | collective-permute-start | bytes 221192 | tf_op jit(solution)/shard_map/ppermute | solution.py:419
  4.5 7.5 %collective-permute-start.1 = (f32[9,16,128]{2,1,0:T(8,128)S(1)}, f32[9,16,128]{2,1,0:T(8,128)S(1)}, u32[]{:S(2)}, u32[]{:S(2)}) collective-permute-start(f32[9,16,128]{2,1,0:T(8,128)S(1)} %get-tuple-element.34), channel_id=1, source_target_pairs={{0,8},{4,12},{8,0},{12,4},{1,9},{5,13},{9,1},{13,5},{2,10},{6,14},... | collective-permute-start | bytes 221192 | tf_op jit(solution)/shard_map/ppermute | solution.py:419
  7.1 5.2 %collective-permute-start.2 = (f32[9,16,128]{2,1,0:T(8,128)S(1)}, f32[9,16,128]{2,1,0:T(8,128)S(1)}, u32[]{:S(2)}, u32[]{:S(2)}) collective-permute-start(f32[9,16,128]{2,1,0:T(8,128)S(1)} %get-tuple-element.35), channel_id=1, source_target_pairs={{0,12},{4,0},{8,4},{12,8},{1,13},{5,1},{9,5},{13,9},{2,14},{6,2},{... | collective-permute-start | bytes 221192 | tf_op jit(solution)/shard_map/ppermute | solution.py:419
  8.5 0.7 %copy-start = (f32[3]{0:T(128)S(1)}, f32[3]{0:T(128)}, u32[]{:S(2)}) copy-start(f32[3]{0:T(128)} %velocity.1) | copy-start | bytes 40
  12.4 2.0 %collective-permute-start.4 = (f32[35,16,128]{2,1,0:T(8,128)S(1)}, f32[35,16,128]{2,1,0:T(8,128)S(1)}, u32[]{:S(2)}, u32[]{:S(2)}) collective-permute-start(f32[35,16,128]{2,1,0:T(8,128)S(1)} %get-tuple-element.39), channel_id=1, source_target_pairs={{0,1},{1,0},{2,3},{3,2},{4,5},{5,4},{6,7},{7,6},{8,9},{9,8},{10,11... | collective-permute-start | bytes 860168 | tf_op jit(solution)/shard_map/ppermute | solution.py:434
  12.4 6.7 %collective-permute-start.3 = (f32[35,16,128]{2,1,0:T(8,128)S(1)}, f32[35,16,128]{2,1,0:T(8,128)S(1)}, u32[]{:S(2)}, u32[]{:S(2)}) collective-permute-start(f32[35,16,128]{2,1,0:T(8,128)S(1)} %get-tuple-element.37), channel_id=1, source_target_pairs={{0,4},{1,2},{2,1},{3,7},{4,0},{5,6},{6,5},{7,3},{8,12},{9,10},{10,... | collective-permute-start | bytes 860168 | tf_op jit(solution)/shard_map/ppermute | solution.py:434
  20.5 6.8 %collective-permute-start.5 = (f32[8,16,128]{2,1,0:T(8,128)S(1)}, f32[8,16,128]{2,1,0:T(8,128)S(1)}, u32[]{:S(2)}, u32[]{:S(2)}) collective-permute-start(f32[8,16,128]{2,1,0:T(8,128)S(1)} %get-tuple-element.56), channel_id=1, source_target_pairs={{0,4},{4,8},{8,12},{12,0},{1,5},{5,9},{9,13},{13,1},{2,6},{6,10},{... | collective-permute-start | bytes 196616 | tf_op jit(solution)/shard_map/ppermute | solution.py:419
  22.4 7.0 %collective-permute-start.6 = (f32[8,16,128]{2,1,0:T(8,128)S(1)}, f32[8,16,128]{2,1,0:T(8,128)S(1)}, u32[]{:S(2)}, u32[]{:S(2)}) collective-permute-start(f32[8,16,128]{2,1,0:T(8,128)S(1)} %get-tuple-element.57), channel_id=1, source_target_pairs={{0,8},{4,12},{8,0},{12,4},{1,9},{5,13},{9,1},{13,5},{2,10},{6,14},... | collective-permute-start | bytes 196616 | tf_op jit(solution)/shard_map/ppermute | solution.py:419
  24.3 5.4 %collective-permute-start.7 = (f32[8,16,128]{2,1,0:T(8,128)S(1)}, f32[8,16,128]{2,1,0:T(8,128)S(1)}, u32[]{:S(2)}, u32[]{:S(2)}) collective-permute-start(f32[8,16,128]{2,1,0:T(8,128)S(1)} %get-tuple-element.58), channel_id=1, source_target_pairs={{0,12},{4,0},{8,4},{12,8},{1,13},{5,1},{9,5},{13,9},{2,14},{6,2},{... | collective-permute-start | bytes 196616 | tf_op jit(solution)/shard_map/ppermute | solution.py:419

commit v5 on v4

--- a/solution.py
+++ b/solution.py
@@ -7,6 +7,7 @@
 from jax.experimental import pallas as pl
 from jax.experimental.pallas import tpu as pltpu
 from jax.sharding import PartitionSpec as P
+
 
 circ_alpha = 0.1
 relax_weights = (
@@ -264,8 +265,8 @@
     made = 2 + levels
     if second_half:
         far, drift = refs[:2]
-        kappa, inverse, *iterates = refs[2 + made + 1 + steps :][:made]
-        source, *outs = refs[2 + made + 1 + steps + made :]
+        kappa, inverse, *iterates = refs[2 + made + 1 :][:made]
+        source, *outs = refs[2 + made + 1 + made :]
         blocks, near = [None] * steps, None
     else:
         blocks, (near, drift) = refs[:steps], refs[steps : steps + 2]
@@ -371,6 +372,8 @@
 
         lax.fori_loop(*rows_of(level), step, 0)
 
+    last_rows = rows_of(levels)
+
     def last_step(row, carry):
         for tile, results in sweep(row, iterates[levels - 1], relax_weights[levels], True):
             for ahead in range(steps):
@@ -382,27 +385,40 @@
                     if is_complex:
                         terms.append((-factor * sine(k * ahead, steps), results[place]))
                         place += 1
-                outs[ahead][(row - reach) * tiles + tile] = combine(terms)
+                outs[ahead][(row - last_rows[0]) * tiles + tile] = combine(terms)
         return carry
 
-    lax.fori_loop(*rows_of(levels), last_step, 0)
+    lax.fori_loop(*last_rows, last_step, 0)
 
 
 def unpack_kernel(tm, space, log_alpha, steps, *refs):
-    blocks, (out, held, semaphores) = refs[:steps], refs[steps:]
+    early, late, (out, held, semaphores) = refs[:steps], refs[steps : 2 * steps], refs[2 * steps :]
     me, up = lax.axis_index(tm), upwards(space)
     depth, rows, columns = out.shape
     width = columns // steps
     tiles = width // lanes
     scale = jnp.exp(jnp.full((depth, lanes), me.astype(jnp.float32) * -log_alpha, jnp.float32))
+    first = rows - reach
+    rising = up == 1
+
+    def at_row(behind, row, tile):
+        if row < first:
+            return early[behind][row * tiles + tile]
+        return late[behind][(row - first) * tiles + tile]
+
     copies = []
     for behind in range(steps):
         owner = lax.rem(me - behind + steps, steps)
         for y in range(rows):
-            row = row_of(y, rows, up)
             for tile in range(tiles):
+                if rows - reach <= min(y, rows - 1 - y):
+                    value = late[behind][(row_of(y, rows, up) - first) * tiles + tile]
+                else:
+                    value = jnp.where(
+                        rising, at_row(behind, y, tile), at_row(behind, rows - 1 - y, tile)
+                    )
                 place = pl.multiple_of((owner * tiles + tile) * lanes, lanes)
-                held[:, y, pl.ds(place, lanes)] = blocks[behind][row * tiles + tile] * scale
+                held[:, y, pl.ds(place, lanes)] = value * scale
         part = pl.ds(pl.multiple_of(owner * width, lanes), width)
         copies.append(
             pltpu.make_async_copy(
@@ -415,10 +431,10 @@
 
 
 def exchange(blocks, steps):
-    moved = [
-        lax.ppermute(blocks[d], "tm", [(i, (i + d) % steps) for i in range(steps)])
-        for d in range(1, steps)
-    ]
+    moved = []
+    for d in range(1, steps):
+        pairs = [(i, (i + d) % steps) for i in range(steps)]
+        moved.append(lax.ppermute(blocks[d], "tm", pairs))
     return [blocks[0]] + moved
 
 
@@ -454,31 +470,34 @@
     )
     near, far = halos([*blocks, own], rows, tiles)
     far, near = swap(far, 1), swap(near, 0)
-    state = [*made, *iterates, made[1]] + [(rows * tiles, depth, lanes)] * steps
+    state = [*made, *iterates, made[1]]
+    early = rows - reach
     solve = functools.partial(solve_kernel, "tm", "space", rows, tiles, steps)
     kept = [kappa, inverse, *margins]
     held = call(
         functools.partial(solve, False),
-        state,
+        state + [(early * tiles, depth, lanes)] * steps,
         *blocks,
         near,
         drift,
         *kept,
         aliases={steps + 2 + i: i for i in range(len(kept))},
     )
+    first_rows = exchange(held[len(state) :], steps)
     held = call(
         functools.partial(solve, True),
-        state,
+        state + [(reach * tiles, depth, lanes)] * steps,
         far,
         drift,
-        *held,
+        *held[: len(state)],
         aliases={2 + i: i for i in range(len(state))},
     )
-    returned = exchange(held[len(kept) + 1 :], steps)
+    last_rows = exchange(held[len(state) :], steps)
     (result,) = call(
         functools.partial(unpack_kernel, "tm", "space", log_alpha, steps),
         [(depth, rows, columns)],
-        *returned,
+        *first_rows,
+        *last_rows,
         kept=False,
         scratch=[
             pltpu.VMEM((depth, rows, columns), jnp.float32),
@@ -598,7 +617,7 @@
 
 def local(rhs, diffusivity, velocity):
     steps = lax.axis_size("tm")
-    local_steps, depth, rows, columns = rhs.shape
+    local_steps, _, rows, columns = rhs.shape
     if local_steps == 1 and rows >= reach and lanes % rows == 0 and columns % (steps * lanes) == 0:
         return fast_local(rhs, diffusivity, velocity)
     return general_local(rhs, diffusivity, velocity)

time: 30.8 us -> 35.7 us (1.16)
  waiting for transfers between devices: 9.06 us -> 11.8 us
  starting transfers between devices: 13.7 us -> 15.8 us
    ppermute x6 -> x9, waiting for transfers between devices: 5.74 us -> 8.49 us  [exchange(): moved.append(lax.ppermute(blocks[d], 'tm', pairs))]
    ppermute x6 -> x9, starting transfers between devices: 11.7 us -> 13.9 us  [exchange(): moved.append(lax.ppermute(blocks[d], 'tm', pairs))]
  transfers between devices with their start and end apart: 8 -> 11, of which waited for: 6 -> 6; matrix products, arithmetic and copies ran while one was open for 0% -> 0% of each run, Pallas kernels for 11% -> 10%
where the time goes in v5:
time: 35.7 us; the launch traced here: 35.5 us
  starting transfers between devices  15.8 us (44%)
  waiting for transfers between devices  11.8 us (33%)
  Pallas kernels  7.17 us (20%)
  local copies, waits for them, and re-layouts  0.65 us (2%)
    ppermute x9, starting transfers between devices, exchange(): moved.append(lax.ppermute(blocks[d], 'tm', pairs))  13.9 us
    ppermute x9, waiting for transfers between devices, exchange(): moved.append(lax.ppermute(blocks[d], 'tm', pairs))  8.49 us
    pallas_call x6, Pallas kernels, call(): pl.pallas_call(kernel, out_shape=[make(o, jnp.float32) for o in outs], in...  7.17 us
    ppermute x2, waiting for transfers between devices, swap(): return lax.ppermute(value, ('tm', 'space'), pairs)  3.32 us
    ppermute x2, starting transfers between devices, swap(): return lax.ppermute(value, ('tm', 'space'), pairs)  1.94 us
  transfers between devices with their start and end apart: 11, of which 6 were waited for; matrix products, arithmetic and copies ran while one was open for 0% of the time, Pallas kernels for 10%

profile of v5, /device:TPU:0, one launch (start us, length us, event | category | flops | bytes accessed | tf_op | source)
XLA Modules:
  0.0 35.5 jit_solution(16954836043208293989)
XLA Ops:
  0.0 1.4 %shard_map.37 = (f32[9,16,128]{2,1,0:T(8,128)S(1)}, f32[9,16,128]{2,1,0:T(8,128)S(1)}, f32[9,16,128]{2,1,0:T(8,128)S(1)}, f32[9,16,128]{2,1,0:T(8,128)S(1)}) custom-call(f32[16,4,1024]{2,1,0:T(4,128)} %bitcast.2), custom_call_target="tpu_custom_call" | custom-call | tf_op jit(solution)/shard_map/pallas_call | solution.py:37
  1.4 3.1 %collective-permute-start = (f32[9,16,128]{2,1,0:T(8,128)S(1)}, f32[9,16,128]{2,1,0:T(8,128)S(1)}, u32[]{:S(2)}, u32[]{:S(2)}) collective-permute-start(f32[9,16,128]{2,1,0:T(8,128)S(1)} %get-tuple-element.33), channel_id=1, source_target_pairs={{0,4},{4,8},{8,12},{12,0},{1,5},{5,9},{9,13},{13,1},{2,6},{6,10},{... | collective-permute-start | bytes 221192 | tf_op jit(solution)/shard_map/ppermute | solution.py:437
  4.5 2.6 %collective-permute-start.1 = (f32[9,16,128]{2,1,0:T(8,128)S(1)}, f32[9,16,128]{2,1,0:T(8,128)S(1)}, u32[]{:S(2)}, u32[]{:S(2)}) collective-permute-start(f32[9,16,128]{2,1,0:T(8,128)S(1)} %get-tuple-element.34), channel_id=1, source_target_pairs={{0,8},{4,12},{8,0},{12,4},{1,9},{5,13},{9,1},{13,5},{2,10},{6,14},... | collective-permute-start | bytes 221192 | tf_op jit(solution)/shard_map/ppermute | solution.py:437
  7.1 1.3 %collective-permute-start.2 = (f32[9,16,128]{2,1,0:T(8,128)S(1)}, f32[9,16,128]{2,1,0:T(8,128)S(1)}, u32[]{:S(2)}, u32[]{:S(2)}) collective-permute-start(f32[9,16,128]{2,1,0:T(8,128)S(1)} %get-tuple-element.35), channel_id=1, source_target_pairs={{0,12},{4,0},{8,4},{12,8},{1,13},{5,1},{9,5},{13,9},{2,14},{6,2},{... | collective-permute-start | bytes 221192 | tf_op jit(solution)/shard_map/ppermute | solution.py:437
  8.5 0.0 copy-start
  8.5 0.7 %copy-done = f32[3]{0:T(128)S(1)} copy-done((f32[3]{0:T(128)S(1)}, f32[3]{0:T(128)}, u32[]{:S(2)}) %copy-start) | copy-done | bytes 36
  9.1 1.9 %shard_map.38 = (f32[9,16,128]{2,1,0:T(8,128)S(1)}, f32[10,3,16,128]{3,2,1,0:T(8,128)S(1)}, f32[4,10,3,16,128]{4,3,2,1,0:T(8,128)S(1)}, f32[3,16,128]{2,1,0:T(8,...) custom-call(f32[16,4,1024]{2,1,0:T(4,128)} %diffusivity.1, ...), custom_call_target="tpu_custom_call" | custom-call | tf_op jit(solution)/shard_map/pallas_call | solution.py:37
  11.0 0.0 collective-permute-done.refs_1_
  11.0 1.0 %collective-permute-done.1.refs_2_ = f32[9,16,128]{2,1,0:T(8,128)S(1)} collective-permute-done((f32[9,16,128]{2,1,0:T(8,128)S(1)}, f32[9,16,128]{2,1,0:T(8,128)S(1)}, u32[]{:S(2)}, u32[]{:S(2)}) %collective-permute-start.1) | collective-permute-done | bytes 73760 | tf_op jit(solution)/shard_map/ppermute | solution.py:437
  12.1 0.2 collective-permute-done.2.refs_3_
  12.4 0.1 collective-permute-start.3
  12.4 1.9 %collective-permute-start.7 = (f32[35,16,128]{2,1,0:T(8,128)S(1)}, f32[35,16,128]{2,1,0:T(8,128)S(1)}, u32[]{:S(2)}, u32[]{:S(2)}) collective-permute-start(f32[35,16,128]{2,1,0:T(8,128)S(1)} %get-tuple-element.48), channel_id=1, source_target_pairs={{0,4},{1,2},{2,1},{3,7},{4,0},{5,6},{6,5},{7,3},{8,12},{9,10},{10,... | collective-permute-start | bytes 860168 | tf_op jit(solution)/shard_map/ppermute | solution.py:450
  14.3 0.0 collective-permute-done.3.refs_4_
  14.3 1.5 %shard_map.40 = (f32[10,3,16,128]{3,2,1,0:T(8,128)S(1)}, f32[4,10,3,16,128]{4,3,2,1,0:T(8,128)S(1)}, f32[4,10,3,32,128]{4,3,2,1,0:T(8,128)S(1)}, f32[4,10,3,32,1...) custom-call(f32[9,16,128]{2,1,0:T(8,128)S(1)} %get-tuple-element.32., ...), custom_call_target="tpu_custom_call", output_to_operand_aliasing={{0}: (6, {}), {1}: (7, {}), {2}: (8, {}), {3}: (9, {}), {4}... | custom-call | tf_op jit(solution)/shard_map/pallas_call | solution.py:37
  15.8 3.3 %collective-permute-done.7.refs_0_ = f32[35,16,128]{2,1,0:T(8,128)S(1)} collective-permute-done((f32[35,16,128]{2,1,0:T(8,128)S(1)}, f32[35,16,128]{2,1,0:T(8,128)S(1)}, u32[]{:S(2)}, u32[]{:S(2)}) %collective-permute-start.7) | collective-permute-done | bytes 286752 | tf_op jit(solution)/shard_map/ppermute | solution.py:450
  19.1 1.4 %shard_map.41 = (f32[10,3,16,128]{3,2,1,0:T(8,128)S(1)}, f32[4,10,3,16,128]{4,3,2,1,0:T(8,128)S(1)}, f32[4,10,3,32,128]{4,3,2,1,0:T(8,128)S(1)}, f32[4,10,3,32,1...) custom-call(f32[35,16,128]{2,1,0:T(8,128)S(1)} %collective-permute-d, ...), custom_call_target="tpu_custom_call", output_to_operand_aliasing={{0}: (2, {}), {1}: (3, {}), {2}: (4, {}), {3}: (5, {}), {4}... | custom-call | tf_op jit(solution)/shard_map/pallas_call | solution.py:37
  20.5 1.9 %collective-permute-start.8 = (f32[6,16,128]{2,1,0:T(8,128)S(1)}, f32[6,16,128]{2,1,0:T(8,128)S(1)}, u32[]{:S(2)}, u32[]{:S(2)}) collective-permute-start(f32[6,16,128]{2,1,0:T(8,128)S(1)} %get-tuple-element.56), channel_id=1, source_target_pairs={{0,4},{4,8},{8,12},{12,0},{1,5},{5,9},{9,13},{13,1},{2,6},{6,10},{... | collective-permute-start | bytes 147464 | tf_op jit(solution)/shard_map/ppermute | solution.py:437
  22.4 1.9 %collective-permute-start.9 = (f32[6,16,128]{2,1,0:T(8,128)S(1)}, f32[6,16,128]{2,1,0:T(8,128)S(1)}, u32[]{:S(2)}, u32[]{:S(2)}) collective-permute-start(f32[6,16,128]{2,1,0:T(8,128)S(1)} %get-tuple-element.57), channel_id=1, source_target_pairs={{0,8},{4,12},{8,0},{12,4},{1,9},{5,13},{9,1},{13,5},{2,10},{6,14},... | collective-permute-start | bytes 147464 | tf_op jit(solution)/shard_map/ppermute | solution.py:437
  24.3 0.9 %collective-permute-start.10 = (f32[6,16,128]{2,1,0:T(8,128)S(1)}, f32[6,16,128]{2,1,0:T(8,128)S(1)}, u32[]{:S(2)}, u32[]{:S(2)}) collective-permute-start(f32[6,16,128]{2,1,0:T(8,128)S(1)} %get-tuple-element.58), channel_id=1, source_target_pairs={{0,12},{4,0},{8,4},{12,8},{1,13},{5,1},{9,5},{13,9},{2,14},{6,2},{... | collective-permute-start | bytes 147464 | tf_op jit(solution)/shard_map/ppermute | solution.py:437
  25.2 1.1 %collective-permute-start.4 = (f32[2,16,128]{2,1,0:T(8,128)S(1)}, f32[2,16,128]{2,1,0:T(8,128)S(1)}, u32[]{:S(2)}, u32[]{:S(2)}) collective-permute-start(f32[2,16,128]{2,1,0:T(8,128)S(1)} %get-tuple-element.45), channel_id=1, source_target_pairs={{0,4},{4,8},{8,12},{12,0},{1,5},{5,9},{9,13},{13,1},{2,6},{6,10},{... | collective-permute-start | bytes 49160 | tf_op jit(solution)/shard_map/ppermute | solution.py:437
  26.4 1.0 %collective-permute-start.5 = (f32[2,16,128]{2,1,0:T(8,128)S(1)}, f32[2,16,128]{2,1,0:T(8,128)S(1)}, u32[]{:S(2)}, u32[]{:S(2)}) collective-permute-start(f32[2,16,128]{2,1,0:T(8,128)S(1)} %get-tuple-element.46), channel_id=1, source_target_pairs={{0,8},{4,12},{8,0},{12,4},{1,9},{5,13},{9,1},{13,5},{2,10},{6,14},... | collective-permute-start | bytes 49160 | tf_op jit(solution)/shard_map/ppermute | solution.py:437
  27.3 3.5 %collective-permute-done.4.refs_1_ = f32[2,16,128]{2,1,0:T(8,128)S(1)} collective-permute-done((f32[2,16,128]{2,1,0:T(8,128)S(1)}, f32[2,16,128]{2,1,0:T(8,128)S(1)}, u32[]{:S(2)}, u32[]{:S(2)}) %collective-permute-start.4) | collective-permute-done | bytes 16416 | tf_op jit(solution)/shard_map/ppermute | solution.py:437
  30.8 0.0 collective-permute-start.6
  30.8 0.4 collective-permute-done.5.refs_2_
  31.2 3.4 %collective-permute-done.6.refs_3_ = f32[2,16,128]{2,1,0:T(8,128)S(1)} collective-permute-done((f32[2,16,128]{2,1,0:T(8,128)S(1)}, f32[2,16,128]{2,1,0:T(8,128)S(1)}, u32[]{:S(2)}, u32[]{:S(2)}) %collective-permute-start.6) | collective-permute-done | bytes 16416 | tf_op jit(solution)/shard_map/ppermute | solution.py:437
  34.5 0.0 collective-permute-done.8.refs_5_
  34.5 0.0 collective-permute-done.9.refs_6_
  34.6 0.0 collective-permute-done.10.refs_7_
  34.6 0.9 %shard_map.42 = f32[16,4,1024]{2,1,0:T(4,128)} custom-call(f32[2,16,128]{2,1,0:T(8,128)S(1)} %get-tuple-element.44.refs_0_, f32[2,16,128]{2,1,0:T(8,128)S(1)} %collective-permute-done.4.refs_1_, f32[2,16,128]{2,1,0:T(8,128)S(1)} %collective-permute-done.5.refs_2_, f32[2,16,128]{2,1,0:T(8,128)S(1)} %collective-permute-done.6.refs_3_, ...), custom_call_target="tpu_custom_call" | custom-call | tf_op jit(solution)/shard_map/pallas_call | solution.py:37
  (1 shorter events, 0.0 us)
Async XLA Ops:
  1.4 9.6 %collective-permute-start = (f32[9,16,128]{2,1,0:T(8,128)S(1)}, f32[9,16,128]{2,1,0:T(8,128)S(1)}, u32[]{:S(2)}, u32[]{:S(2)}) collective-permute-start(f32[9,16,128]{2,1,0:T(8,128)S(1)} %get-tuple-element.33), channel_id=1, source_target_pairs={{0,4},{4,8},{8,12},{12,0},{1,5},{5,9},{9,13},{13,1},{2,6},{6,10},{... | collective-permute-start | bytes 221192 | tf_op jit(solution)/shard_map/ppermute | solution.py:437
  4.5 7.5 %collective-permute-start.1 = (f32[9,16,128]{2,1,0:T(8,128)S(1)}, f32[9,16,128]{2,1,0:T(8,128)S(1)}, u32[]{:S(2)}, u32[]{:S(2)}) collective-permute-start(f32[9,16,128]{2,1,0:T(8,128)S(1)} %get-tuple-element.34), channel_id=1, source_target_pairs={{0,8},{4,12},{8,0},{12,4},{1,9},{5,13},{9,1},{13,5},{2,10},{6,14},... | collective-permute-start | bytes 221192 | tf_op jit(solution)/shard_map/ppermute | solution.py:437
  7.1 5.2 %collective-permute-start.2 = (f32[9,16,128]{2,1,0:T(8,128)S(1)}, f32[9,16,128]{2,1,0:T(8,128)S(1)}, u32[]{:S(2)}, u32[]{:S(2)}) collective-permute-start(f32[9,16,128]{2,1,0:T(8,128)S(1)} %get-tuple-element.35), channel_id=1, source_target_pairs={{0,12},{4,0},{8,4},{12,8},{1,13},{5,1},{9,5},{13,9},{2,14},{6,2},{... | collective-permute-start | bytes 221192 | tf_op jit(solution)/shard_map/ppermute | solution.py:437
  8.5 0.7 %copy-start = (f32[3]{0:T(128)S(1)}, f32[3]{0:T(128)}, u32[]{:S(2)}) copy-start(f32[3]{0:T(128)} %velocity.1) | copy-start | bytes 40
  12.4 2.0 %collective-permute-start.3 = (f32[35,16,128]{2,1,0:T(8,128)S(1)}, f32[35,16,128]{2,1,0:T(8,128)S(1)}, u32[]{:S(2)}, u32[]{:S(2)}) collective-permute-start(f32[35,16,128]{2,1,0:T(8,128)S(1)} %get-tuple-element.37), channel_id=1, source_target_pairs={{0,1},{1,0},{2,3},{3,2},{4,5},{5,4},{6,7},{7,6},{8,9},{9,8},{10,11... | collective-permute-start | bytes 860168 | tf_op jit(solution)/shard_map/ppermute | solution.py:450
  12.4 6.7 %collective-permute-start.7 = (f32[35,16,128]{2,1,0:T(8,128)S(1)}, f32[35,16,128]{2,1,0:T(8,128)S(1)}, u32[]{:S(2)}, u32[]{:S(2)}) collective-permute-start(f32[35,16,128]{2,1,0:T(8,128)S(1)} %get-tuple-element.48), channel_id=1, source_target_pairs={{0,4},{1,2},{2,1},{3,7},{4,0},{5,6},{6,5},{7,3},{8,12},{9,10},{10,... | collective-permute-start | bytes 860168 | tf_op jit(solution)/shard_map/ppermute | solution.py:450
  20.5 14.0 %collective-permute-start.8 = (f32[6,16,128]{2,1,0:T(8,128)S(1)}, f32[6,16,128]{2,1,0:T(8,128)S(1)}, u32[]{:S(2)}, u32[]{:S(2)}) collective-permute-start(f32[6,16,128]{2,1,0:T(8,128)S(1)} %get-tuple-element.56), channel_id=1, source_target_pairs={{0,4},{4,8},{8,12},{12,0},{1,5},{5,9},{9,13},{13,1},{2,6},{6,10},{... | collective-permute-start | bytes 147464 | tf_op jit(solution)/shard_map/ppermute | solution.py:437
  22.4 12.2 %collective-permute-start.9 = (f32[6,16,128]{2,1,0:T(8,128)S(1)}, f32[6,16,128]{2,1,0:T(8,128)S(1)}, u32[]{:S(2)}, u32[]{:S(2)}) collective-permute-start(f32[6,16,128]{2,1,0:T(8,128)S(1)} %get-tuple-element.57), channel_id=1, source_target_pairs={{0,8},{4,12},{8,0},{12,4},{1,9},{5,13},{9,1},{13,5},{2,10},{6,14},... | collective-permute-start | bytes 147464 | tf_op jit(solution)/shard_map/ppermute | solution.py:437
  24.3 10.2 %collective-permute-start.10 = (f32[6,16,128]{2,1,0:T(8,128)S(1)}, f32[6,16,128]{2,1,0:T(8,128)S(1)}, u32[]{:S(2)}, u32[]{:S(2)}) collective-permute-start(f32[6,16,128]{2,1,0:T(8,128)S(1)} %get-tuple-element.58), channel_id=1, source_target_pairs={{0,12},{4,0},{8,4},{12,8},{1,13},{5,1},{9,5},{13,9},{2,14},{6,2},{... | collective-permute-start | bytes 147464 | tf_op jit(solution)/shard_map/ppermute | solution.py:437
  25.2 5.6 %collective-permute-start.4 = (f32[2,16,128]{2,1,0:T(8,128)S(1)}, f32[2,16,128]{2,1,0:T(8,128)S(1)}, u32[]{:S(2)}, u32[]{:S(2)}) collective-permute-start(f32[2,16,128]{2,1,0:T(8,128)S(1)} %get-tuple-element.45), channel_id=1, source_target_pairs={{0,4},{4,8},{8,12},{12,0},{1,5},{5,9},{9,13},{13,1},{2,6},{6,10},{... | collective-permute-start | bytes 49160 | tf_op jit(solution)/shard_map/ppermute | solution.py:437
  26.4 4.8 %collective-permute-start.5 = (f32[2,16,128]{2,1,0:T(8,128)S(1)}, f32[2,16,128]{2,1,0:T(8,128)S(1)}, u32[]{:S(2)}, u32[]{:S(2)}) collective-permute-start(f32[2,16,128]{2,1,0:T(8,128)S(1)} %get-tuple-element.46), channel_id=1, source_target_pairs={{0,8},{4,12},{8,0},{12,4},{1,9},{5,13},{9,1},{13,5},{2,10},{6,14},... | collective-permute-start | bytes 49160 | tf_op jit(solution)/shard_map/ppermute | solution.py:437
  30.8 3.7 %collective-permute-start.6 = (f32[2,16,128]{2,1,0:T(8,128)S(1)}, f32[2,16,128]{2,1,0:T(8,128)S(1)}, u32[]{:S(2)}, u32[]{:S(2)}) collective-permute-start(f32[2,16,128]{2,1,0:T(8,128)S(1)} %get-tuple-element.47), channel_id=1, source_target_pairs={{0,12},{4,0},{8,4},{12,8},{1,13},{5,1},{9,5},{13,9},{2,14},{6,2},{... | collective-permute-start | bytes 49160 | tf_op jit(solution)/shard_map/ppermute | solution.py:437

commit v6 on v5

--- a/solution.py
+++ b/solution.py
@@ -20,6 +20,8 @@
 
 reach = len(relax_weights) - 1
 lanes = 128
+sublanes = 8
+early_moves = (2, 3)
 vmem = pl.BlockSpec(memory_space=pltpu.VMEM)
 smem = pl.BlockSpec(memory_space=pltpu.SMEM)
 hbm = pl.BlockSpec(memory_space=pltpu.HBM)
@@ -60,8 +62,33 @@
     return up * y + (1 - up) * (rows - 1 - y)
 
 
-def pick_block(source, write, owner, owners, up):
+def heading(step, steps):
+    return 1 - 2 * (step % 2) if steps % 2 == 0 else 1
+
+
+def slot_time(step, slot, steps):
+    return (step + heading(step, steps) * slot) % steps
+
+
+def slot_owner(me, slot, steps):
+    forwards = 1 - 2 * lax.rem(me, 2) if steps % 2 == 0 else 1
+    turn = forwards * slot if steps % 2 == 0 and slot % 2 else -forwards * slot
+    return lax.rem(me + turn + steps, steps)
+
+
+def put(block, index, value):
+    sheets = value.shape[0] // sublanes
+    block[pl.ds(index * sheets, sheets)] = value.reshape(sheets, sublanes, lanes)
+
+
+def slot_width(rows, sheets):
+    return lanes // (rows * sheets)
+
+
+def pick_block(source, write, write_halo, owner, owners, up):
     depth, rows, columns = source.shape
+    sheets = depth // sublanes
+    width = slot_width(rows, sheets)
     total = columns // lanes
     tiles = total // owners
     left_tile = jnp.maximum(owner * tiles - 1, 0)
@@ -79,9 +106,11 @@
         for tile in range(tiles):
             write(row * tiles + tile, tile_at(y, owner * tiles + tile))
         halo = tile_at(y, right_tile) * keep_right + tile_at(y, left_tile) * keep_left
-        halo = pltpu.roll(halo, row * (lanes // rows), 1)
-        packed = halo if packed is None else packed + halo
-    write(rows * tiles, packed)
+        for sheet in range(sheets):
+            part = halo[sheet * sublanes : (sheet + 1) * sublanes]
+            part = pltpu.roll(part, (row * sheets + sheet) * width, 1)
+            packed = part if packed is None else packed + part
+    write_halo(packed)
 
 
 def fetch(source, target, semaphores):
@@ -102,16 +131,19 @@
 def pack_kernel(tm, space, log_alpha, steps, rhs, *refs):
     outs, (held, semaphores) = refs[:steps], refs[steps:]
     me, up = lax.axis_index(tm), upwards(space)
-    depth = rhs.shape[0]
     fetch(rhs, held, semaphores)
-    scale = jnp.exp(jnp.full((depth, lanes), me.astype(jnp.float32) * log_alpha, jnp.float32))
-    for ahead in range(steps):
+    scale = jnp.exp(jnp.full((sublanes, lanes), me.astype(jnp.float32) * log_alpha, jnp.float32))
+    tall = jnp.concatenate([scale] * (rhs.shape[0] // sublanes))
+    for ahead in reversed(range(steps)):
         out = outs[ahead]
 
         def write(index, value, out=out):
-            out[index] = value * scale
-
-        pick_block(held, write, lax.rem(me + ahead, steps), steps, up)
+            put(out, index, value * tall)
+
+        def write_halo(value, out=out):
+            out[out.shape[0] - 1] = value * scale
+
+        pick_block(held, write, write_halo, slot_owner(me, ahead, steps), steps, up)
 
 
 def staging(shape):
@@ -124,56 +156,59 @@
     tiles = columns // steps // lanes
     log_alpha = math.log(circ_alpha) / steps
     kernel = functools.partial(pack_kernel, "tm", "space", log_alpha, steps)
-    out = (rows * tiles + 1, depth, lanes)
+    out = (rows * tiles * depth // sublanes + 1, sublanes, lanes)
     return call(kernel, [out] * steps, rhs, specs={0: hbm}, scratch=staging(rhs.shape))
 
 
-def first_row(near, rows):
-    return 0 if near else rows - reach
-
-
-def halo_kernel(rows, tiles, count, *refs):
-    blocks, (near, far) = refs[:count], refs[count:]
-    piece = reach * tiles + 1
+def copy_piece(block, is_near, piece, target, first):
+    last = block.shape[0] - 1
+    start = 0 if is_near else last - (piece - 1)
+    target[pl.ds(first, piece - 1)] = block[pl.ds(start, piece - 1)]
+    target[first + piece - 1] = block[last]
+
+
+def halo_kernel(piece, *refs):
+    blocks, (near, far) = refs[:-2], refs[-2:]
     for step, block in enumerate(blocks):
-        for out, is_near in ((near, True), (far, False)):
-            start = first_row(is_near, rows) * tiles
-            for place in range(reach * tiles):
-                out[step * piece + place] = block[start + place]
-            out[step * piece + reach * tiles] = block[rows * tiles]
-
-
-def halos(blocks, rows, tiles):
-    depth = blocks[0].shape[1]
-    out = (len(blocks) * (reach * tiles + 1), depth, lanes)
-    kernel = functools.partial(halo_kernel, rows, tiles, len(blocks))
-    return call(kernel, [out, out], *blocks)
-
-
-def row_piece(own, near, far, step, row, tile, rows, tiles):
-    piece = reach * tiles + 1
+        copy_piece(block, True, piece, near, step * piece)
+        if (step + 1) * piece <= far.shape[0]:
+            copy_piece(block, False, piece, far, step * piece)
+
+
+def halos(blocks, own, piece):
+    outs = [(count * piece, sublanes, lanes) for count in (len(blocks) + 1, len(blocks))]
+    return call(functools.partial(halo_kernel, piece), outs, *blocks, own)
+
+
+def row_piece(own, near, far, step, row, tile, rows, tiles, depth):
+    sheets = depth // sublanes
+    piece = reach * tiles * sheets + 1
+    base, start, held = step * piece, 0, reach
     if row < reach:
-        source, base, there, start = near, step * piece, reach - 1 - row, 0
-        packed = base + reach * tiles
+        source, there = near, reach - 1 - row
     elif row < reach + rows:
-        source, base, there, start = own, 0, row - reach, 0
-        packed = rows * tiles
+        source, base, there, held = own, 0, row - reach, rows
     else:
-        source, base, there = far, step * piece, 2 * rows + reach - 1 - row
-        start = rows - reach
-        packed = base + reach * tiles
+        source, there, start = far, 2 * rows + reach - 1 - row, rows - reach
     if tile < tiles:
-        return source[base + (there - start) * tiles + tile]
-    value = source[packed]
-    shift = there * (lanes // rows)
-    return pltpu.roll(value, lanes - shift, 1) if shift else value
+        first = base + ((there - start) * tiles + tile) * sheets
+        return source[pl.ds(first, sheets)].reshape(depth, lanes)
+    value = source[base + held * tiles * sheets]
+    width = slot_width(rows, sheets)
+    parts = []
+    for sheet in range(sheets):
+        shift = (there * sheets + sheet) * width
+        parts.append(pltpu.roll(value, lanes - shift, 1) if shift else value)
+    return jnp.concatenate(parts)
 
 
 def frequencies(steps):
     return [(k, 2 * k % steps != 0) for k in range(steps // 2 + 1)]
 
 
-def write_coefficients(row, tile, value, mask, steps, kappa, inverse):
+def write_coefficients(tm, row, tile, value, mask, steps, kappa, inverse):
+    backwards = lax.rem(lax.axis_index(tm), 2) if steps % 2 == 0 else 0
+    turn = jnp.float32(1 - 2 * backwards)
     shift_factor = circ_alpha ** (1.0 / steps)
     kappa[row, tile] = value
     place = 0
@@ -183,7 +218,7 @@
         if is_complex:
             imag = shift_factor * math.sin(phase)
             reciprocal = 1.0 / (real * real + imag * imag)
-            pair = (real * reciprocal, imag * reciprocal)
+            pair = (real * reciprocal, (imag * turn) * reciprocal)
         else:
             pair = (1.0 / real,)
         for part in pair:
@@ -200,7 +235,7 @@
 
 
 def prepare_kernel(tm, space, rows, tiles, steps, diffusivity, velocity, *refs):
-    own, kappa, inverse, drift, *iterates = refs[:-2]
+    own, own_far, kappa, inverse, drift, *iterates = refs[:-2]
     held, semaphores = refs[-2:]
     up = upwards(space)
     depth = diffusivity.shape[0]
@@ -219,15 +254,19 @@
     fetch(diffusivity, held, semaphores)
 
     def write(index, value):
-        own[index] = value
-
-    pick_block(held, write, lax.axis_index(tm), steps, up)
+        put(own, index, value)
+
+    def write_halo(value):
+        own[own.shape[0] - 1] = value
+
+    pick_block(held, write, write_halo, lax.axis_index(tm), steps, up)
+    copy_piece(own, False, own_far.shape[0], own_far, 0)
     halo_mask = side_mask(tm, steps, depth)
     for row in range(reach, reach + rows):
         for tile in range(tiles + 1):
-            value = row_piece(own, None, None, 0, row, tile, rows, tiles)
+            value = row_piece(own, None, None, 0, row, tile, rows, tiles, depth)
             mask = halo_mask if tile == tiles else None
-            write_coefficients(row, tile, value, mask, steps, kappa, inverse)
+            write_coefficients(tm, row, tile, value, mask, steps, kappa, inverse)
 
 
 def combine(terms):
@@ -264,15 +303,17 @@
     levels = reach
     made = 2 + levels
     if second_half:
-        far, drift = refs[:2]
-        kappa, inverse, *iterates = refs[2 + made + 1 :][:made]
-        source, *outs = refs[2 + made + 1 + made :]
+        far, kappa_far, drift = refs[:3]
+        done = sum(ahead not in early_moves for ahead in range(1, steps))
+        finished, refs = refs[4 + made : 4 + made + done], refs[4 + made + done :]
+        kappa, inverse, *iterates = refs[:made]
+        source, *outs = refs[made:]
         blocks, near = [None] * steps, None
     else:
         blocks, (near, drift) = refs[:steps], refs[steps : steps + 2]
         kappa, inverse, *iterates = refs[steps + 2 + made :][:made]
         source, *outs = refs[steps + 2 + made + made :]
-        far = None
+        far, kappa_far = None, None
     depth = kappa.shape[2]
     pad = 8
     middle = pl.ds(pad, depth)
@@ -295,9 +336,10 @@
     row_mask = jnp.full((depth, lanes), inside, jnp.float32)
     for row in range(known, extended) if second_half else range(reach):
         for tile in range(wide):
-            value = row_piece(None, near, far, steps, row, tile, rows, tiles)
+            step = 0 if second_half else steps
+            value = row_piece(None, near, kappa_far, step, row, tile, rows, tiles, depth)
             mask = halo_mask if tile == tiles else row_mask
-            write_coefficients(row, tile, value, mask, steps, kappa, inverse)
+            write_coefficients(tm, row, tile, value, mask, steps, kappa, inverse)
 
     def divide(values, row, tile):
         result, place = [], 0
@@ -317,13 +359,14 @@
             if tile == tiles and not 1 <= row < extended - 1:
                 continue
             held = [
-                row_piece(blocks[b], near, far, b, row, tile, rows, tiles) for b in range(steps)
+                row_piece(blocks[b], near, far, b, row, tile, rows, tiles, depth)
+                for b in range(steps)
             ]
             values = []
             for k, is_complex in freqs:
                 values.append(combine((cosine(k * b, steps), held[b]) for b in range(steps)))
                 if is_complex:
-                    values.append(combine((sine(k * b, steps), held[b]) for b in range(steps)))
+                    values.append(combine((-sine(k * b, steps), held[b]) for b in range(steps)))
             quotients = divide(values, row, tile)
             for field in range(fields):
                 source[field, row, tile] = values[field]
@@ -373,26 +416,35 @@
         lax.fori_loop(*rows_of(level), step, 0)
 
     last_rows = rows_of(levels)
+    skipped = [0] * steps
+    if second_half:
+        whole = [ahead for ahead in range(1, steps) if ahead not in early_moves]
+        for ahead, block in zip(whole, finished, strict=True):
+            skipped[ahead] = (rows - reach) * tiles
+            outs[ahead][pl.ds(0, block.shape[0])] = block[...]
 
     def last_step(row, carry):
         for tile, results in sweep(row, iterates[levels - 1], relax_weights[levels], True):
             for ahead in range(steps):
-                terms, place = [], 0
+                terms, field = [], 0
                 for k, is_complex in freqs:
                     factor = (2.0 if is_complex else 1.0) / steps
-                    terms.append((factor * cosine(k * ahead, steps), results[place]))
-                    place += 1
+                    terms.append((factor * cosine(k * ahead, steps), results[field]))
+                    field += 1
                     if is_complex:
-                        terms.append((-factor * sine(k * ahead, steps), results[place]))
-                        place += 1
-                outs[ahead][(row - last_rows[0]) * tiles + tile] = combine(terms)
+                        terms.append((-factor * sine(k * ahead, steps), results[field]))
+                        field += 1
+                place = (row - last_rows[0]) * tiles + tile + skipped[ahead]
+                outs[ahead][place] = combine(terms)
         return carry
 
     lax.fori_loop(*last_rows, last_step, 0)
 
 
-def unpack_kernel(tm, space, log_alpha, steps, *refs):
-    early, late, (out, held, semaphores) = refs[:steps], refs[steps : 2 * steps], refs[2 * steps :]
+def unpack_kernel(tm, space, log_alpha, steps, early, *refs):
+    refs = list(refs)
+    heads = [refs.pop(0) if two else None for two in early]
+    tails, (out, held, semaphores) = refs[:steps], refs[steps:]
     me, up = lax.axis_index(tm), upwards(space)
     depth, rows, columns = out.shape
     width = columns // steps
@@ -402,21 +454,20 @@
     rising = up == 1
 
     def at_row(behind, row, tile):
+        if heads[behind] is None:
+            return tails[behind][row * tiles + tile]
         if row < first:
-            return early[behind][row * tiles + tile]
-        return late[behind][(row - first) * tiles + tile]
+            return heads[behind][row * tiles + tile]
+        return tails[behind][(row - first) * tiles + tile]
 
     copies = []
     for behind in range(steps):
-        owner = lax.rem(me - behind + steps, steps)
+        owner = slot_owner(me, behind, steps)
         for y in range(rows):
             for tile in range(tiles):
-                if rows - reach <= min(y, rows - 1 - y):
-                    value = late[behind][(row_of(y, rows, up) - first) * tiles + tile]
-                else:
-                    value = jnp.where(
-                        rising, at_row(behind, y, tile), at_row(behind, rows - 1 - y, tile)
-                    )
+                value = jnp.where(
+                    rising, at_row(behind, y, tile), at_row(behind, rows - 1 - y, tile)
+                )
                 place = pl.multiple_of((owner * tiles + tile) * lanes, lanes)
                 held[:, y, pl.ds(place, lanes)] = value * scale
         part = pl.ds(pl.multiple_of(owner * width, lanes), width)
@@ -430,45 +481,68 @@
         copy.wait()
 
 
-def exchange(blocks, steps):
-    moved = []
-    for d in range(1, steps):
-        pairs = [(i, (i + d) % steps) for i in range(steps)]
-        moved.append(lax.ppermute(blocks[d], "tm", pairs))
-    return [blocks[0]] + moved
+def gather(blocks, steps):
+    result = [blocks[0]] + [None] * (steps - 1)
+    for d in reversed(range(1, steps)):
+        pairs = [(slot_time(t, d, steps), t) for t in range(steps)]
+        result[d] = lax.ppermute(blocks[d], "tm", pairs)
+    return result
+
+
+def scatter(blocks, steps):
+    result = list(blocks)
+    for d in reversed(range(1, steps)):
+        if blocks[d] is not None:
+            pairs = [(t, slot_time(t, d, steps)) for t in range(steps)]
+            result[d] = lax.ppermute(blocks[d], "tm", pairs)
+    return result
 
 
 def swap(value, first):
-    size, steps = lax.axis_size("space"), lax.axis_size("tm")
+    names = ("parts", "tm", "space")
+    parts, steps, size = (lax.axis_size(name) for name in names)
     pairs = []
-    for step in range(steps):
-        beside = step ^ 1 if steps % 2 == 0 else (step + 1) % steps
-        for slab in range(size):
-            partner = slab + 1 if (slab - first) % 2 == 0 else slab - 1
-            target = (step, partner) if 0 <= partner < size else (beside, slab)
-            pairs.append((step * size + slab, target[0] * size + target[1]))
-    return lax.ppermute(value, ("tm", "space"), pairs)
+    for part in range(parts):
+        for step in range(steps):
+            beside = (part ^ 1, step) if parts % 2 == 0 else (part, (step + 1) % steps)
+            for slab in range(size):
+                partner = slab + 1 if (slab - first) % 2 == 0 else slab - 1
+                target = (part, step, partner) if 0 <= partner < size else (*beside, slab)
+                here, there = (
+                    (p * steps + t) * size + c for p, t, c in ((part, step, slab), target)
+                )
+                pairs.append((here, there))
+    return lax.ppermute(value, names, pairs)
 
 
 def fast_local(rhs, diffusivity, velocity):
     _, depth, rows, columns = rhs.shape
     steps = lax.axis_size("tm")
     tiles = columns // steps // lanes
+    sheets = depth // sublanes
     log_alpha = math.log(circ_alpha) / steps
     extended, wide = rows + 2 * reach, tiles + 1
     fields = steps
-    blocks = exchange(pack(rhs[0], steps), steps)
+    blocks = gather(pack(rhs[0], steps), steps)
+    piece = reach * tiles * sheets + 1
     made = [(extended, wide, depth, lanes), (fields, extended, wide, depth, lanes)]
     iterates = [(fields, extended, wide, depth + 16, lanes)] * reach
-    own, kappa, inverse, drift, *margins = call(
+    own, own_far, kappa, inverse, drift, *margins = call(
         functools.partial(prepare_kernel, "tm", "space", rows, tiles, steps),
-        [(rows * tiles + 1, depth, lanes), *made, (3, depth, lanes), *iterates],
+        [
+            (rows * tiles * sheets + 1, sublanes, lanes),
+            (piece, sublanes, lanes),
+            *made,
+            (3, depth, lanes),
+            *iterates,
+        ],
         diffusivity,
         velocity,
         specs={0: hbm, 1: smem},
         scratch=staging(diffusivity.shape),
     )
-    near, far = halos([*blocks, own], rows, tiles)
+    kappa_far = swap(own_far, 1)
+    near, far = halos(blocks, own, piece)
     far, near = swap(far, 1), swap(near, 0)
     state = [*made, *iterates, made[1]]
     early = rows - reach
@@ -483,21 +557,26 @@
         *kept,
         aliases={steps + 2 + i: i for i in range(len(kept))},
     )
-    first_rows = exchange(held[len(state) :], steps)
+    state_now, finished = held[: len(state)], held[len(state) :]
+    in_two = [d == 0 or d in early_moves for d in range(steps)]
+    heads = scatter([finished[d] if in_two[d] else None for d in range(steps)], steps)
+    heads = [head for head in heads if head is not None]
     held = call(
         functools.partial(solve, True),
-        state + [(reach * tiles, depth, lanes)] * steps,
+        state + [((reach if two else rows) * tiles, depth, lanes) for two in in_two],
         far,
+        kappa_far,
         drift,
-        *held[: len(state)],
-        aliases={2 + i: i for i in range(len(state))},
-    )
-    last_rows = exchange(held[len(state) :], steps)
+        *state_now,
+        *(finished[d] for d in range(steps) if not in_two[d]),
+        aliases={3 + i: i for i in range(len(state))},
+    )
+    tails = scatter(held[len(state) :], steps)
     (result,) = call(
-        functools.partial(unpack_kernel, "tm", "space", log_alpha, steps),
+        functools.partial(unpack_kernel, "tm", "space", log_alpha, steps, tuple(in_two)),
         [(depth, rows, columns)],
-        *first_rows,
-        *last_rows,
+        *heads,
+        *tails,
         kept=False,
         scratch=[
             pltpu.VMEM((depth, rows, columns), jnp.float32),
@@ -617,8 +696,10 @@
 
 def local(rhs, diffusivity, velocity):
     steps = lax.axis_size("tm")
-    local_steps, _, rows, columns = rhs.shape
-    if local_steps == 1 and rows >= reach and lanes % rows == 0 and columns % (steps * lanes) == 0:
+    local_steps, depth, rows, columns = rhs.shape
+    slots = rows * (depth // sublanes)
+    tiled = columns % (steps * lanes) == 0 and depth % sublanes == 0
+    if local_steps == 1 and rows >= reach and tiled and 2 * reach * slots <= lanes:
         return fast_local(rhs, diffusivity, velocity)
     return general_local(rhs, diffusivity, velocity)
 

time: 35.7 us -> 33.4 us (0.936)
  starting transfers between devices: 15.8 us -> 14.6 us
  waiting for transfers between devices: 11.8 us -> 10.7 us
    ppermute x11, starting transfers between devices: 15.8 us -> 14.6 us  [the longest x5 6.7 us: scatter(): result[d] = lax.ppermute(blocks[d], 'tm', pairs)]
    ppermute x11, waiting for transfers between devices: 11.8 us -> 10.7 us  [the longest x5 4.19 us: scatter(): result[d] = lax.ppermute(blocks[d], 'tm', pairs)]
  transfers between devices with their start and end apart: 11 -> 11, of which waited for: 6 -> 5; matrix products, arithmetic and copies ran while one was open for 0% -> 0% of each run, Pallas kernels for 10% -> 10%
where the time goes in v6:
time: 33.4 us; the launch traced here: 33.1 us
  starting transfers between devices  14.6 us (44%)
  waiting for transfers between devices  10.7 us (32%)
  Pallas kernels  7.13 us (21%)
  local copies, waits for them, and re-layouts  0.66 us (2%)
    pallas_call x6, Pallas kernels, call(): pl.pallas_call(kernel, out_shape=[make(o, jnp.float32) for o in outs], in...  7.13 us
    ppermute x5, starting transfers between devices, scatter(): result[d] = lax.ppermute(blocks[d], 'tm', pairs)  6.7 us
    ppermute x3, starting transfers between devices, gather(): result[d] = lax.ppermute(blocks[d], 'tm', pairs)  5.71 us
    ppermute x5, waiting for transfers between devices, scatter(): result[d] = lax.ppermute(blocks[d], 'tm', pairs)  4.19 us
    ppermute x3, waiting for transfers between devices, gather(): result[d] = lax.ppermute(blocks[d], 'tm', pairs)  3.63 us
    ppermute x3, waiting for transfers between devices, swap(): return lax.ppermute(value, names, pairs)  2.89 us
    ppermute x3, starting transfers between devices, swap(): return lax.ppermute(value, names, pairs)  2.16 us
  transfers between devices with their start and end apart: 11, of which 5 were waited for; matrix products, arithmetic and copies ran while one was open for 0% of the time, Pallas kernels for 10%

profile of v6, /device:TPU:0, one launch (start us, length us, event | category | flops | bytes accessed | tf_op | source)
XLA Modules:
  0.0 33.1 jit_solution(1900123624366358384)
XLA Ops:
  0.0 1.4 %shard_map.37 = (f32[17,8,128]{2,1,0:T(8,128)S(1)}, f32[17,8,128]{2,1,0:T(8,128)S(1)}, f32[17,8,128]{2,1,0:T(8,128)S(1)}, f32[17,8,128]{2,1,0:T(8,128)S(1)}) custom-call(f32[16,4,1024]{2,1,0:T(4,128)} %bitcast.2), custom_call_target="tpu_custom_call" | custom-call | tf_op jit(solution)/shard_map/pallas_call | solution.py:39
  1.4 3.1 %collective-permute-start = (f32[17,8,128]{2,1,0:T(8,128)S(1)}, f32[17,8,128]{2,1,0:T(8,128)S(1)}, u32[]{:S(2)}, u32[]{:S(2)}) collective-permute-start(f32[17,8,128]{2,1,0:T(8,128)S(1)} %get-tuple-element.34), channel_id=1, source_target_pairs={{4,0},{0,4},{12,8},{8,12},{5,1},{1,5},{13,9},{9,13},{6,2},{2,6},{1... | collective-permute-start | bytes 208904 | tf_op jit(solution)/shard_map/ppermute | solution.py:488
  4.5 2.6 %collective-permute-start.1 = (f32[17,8,128]{2,1,0:T(8,128)S(1)}, f32[17,8,128]{2,1,0:T(8,128)S(1)}, u32[]{:S(2)}, u32[]{:S(2)}) collective-permute-start(f32[17,8,128]{2,1,0:T(8,128)S(1)} %get-tuple-element.35), channel_id=1, source_target_pairs={{8,0},{12,4},{0,8},{4,12},{9,1},{13,5},{1,9},{5,13},{10,2},{14,6},... | collective-permute-start | bytes 208904 | tf_op jit(solution)/shard_map/ppermute | solution.py:488
  7.1 0.0 collective-permute-start.2
  7.1 0.0 copy-start
  7.1 0.7 %copy-done = f32[3]{0:T(128)S(1)} copy-done((f32[3]{0:T(128)S(1)}, f32[3]{0:T(128)}, u32[]{:S(2)}) %copy-start) | copy-done | bytes 36
  7.7 1.9 %shard_map.38 = (f32[17,8,128]{2,1,0:T(8,128)S(1)}, f32[13,8,128]{2,1,0:T(8,128)S(1)}, f32[10,3,16,128]{3,2,1,0:T(8,128)S(1)}, f32[4,10,3,16,128]{4,3,2,1,0:T(8,...) custom-call(f32[16,4,1024]{2,1,0:T(4,128)} %diffusivity.1, ...), custom_call_target="tpu_custom_call" | custom-call | tf_op jit(solution)/shard_map/pallas_call | solution.py:39
  9.6 0.0 collective-permute-done.refs_1_
  9.7 2.4 %collective-permute-done.1.refs_2_ = f32[17,8,128]{2,1,0:T(8,128)S(1)} collective-permute-done((f32[17,8,128]{2,1,0:T(8,128)S(1)}, f32[17,8,128]{2,1,0:T(8,128)S(1)}, u32[]{:S(2)}, u32[]{:S(2)}) %collective-permute-start.1) | collective-permute-done | bytes 69664 | tf_op jit(solution)/shard_map/ppermute | solution.py:488
  12.0 1.3 %collective-permute-done.2.refs_3_ = f32[17,8,128]{2,1,0:T(8,128)S(1)} collective-permute-done((f32[17,8,128]{2,1,0:T(8,128)S(1)}, f32[17,8,128]{2,1,0:T(8,128)S(1)}, u32[]{:S(2)}, u32[]{:S(2)}) %collective-permute-start.2) | collective-permute-done | bytes 69664 | tf_op jit(solution)/shard_map/ppermute | solution.py:488
  13.3 0.1 collective-permute-start.3
  13.4 1.6 %collective-permute-start.6 = (f32[52,8,128]{2,1,0:T(8,128)S(1)}, f32[52,8,128]{2,1,0:T(8,128)S(1)}, u32[]{:S(2)}, u32[]{:S(2)}) collective-permute-start(f32[52,8,128]{2,1,0:T(8,128)S(1)} %get-tuple-element.48), channel_id=1, source_target_pairs={{0,16},{1,2},{2,1},{3,19},{4,20},{5,6},{6,5},{7,23},{8,24},{9,10},... | collective-permute-start | bytes 638984 | tf_op jit(solution)/shard_map/ppermute | solution.py:515
  15.0 0.5 %collective-permute-start.7 = (f32[13,8,128]{2,1,0:T(8,128)S(1)}, f32[13,8,128]{2,1,0:T(8,128)S(1)}, u32[]{:S(2)}, u32[]{:S(2)}) collective-permute-start(f32[13,8,128]{2,1,0:T(8,128)S(1)} %get-tuple-element.49), channel_id=1, source_target_pairs={{0,16},{1,2},{2,1},{3,19},{4,20},{5,6},{6,5},{7,23},{8,24},{9,10},... | collective-permute-start | bytes 159752 | tf_op jit(solution)/shard_map/ppermute | solution.py:515
  15.5 0.0 collective-permute-done.3.refs_4_
  15.5 1.5 %shard_map.40 = (f32[10,3,16,128]{3,2,1,0:T(8,128)S(1)}, f32[4,10,3,16,128]{4,3,2,1,0:T(8,128)S(1)}, f32[4,10,3,32,128]{4,3,2,1,0:T(8,128)S(1)}, f32[4,10,3,32,1...) custom-call(f32[17,8,128]{2,1,0:T(8,128)S(1)} %get-tuple-element.33., ...), custom_call_target="tpu_custom_call", output_to_operand_aliasing={{0}: (6, {}), {1}: (7, {}), {2}: (8, {}), {3}: (9, {}), {4}... | custom-call | tf_op jit(solution)/shard_map/pallas_call | solution.py:39
  17.0 2.9 %collective-permute-done.7.refs_1_ = f32[13,8,128]{2,1,0:T(8,128)S(1)} collective-permute-done((f32[13,8,128]{2,1,0:T(8,128)S(1)}, f32[13,8,128]{2,1,0:T(8,128)S(1)}, u32[]{:S(2)}, u32[]{:S(2)}) %collective-permute-start.7) | collective-permute-done | bytes 53280 | tf_op jit(solution)/shard_map/ppermute | solution.py:515
  19.9 0.0 collective-permute-done.6.refs_0_
  19.9 1.4 %shard_map.41 = (f32[10,3,16,128]{3,2,1,0:T(8,128)S(1)}, f32[4,10,3,16,128]{4,3,2,1,0:T(8,128)S(1)}, f32[4,10,3,32,128]{4,3,2,1,0:T(8,128)S(1)}, f32[4,10,3,32,1...) custom-call(f32[52,8,128]{2,1,0:T(8,128)S(1)} %collective-permute-do, ...), custom_call_target="tpu_custom_call", output_to_operand_aliasing={{0}: (3, {}), {1}: (4, {}), {2}: (5, {}), {3}: (6, {}), {4}... | custom-call | tf_op jit(solution)/shard_map/pallas_call | solution.py:39
  21.3 0.8 %collective-permute-start.8 = (f32[8,16,128]{2,1,0:T(8,128)S(1)}, f32[8,16,128]{2,1,0:T(8,128)S(1)}, u32[]{:S(2)}, u32[]{:S(2)}) collective-permute-start(f32[8,16,128]{2,1,0:T(8,128)S(1)} %get-tuple-element.58), channel_id=1, source_target_pairs={{0,4},{4,0},{8,12},{12,8},{1,5},{5,1},{9,13},{13,9},{2,6},{6,2},{1... | collective-permute-start | bytes 196616 | tf_op jit(solution)/shard_map/ppermute | solution.py:497
  22.1 1.7 %collective-permute-start.9 = (f32[6,16,128]{2,1,0:T(8,128)S(1)}, f32[6,16,128]{2,1,0:T(8,128)S(1)}, u32[]{:S(2)}, u32[]{:S(2)}) collective-permute-start(f32[6,16,128]{2,1,0:T(8,128)S(1)} %get-tuple-element.59), channel_id=1, source_target_pairs={{0,8},{4,12},{8,0},{12,4},{1,9},{5,13},{9,1},{13,5},{2,10},{6,14},... | collective-permute-start | bytes 147464 | tf_op jit(solution)/shard_map/ppermute | solution.py:497
  23.9 1.9 %collective-permute-start.10 = (f32[6,16,128]{2,1,0:T(8,128)S(1)}, f32[6,16,128]{2,1,0:T(8,128)S(1)}, u32[]{:S(2)}, u32[]{:S(2)}) collective-permute-start(f32[6,16,128]{2,1,0:T(8,128)S(1)} %get-tuple-element.60), channel_id=1, source_target_pairs={{0,12},{4,8},{8,4},{12,0},{1,13},{5,9},{9,5},{13,1},{2,14},{6,10},... | collective-permute-start | bytes 147464 | tf_op jit(solution)/shard_map/ppermute | solution.py:497
  25.7 0.9 %collective-permute-start.4 = (f32[2,16,128]{2,1,0:T(8,128)S(1)}, f32[2,16,128]{2,1,0:T(8,128)S(1)}, u32[]{:S(2)}, u32[]{:S(2)}) collective-permute-start(f32[2,16,128]{2,1,0:T(8,128)S(1)} %get-tuple-element.46), channel_id=1, source_target_pairs={{0,8},{4,12},{8,0},{12,4},{1,9},{5,13},{9,1},{13,5},{2,10},{6,14},... | collective-permute-start | bytes 49160 | tf_op jit(solution)/shard_map/ppermute | solution.py:497
  26.6 1.3 %collective-permute-start.5 = (f32[2,16,128]{2,1,0:T(8,128)S(1)}, f32[2,16,128]{2,1,0:T(8,128)S(1)}, u32[]{:S(2)}, u32[]{:S(2)}) collective-permute-start(f32[2,16,128]{2,1,0:T(8,128)S(1)} %get-tuple-element.47), channel_id=1, source_target_pairs={{0,12},{4,8},{8,4},{12,0},{1,13},{5,9},{9,5},{13,1},{2,14},{6,10},... | collective-permute-start | bytes 49160 | tf_op jit(solution)/shard_map/ppermute | solution.py:497
  28.0 3.1 %collective-permute-done.4.refs_1_ = f32[2,16,128]{2,1,0:T(8,128)S(1)} collective-permute-done((f32[2,16,128]{2,1,0:T(8,128)S(1)}, f32[2,16,128]{2,1,0:T(8,128)S(1)}, u32[]{:S(2)}, u32[]{:S(2)}) %collective-permute-start.4) | collective-permute-done | bytes 16416 | tf_op jit(solution)/shard_map/ppermute | solution.py:497
  31.1 1.1 %collective-permute-done.5.refs_2_ = f32[2,16,128]{2,1,0:T(8,128)S(1)} collective-permute-done((f32[2,16,128]{2,1,0:T(8,128)S(1)}, f32[2,16,128]{2,1,0:T(8,128)S(1)}, u32[]{:S(2)}, u32[]{:S(2)}) %collective-permute-start.5) | collective-permute-done | bytes 16416 | tf_op jit(solution)/shard_map/ppermute | solution.py:497
  32.2 0.0 collective-permute-done.9.refs_5_
  32.2 0.0 collective-permute-done.10.refs_6_
  32.2 0.0 collective-permute-done.8.refs_4_
  32.2 0.9 %shard_map.42 = f32[16,4,1024]{2,1,0:T(4,128)} custom-call(f32[2,16,128]{2,1,0:T(8,128)S(1)} %get-tuple-element.45.refs_0_, f32[2,16,128]{2,1,0:T(8,128)S(1)} %collective-permute-done.4.refs_1_, f32[2,16,128]{2,1,0:T(8,128)S(1)} %collective-permute-done.5.refs_2_, f32[6,16,128]{2,1,0:T(8,128)S(1)} %get-tuple-element.57.refs_3_, ...), custom_call_target="tpu_custom_call" | custom-call | tf_op jit(solution)/shard_map/pallas_call | solution.py:39
  (1 shorter events, 0.0 us)
Async XLA Ops:
  1.4 8.3 %collective-permute-start = (f32[17,8,128]{2,1,0:T(8,128)S(1)}, f32[17,8,128]{2,1,0:T(8,128)S(1)}, u32[]{:S(2)}, u32[]{:S(2)}) collective-permute-start(f32[17,8,128]{2,1,0:T(8,128)S(1)} %get-tuple-element.34), channel_id=1, source_target_pairs={{4,0},{0,4},{12,8},{8,12},{5,1},{1,5},{13,9},{9,13},{6,2},{2,6},{1... | collective-permute-start | bytes 208904 | tf_op jit(solution)/shard_map/ppermute | solution.py:488
  4.5 7.5 %collective-permute-start.1 = (f32[17,8,128]{2,1,0:T(8,128)S(1)}, f32[17,8,128]{2,1,0:T(8,128)S(1)}, u32[]{:S(2)}, u32[]{:S(2)}) collective-permute-start(f32[17,8,128]{2,1,0:T(8,128)S(1)} %get-tuple-element.35), channel_id=1, source_target_pairs={{8,0},{12,4},{0,8},{4,12},{9,1},{13,5},{1,9},{5,13},{10,2},{14,6},... | collective-permute-start | bytes 208904 | tf_op jit(solution)/shard_map/ppermute | solution.py:488
  7.1 6.2 %collective-permute-start.2 = (f32[17,8,128]{2,1,0:T(8,128)S(1)}, f32[17,8,128]{2,1,0:T(8,128)S(1)}, u32[]{:S(2)}, u32[]{:S(2)}) collective-permute-start(f32[17,8,128]{2,1,0:T(8,128)S(1)} %get-tuple-element.36), channel_id=1, source_target_pairs={{12,0},{8,4},{4,8},{0,12},{13,1},{9,5},{5,9},{1,13},{14,2},{10,6},... | collective-permute-start | bytes 208904 | tf_op jit(solution)/shard_map/ppermute | solution.py:488
  7.1 0.7 %copy-start = (f32[3]{0:T(128)S(1)}, f32[3]{0:T(128)}, u32[]{:S(2)}) copy-start(f32[3]{0:T(128)} %velocity.1) | copy-start | bytes 40
  13.3 2.2 %collective-permute-start.3 = (f32[65,8,128]{2,1,0:T(8,128)S(1)}, f32[65,8,128]{2,1,0:T(8,128)S(1)}, u32[]{:S(2)}, u32[]{:S(2)}) collective-permute-start(f32[65,8,128]{2,1,0:T(8,128)S(1)} %get-tuple-element.38), channel_id=1, source_target_pairs={{0,1},{1,0},{2,3},{3,2},{4,5},{5,4},{6,7},{7,6},{8,9},{9,8},{10,11... | collective-permute-start | bytes 798728 | tf_op jit(solution)/shard_map/ppermute | solution.py:515
  13.4 6.5 %collective-permute-start.6 = (f32[52,8,128]{2,1,0:T(8,128)S(1)}, f32[52,8,128]{2,1,0:T(8,128)S(1)}, u32[]{:S(2)}, u32[]{:S(2)}) collective-permute-start(f32[52,8,128]{2,1,0:T(8,128)S(1)} %get-tuple-element.48), channel_id=1, source_target_pairs={{0,16},{1,2},{2,1},{3,19},{4,20},{5,6},{6,5},{7,23},{8,24},{9,10},... | collective-permute-start | bytes 638984 | tf_op jit(solution)/shard_map/ppermute | solution.py:515
  15.0 4.9 %collective-permute-start.7 = (f32[13,8,128]{2,1,0:T(8,128)S(1)}, f32[13,8,128]{2,1,0:T(8,128)S(1)}, u32[]{:S(2)}, u32[]{:S(2)}) collective-permute-start(f32[13,8,128]{2,1,0:T(8,128)S(1)} %get-tuple-element.49), channel_id=1, source_target_pairs={{0,16},{1,2},{2,1},{3,19},{4,20},{5,6},{6,5},{7,23},{8,24},{9,10},... | collective-permute-start | bytes 159752 | tf_op jit(solution)/shard_map/ppermute | solution.py:515
  21.3 10.9 %collective-permute-start.8 = (f32[8,16,128]{2,1,0:T(8,128)S(1)}, f32[8,16,128]{2,1,0:T(8,128)S(1)}, u32[]{:S(2)}, u32[]{:S(2)}) collective-permute-start(f32[8,16,128]{2,1,0:T(8,128)S(1)} %get-tuple-element.58), channel_id=1, source_target_pairs={{0,4},{4,0},{8,12},{12,8},{1,5},{5,1},{9,13},{13,9},{2,6},{6,2},{1... | collective-permute-start | bytes 196616 | tf_op jit(solution)/shard_map/ppermute | solution.py:497
  22.1 10.0 %collective-permute-start.9 = (f32[6,16,128]{2,1,0:T(8,128)S(1)}, f32[6,16,128]{2,1,0:T(8,128)S(1)}, u32[]{:S(2)}, u32[]{:S(2)}) collective-permute-start(f32[6,16,128]{2,1,0:T(8,128)S(1)} %get-tuple-element.59), channel_id=1, source_target_pairs={{0,8},{4,12},{8,0},{12,4},{1,9},{5,13},{9,1},{13,5},{2,10},{6,14},... | collective-permute-start | bytes 147464 | tf_op jit(solution)/shard_map/ppermute | solution.py:497
  23.9 8.3 %collective-permute-start.10 = (f32[6,16,128]{2,1,0:T(8,128)S(1)}, f32[6,16,128]{2,1,0:T(8,128)S(1)}, u32[]{:S(2)}, u32[]{:S(2)}) collective-permute-start(f32[6,16,128]{2,1,0:T(8,128)S(1)} %get-tuple-element.60), channel_id=1, source_target_pairs={{0,12},{4,8},{8,4},{12,0},{1,13},{5,9},{9,5},{13,1},{2,14},{6,10},... | collective-permute-start | bytes 147464 | tf_op jit(solution)/shard_map/ppermute | solution.py:497
  25.7 5.4 %collective-permute-start.4 = (f32[2,16,128]{2,1,0:T(8,128)S(1)}, f32[2,16,128]{2,1,0:T(8,128)S(1)}, u32[]{:S(2)}, u32[]{:S(2)}) collective-permute-start(f32[2,16,128]{2,1,0:T(8,128)S(1)} %get-tuple-element.46), channel_id=1, source_target_pairs={{0,8},{4,12},{8,0},{12,4},{1,9},{5,13},{9,1},{13,5},{2,10},{6,14},... | collective-permute-start | bytes 49160 | tf_op jit(solution)/shard_map/ppermute | solution.py:497
  26.6 5.5 %collective-permute-start.5 = (f32[2,16,128]{2,1,0:T(8,128)S(1)}, f32[2,16,128]{2,1,0:T(8,128)S(1)}, u32[]{:S(2)}, u32[]{:S(2)}) collective-permute-start(f32[2,16,128]{2,1,0:T(8,128)S(1)} %get-tuple-element.47), channel_id=1, source_target_pairs={{0,12},{4,8},{8,4},{12,0},{1,13},{5,9},{9,5},{13,1},{2,14},{6,10},... | collective-permute-start | bytes 49160 | tf_op jit(solution)/shard_map/ppermute | solution.py:497

commit v7 on v6

--- a/solution.py
+++ b/solution.py
@@ -85,11 +85,18 @@
     return lanes // (rows * sheets)
 
 
-def pick_block(source, write, write_halo, owner, owners, up):
-    depth, rows, columns = source.shape
+def turn(source, target, scale=None):
+    _, rows, columns = source.shape
+    for tile in range(columns // lanes):
+        column = pltpu.einshape("zyx->yzx", source[:, :, tile * lanes : (tile + 1) * lanes])
+        target[pl.ds(tile * rows, rows)] = column if scale is None else column * scale
+
+
+def pick_block(source, rows, out, owner, owners, up):
+    count, depth, _ = source.shape
     sheets = depth // sublanes
     width = slot_width(rows, sheets)
-    total = columns // lanes
+    total = count // rows
     tiles = total // owners
     left_tile = jnp.maximum(owner * tiles - 1, 0)
     right_tile = jnp.minimum((owner + 1) * tiles, total - 1)
@@ -97,20 +104,16 @@
     right = (owner < owners - 1).astype(jnp.float32)
     keep_right, keep_left = column_mask(left, right, (depth, lanes))
     packed = None
-
-    def tile_at(y, tile):
-        return source[:, y, pl.ds(pl.multiple_of(tile * lanes, lanes), lanes)]
-
     for y in range(rows):
         row = row_of(y, rows, up)
         for tile in range(tiles):
-            write(row * tiles + tile, tile_at(y, owner * tiles + tile))
-        halo = tile_at(y, right_tile) * keep_right + tile_at(y, left_tile) * keep_left
+            put(out, row * tiles + tile, source[(owner * tiles + tile) * rows + y])
+        halo = source[right_tile * rows + y] * keep_right + source[left_tile * rows + y] * keep_left
         for sheet in range(sheets):
             part = halo[sheet * sublanes : (sheet + 1) * sublanes]
             part = pltpu.roll(part, (row * sheets + sheet) * width, 1)
             packed = part if packed is None else packed + part
-    write_halo(packed)
+    out[out.shape[0] - 1] = packed
 
 
 def fetch(source, target, semaphores):
@@ -129,26 +132,22 @@
 
 
 def pack_kernel(tm, space, log_alpha, steps, rhs, *refs):
-    outs, (held, semaphores) = refs[:steps], refs[steps:]
+    outs, (held, semaphores, turned) = refs[:steps], refs[steps:]
     me, up = lax.axis_index(tm), upwards(space)
     fetch(rhs, held, semaphores)
-    scale = jnp.exp(jnp.full((sublanes, lanes), me.astype(jnp.float32) * log_alpha, jnp.float32))
-    tall = jnp.concatenate([scale] * (rhs.shape[0] // sublanes))
+    shape = (1, rhs.shape[0], lanes)
+    turn(held, turned, jnp.exp(jnp.full(shape, me.astype(jnp.float32) * log_alpha, jnp.float32)))
     for ahead in reversed(range(steps)):
-        out = outs[ahead]
-
-        def write(index, value, out=out):
-            put(out, index, value * tall)
-
-        def write_halo(value, out=out):
-            out[out.shape[0] - 1] = value * scale
-
-        pick_block(held, write, write_halo, slot_owner(me, ahead, steps), steps, up)
+        pick_block(turned, rhs.shape[1], outs[ahead], slot_owner(me, ahead, steps), steps, up)
 
 
 def staging(shape):
-    pieces = math.gcd(shape[0], 4)
-    return [pltpu.VMEM(shape, jnp.float32), pltpu.SemaphoreType.DMA((pieces,))]
+    depth, rows, columns = shape
+    return [
+        pltpu.VMEM(shape, jnp.float32),
+        pltpu.SemaphoreType.DMA((math.gcd(depth, 4),)),
+        pltpu.VMEM((columns // lanes * rows, depth, lanes), jnp.float32),
+    ]
 
 
 def pack(rhs, steps):
@@ -168,16 +167,16 @@
 
 
 def halo_kernel(piece, *refs):
-    blocks, (near, far) = refs[:-2], refs[-2:]
+    blocks, (near, far) = refs[:-3], refs[-2:]
     for step, block in enumerate(blocks):
         copy_piece(block, True, piece, near, step * piece)
         if (step + 1) * piece <= far.shape[0]:
             copy_piece(block, False, piece, far, step * piece)
 
 
-def halos(blocks, own, piece):
+def halos(blocks, own, ready, piece):
     outs = [(count * piece, sublanes, lanes) for count in (len(blocks) + 1, len(blocks))]
-    return call(functools.partial(halo_kernel, piece), outs, *blocks, own)
+    return call(functools.partial(halo_kernel, piece), outs, *blocks, own, ready)
 
 
 def row_piece(own, near, far, step, row, tile, rows, tiles, depth):
@@ -234,15 +233,25 @@
     return keep_right + keep_left
 
 
-def prepare_kernel(tm, space, rows, tiles, steps, diffusivity, velocity, *refs):
-    own, own_far, kappa, inverse, drift, *iterates = refs[:-2]
-    held, semaphores = refs[-2:]
+def kappa_kernel(tm, space, steps, diffusivity, velocity, *refs):
+    own, own_far, drift, held, semaphores, turned, speeds, semaphore = refs
     up = upwards(space)
-    depth = diffusivity.shape[0]
+    copy = pltpu.make_async_copy(velocity, speeds, semaphore)
+    copy.start()
+    fetch(diffusivity, held, semaphores)
+
+    turn(held, turned)
+    pick_block(turned, diffusivity.shape[1], own, lax.axis_index(tm), steps, up)
+    copy_piece(own, False, own_far.shape[0], own_far, 0)
+    copy.wait()
     direction = (2 * up - 1).astype(jnp.float32)
     for j in range(3):
-        speed = 0.5 * velocity[j]
-        drift[j] = jnp.full((depth, lanes), speed * direction if j == 1 else speed, jnp.float32)
+        speed = 0.5 * speeds[j]
+        drift[j] = jnp.full(drift.shape[1:], speed * direction if j == 1 else speed, jnp.float32)
+
+
+def prepare_kernel(tm, rows, tiles, steps, own, kappa, inverse, *iterates):
+    depth = kappa.shape[2]
     zero = jnp.zeros((8, lanes), jnp.float32)
     for level, ref in enumerate(iterates):
         fields, extended, wide = ref.shape[:3]
@@ -251,16 +260,6 @@
                 for tile in range(wide):
                     ref[field, row, tile, pl.ds(0, 8), :] = zero
                     ref[field, row, tile, pl.ds(8 + depth, 8), :] = zero
-    fetch(diffusivity, held, semaphores)
-
-    def write(index, value):
-        put(own, index, value)
-
-    def write_halo(value):
-        own[own.shape[0] - 1] = value
-
-    pick_block(held, write, write_halo, lax.axis_index(tm), steps, up)
-    copy_piece(own, False, own_far.shape[0], own_far, 0)
     halo_mask = side_mask(tm, steps, depth)
     for row in range(reach, reach + rows):
         for tile in range(tiles + 1):
@@ -305,14 +304,14 @@
     if second_half:
         far, kappa_far, drift = refs[:3]
         done = sum(ahead not in early_moves for ahead in range(1, steps))
-        finished, refs = refs[4 + made : 4 + made + done], refs[4 + made + done :]
+        finished, refs = refs[3 + made : 3 + made + done], refs[3 + made + done :]
         kappa, inverse, *iterates = refs[:made]
-        source, *outs = refs[made:]
+        outs = refs[made:]
         blocks, near = [None] * steps, None
     else:
         blocks, (near, drift) = refs[:steps], refs[steps : steps + 2]
         kappa, inverse, *iterates = refs[steps + 2 + made :][:made]
-        source, *outs = refs[steps + 2 + made + made :]
+        outs = refs[steps + 2 + made + made :]
         far, kappa_far = None, None
     depth = kappa.shape[2]
     pad = 8
@@ -369,18 +368,25 @@
                     values.append(combine((-sine(k * b, steps), held[b]) for b in range(steps)))
             quotients = divide(values, row, tile)
             for field in range(fields):
-                source[field, row, tile] = values[field]
-                iterates[0][field, row, tile, middle, :] = relax_weights[0] * quotients[field]
-
-    def sweep(row, old, weight, last):
+                iterates[0][field, row, tile, middle, :] = quotients[field]
+
+
+    def sweep(row, level):
+        with_halo = level < row < extended - 1 - level and level < levels
+        old = iterates[level - 1]
+        scale, weight = relax_weights[level - 1], relax_weights[level]
+        keep = (1.0 - weight) * scale / weight + (1.0 if level == 1 else 0.0)
+        tilt = [scale * h for h in half]
         centers = [
             [old[field, row, tile, middle, :] for tile in range(wide)] for field in range(fields)
         ]
         shifted_down = [[pltpu.roll(c, 1, 1) for c in line] for line in centers]
         shifted_up = [[pltpu.roll(c, lanes - 1, 1) for c in line] for line in centers]
-        for tile in range(tiles if last else wide):
+        for tile in range(wide if with_halo else tiles):
             values = []
-            coefficient = kappa[row, tile]
+            scaled = scale * kappa[row, tile]
+            below = [scaled + t for t in tilt]
+            above = [scaled - t for t in tilt]
             for field in range(fields):
                 lower_x = jnp.where(
                     at_first, shifted_down[field][(tile - 1) % wide], shifted_down[field][tile]
@@ -392,28 +398,25 @@
                 upper_z = old[field, row, tile, pl.ds(pad + 1, depth), :]
                 lower_y = old[field, row - 1, tile, middle, :]
                 upper_y = old[field, row + 1, tile, middle, :]
-                around = (lower_z + upper_z) + (lower_y + upper_y) + (lower_x + upper_x)
-                slope = (
-                    half[0] * (lower_z - upper_z)
-                    + half[1] * (lower_y - upper_y)
-                    + half[2] * (lower_x - upper_x)
+                values.append(
+                    (below[0] * lower_z + above[0] * upper_z)
+                    + (below[1] * lower_y + above[1] * upper_y)
+                    + (below[2] * lower_x + above[2] * upper_x)
                 )
-                values.append(source[field, row, tile] + (coefficient * around + slope))
             quotients = divide(values, row, tile)
-            yield tile, [
-                (1.0 - weight) * centers[field][tile] + weight * quotients[field]
-                for field in range(fields)
-            ]
+            results = []
+            for field in range(fields):
+                value = keep * centers[field][tile] + quotients[field]
+                if level > 1:
+                    value = value + iterates[0][field, row, tile, middle, :]
+                results.append(value)
+            yield tile, results
 
     for level in range(1, levels):
-
-        def step(row, carry, level=level):
-            for tile, results in sweep(row, iterates[level - 1], relax_weights[level], False):
+        for row in range(*rows_of(level)):
+            for tile, results in sweep(row, level):
                 for field in range(fields):
                     iterates[level][field, row, tile, middle, :] = results[field]
-            return carry
-
-        lax.fori_loop(*rows_of(level), step, 0)
 
     last_rows = rows_of(levels)
     skipped = [0] * steps
@@ -423,12 +426,12 @@
             skipped[ahead] = (rows - reach) * tiles
             outs[ahead][pl.ds(0, block.shape[0])] = block[...]
 
-    def last_step(row, carry):
-        for tile, results in sweep(row, iterates[levels - 1], relax_weights[levels], True):
+    for row in range(*last_rows):
+        for tile, results in sweep(row, levels):
             for ahead in range(steps):
                 terms, field = [], 0
                 for k, is_complex in freqs:
-                    factor = (2.0 if is_complex else 1.0) / steps
+                    factor = relax_weights[levels] * (2.0 if is_complex else 1.0) / steps
                     terms.append((factor * cosine(k * ahead, steps), results[field]))
                     field += 1
                     if is_complex:
@@ -436,9 +439,6 @@
                         field += 1
                 place = (row - last_rows[0]) * tiles + tile + skipped[ahead]
                 outs[ahead][place] = combine(terms)
-        return carry
-
-    lax.fori_loop(*last_rows, last_step, 0)
 
 
 def unpack_kernel(tm, space, log_alpha, steps, early, *refs):
@@ -449,7 +449,8 @@
     depth, rows, columns = out.shape
     width = columns // steps
     tiles = width // lanes
-    scale = jnp.exp(jnp.full((depth, lanes), me.astype(jnp.float32) * -log_alpha, jnp.float32))
+    shape = (1, depth, lanes)
+    scale = jnp.exp(jnp.full(shape, me.astype(jnp.float32) * -log_alpha, jnp.float32))
     first = rows - reach
     rising = up == 1
 
@@ -463,13 +464,14 @@
     copies = []
     for behind in range(steps):
         owner = slot_owner(me, behind, steps)
-        for y in range(rows):
-            for tile in range(tiles):
-                value = jnp.where(
-                    rising, at_row(behind, y, tile), at_row(behind, rows - 1 - y, tile)
-                )
-                place = pl.multiple_of((owner * tiles + tile) * lanes, lanes)
-                held[:, y, pl.ds(place, lanes)] = value * scale
+        for tile in range(tiles):
+            column = [
+                jnp.where(rising, at_row(behind, y, tile), at_row(behind, rows - 1 - y, tile))
+                for y in range(rows)
+            ]
+            column = pltpu.einshape("yzx->zyx", jnp.stack(column) * scale)
+            place = pl.multiple_of((owner * tiles + tile) * lanes, lanes)
+            held[:, :, pl.ds(place, lanes)] = column
         part = pl.ds(pl.multiple_of(owner * width, lanes), width)
         copies.append(
             pltpu.make_async_copy(
@@ -527,24 +529,30 @@
     piece = reach * tiles * sheets + 1
     made = [(extended, wide, depth, lanes), (fields, extended, wide, depth, lanes)]
     iterates = [(fields, extended, wide, depth + 16, lanes)] * reach
-    own, own_far, kappa, inverse, drift, *margins = call(
-        functools.partial(prepare_kernel, "tm", "space", rows, tiles, steps),
+    own, own_far, drift = call(
+        functools.partial(kappa_kernel, "tm", "space", steps),
         [
             (rows * tiles * sheets + 1, sublanes, lanes),
             (piece, sublanes, lanes),
-            *made,
             (3, depth, lanes),
-            *iterates,
         ],
         diffusivity,
         velocity,
-        specs={0: hbm, 1: smem},
-        scratch=staging(diffusivity.shape),
+        specs={0: hbm, 1: hbm},
+        scratch=[
+            *staging(diffusivity.shape),
+            pltpu.SMEM(velocity.shape, jnp.float32),
+            pltpu.SemaphoreType.DMA,
+        ],
     )
     kappa_far = swap(own_far, 1)
-    near, far = halos(blocks, own, piece)
-    far, near = swap(far, 1), swap(near, 0)
-    state = [*made, *iterates, made[1]]
+    kappa, inverse, *margins = call(
+        functools.partial(prepare_kernel, "tm", rows, tiles, steps), [*made, *iterates], own
+    )
+    near, far = halos(blocks, own, kappa, piece)
+    far = swap(far, 1)
+    near = swap(near, 0)
+    state = [*made, *iterates]
     early = rows - reach
     solve = functools.partial(solve_kernel, "tm", "space", rows, tiles, steps)
     kept = [kappa, inverse, *margins]

time: 33.4 us -> 32.4 us (0.970)
  Pallas kernels: 7.13 us -> 5.13 us
  waiting for transfers between devices: 10.7 us -> 12.5 us
  local copies, waits for them, and re-layouts: 0.66 us -> 0 us
    pallas_call x6 -> x7, Pallas kernels: 7.13 us -> 5.13 us  [call(): pl.pallas_call(kernel, out_shape=[make(o, jnp.float32) for o in outs], in...]
    ppermute x3, waiting for transfers between devices: 3.63 us -> 4.85 us  [gather(): result[d] = lax.ppermute(blocks[d], 'tm', pairs)]
    unnamed x2 -> x0, local copies, waits for them, and re-layouts: 0.66 us -> none
    ppermute x3, waiting for transfers between devices: 2.89 us -> 3.43 us  [swap(): return lax.ppermute(value, names, pairs)]
  transfers between devices with their start and end apart: 11 -> 11, of which waited for: 5 -> 5; matrix products, arithmetic and copies ran while one was open for 0% -> 0% of each run, Pallas kernels for 10% -> 7%
where the time goes in v7:
time: 32.4 us; the launch traced here: 32.2 us
  starting transfers between devices  14.6 us (45%)
  waiting for transfers between devices  12.5 us (39%)
  Pallas kernels  5.13 us (16%)
    ppermute x5, starting transfers between devices, scatter(): result[d] = lax.ppermute(blocks[d], 'tm', pairs)  6.7 us
    ppermute x3, starting transfers between devices, gather(): result[d] = lax.ppermute(blocks[d], 'tm', pairs)  5.71 us
    pallas_call x7, Pallas kernels, call(): pl.pallas_call(kernel, out_shape=[make(o, jnp.float32) for o in outs], in...  5.13 us
    ppermute x3, waiting for transfers between devices, gather(): result[d] = lax.ppermute(blocks[d], 'tm', pairs)  4.85 us
    ppermute x5, waiting for transfers between devices, scatter(): result[d] = lax.ppermute(blocks[d], 'tm', pairs)  4.19 us
    ppermute x3, waiting for transfers between devices, swap(): return lax.ppermute(value, names, pairs)  3.43 us
    ppermute x3, starting transfers between devices, swap(): return lax.ppermute(value, names, pairs)  2.16 us
  transfers between devices with their start and end apart: 11, of which 5 were waited for; matrix products, arithmetic and copies ran while one was open for 0% of the time, Pallas kernels for 7%

profile of v7, /device:TPU:0, one launch (start us, length us, event | category | flops | bytes accessed | tf_op | source)
XLA Modules:
  0.0 32.2 jit_solution(7294438325510251205)
XLA Ops:
  0.0 1.2 %shard_map.37 = (f32[17,8,128]{2,1,0:T(8,128)S(1)}, f32[17,8,128]{2,1,0:T(8,128)S(1)}, f32[17,8,128]{2,1,0:T(8,128)S(1)}, f32[17,8,128]{2,1,0:T(8,128)S(1)}) custom-call(f32[16,4,1024]{2,1,0:T(4,128)} %bitcast.2), custom_call_target="tpu_custom_call" | custom-call | tf_op jit(solution)/shard_map/pallas_call | solution.py:39
  1.2 3.1 %collective-permute-start = (f32[17,8,128]{2,1,0:T(8,128)S(1)}, f32[17,8,128]{2,1,0:T(8,128)S(1)}, u32[]{:S(2)}, u32[]{:S(2)}) collective-permute-start(f32[17,8,128]{2,1,0:T(8,128)S(1)} %get-tuple-element.33), channel_id=1, source_target_pairs={{4,0},{0,4},{12,8},{8,12},{5,1},{1,5},{13,9},{9,13},{6,2},{2,6},{1... | collective-permute-start | bytes 208904 | tf_op jit(solution)/shard_map/ppermute | solution.py:490
  4.3 2.6 %collective-permute-start.1 = (f32[17,8,128]{2,1,0:T(8,128)S(1)}, f32[17,8,128]{2,1,0:T(8,128)S(1)}, u32[]{:S(2)}, u32[]{:S(2)}) collective-permute-start(f32[17,8,128]{2,1,0:T(8,128)S(1)} %get-tuple-element.34), channel_id=1, source_target_pairs={{8,0},{12,4},{0,8},{4,12},{9,1},{13,5},{1,9},{5,13},{10,2},{14,6},... | collective-permute-start | bytes 208904 | tf_op jit(solution)/shard_map/ppermute | solution.py:490
  6.9 0.0 collective-permute-start.2
  6.9 1.1 %shard_map.38 = (f32[17,8,128]{2,1,0:T(8,128)S(1)}, f32[13,8,128]{2,1,0:T(8,128)S(1)}, f32[3,16,128]{2,1,0:T(8,128)S(1)}) custom-call(f32[16,4,1024]{2,1,0:T(4,128)} %diffusivity.1, f32[3]{0:T(128)} %velocity.1), custom_call_target="tpu_custom_call" | custom-call | tf_op jit(solution)/shard_map/pallas_call | solution.py:39
  8.0 0.2 shard_map.39
  8.2 0.0 collective-permute-done.refs_1_
  8.3 3.6 %collective-permute-done.1.refs_2_ = f32[17,8,128]{2,1,0:T(8,128)S(1)} collective-permute-done((f32[17,8,128]{2,1,0:T(8,128)S(1)}, f32[17,8,128]{2,1,0:T(8,128)S(1)}, u32[]{:S(2)}, u32[]{:S(2)}) %collective-permute-start.1) | collective-permute-done | bytes 69664 | tf_op jit(solution)/shard_map/ppermute | solution.py:490
  11.8 1.3 %collective-permute-done.2.refs_3_ = f32[17,8,128]{2,1,0:T(8,128)S(1)} collective-permute-done((f32[17,8,128]{2,1,0:T(8,128)S(1)}, f32[17,8,128]{2,1,0:T(8,128)S(1)}, u32[]{:S(2)}, u32[]{:S(2)}) %collective-permute-start.2) | collective-permute-done | bytes 69664 | tf_op jit(solution)/shard_map/ppermute | solution.py:490
  13.1 0.1 collective-permute-start.3
  13.2 1.6 %collective-permute-start.6 = (f32[52,8,128]{2,1,0:T(8,128)S(1)}, f32[52,8,128]{2,1,0:T(8,128)S(1)}, u32[]{:S(2)}, u32[]{:S(2)}) collective-permute-start(f32[52,8,128]{2,1,0:T(8,128)S(1)} %get-tuple-element.47), channel_id=1, source_target_pairs={{0,16},{1,2},{2,1},{3,19},{4,20},{5,6},{6,5},{7,23},{8,24},{9,10},... | collective-permute-start | bytes 638984 | tf_op jit(solution)/shard_map/ppermute | solution.py:517
  14.8 0.5 %collective-permute-start.7 = (f32[13,8,128]{2,1,0:T(8,128)S(1)}, f32[13,8,128]{2,1,0:T(8,128)S(1)}, u32[]{:S(2)}, u32[]{:S(2)}) collective-permute-start(f32[13,8,128]{2,1,0:T(8,128)S(1)} %get-tuple-element.48), channel_id=1, source_target_pairs={{0,16},{1,2},{2,1},{3,19},{4,20},{5,6},{6,5},{7,23},{8,24},{9,10},... | collective-permute-start | bytes 159752 | tf_op jit(solution)/shard_map/ppermute | solution.py:517
  15.3 0.0 collective-permute-done.3.refs_4_
  15.3 1.0 %shard_map.41 = (f32[10,3,16,128]{3,2,1,0:T(8,128)S(1)}, f32[4,10,3,16,128]{4,3,2,1,0:T(8,128)S(1)}, f32[4,10,3,32,128]{4,3,2,1,0:T(8,128)S(1)}, f32[4,10,3,32,1...) custom-call(f32[17,8,128]{2,1,0:T(8,128)S(1)} %get-tuple-element.32., ...), custom_call_target="tpu_custom_call", output_to_operand_aliasing={{0}: (6, {}), {1}: (7, {}), {2}: (8, {}), {3}: (9, {}), {4}... | custom-call | tf_op jit(solution)/shard_map/pallas_call | solution.py:39
  16.3 3.4 %collective-permute-done.7.refs_1_ = f32[13,8,128]{2,1,0:T(8,128)S(1)} collective-permute-done((f32[13,8,128]{2,1,0:T(8,128)S(1)}, f32[13,8,128]{2,1,0:T(8,128)S(1)}, u32[]{:S(2)}, u32[]{:S(2)}) %collective-permute-start.7) | collective-permute-done | bytes 53280 | tf_op jit(solution)/shard_map/ppermute | solution.py:517
  19.7 0.0 collective-permute-done.6.refs_0_
  19.7 0.8 %shard_map.42 = (f32[10,3,16,128]{3,2,1,0:T(8,128)S(1)}, f32[4,10,3,16,128]{4,3,2,1,0:T(8,128)S(1)}, f32[4,10,3,32,128]{4,3,2,1,0:T(8,128)S(1)}, f32[4,10,3,32,1...) custom-call(f32[52,8,128]{2,1,0:T(8,128)S(1)} %collective-permute-do, ...), custom_call_target="tpu_custom_call", output_to_operand_aliasing={{0}: (3, {}), {1}: (4, {}), {2}: (5, {}), {3}: (6, {}), {4}... | custom-call | tf_op jit(solution)/shard_map/pallas_call | solution.py:39
  20.6 0.9 %collective-permute-start.8 = (f32[8,16,128]{2,1,0:T(8,128)S(1)}, f32[8,16,128]{2,1,0:T(8,128)S(1)}, u32[]{:S(2)}, u32[]{:S(2)}) collective-permute-start(f32[8,16,128]{2,1,0:T(8,128)S(1)} %get-tuple-element.56), channel_id=1, source_target_pairs={{0,4},{4,0},{8,12},{12,8},{1,5},{5,1},{9,13},{13,9},{2,6},{6,2},{1... | collective-permute-start | bytes 196616 | tf_op jit(solution)/shard_map/ppermute | solution.py:499
  21.4 1.7 %collective-permute-start.9 = (f32[6,16,128]{2,1,0:T(8,128)S(1)}, f32[6,16,128]{2,1,0:T(8,128)S(1)}, u32[]{:S(2)}, u32[]{:S(2)}) collective-permute-start(f32[6,16,128]{2,1,0:T(8,128)S(1)} %get-tuple-element.57), channel_id=1, source_target_pairs={{0,8},{4,12},{8,0},{12,4},{1,9},{5,13},{9,1},{13,5},{2,10},{6,14},... | collective-permute-start | bytes 147464 | tf_op jit(solution)/shard_map/ppermute | solution.py:499
  23.1 1.9 %collective-permute-start.10 = (f32[6,16,128]{2,1,0:T(8,128)S(1)}, f32[6,16,128]{2,1,0:T(8,128)S(1)}, u32[]{:S(2)}, u32[]{:S(2)}) collective-permute-start(f32[6,16,128]{2,1,0:T(8,128)S(1)} %get-tuple-element.58), channel_id=1, source_target_pairs={{0,12},{4,8},{8,4},{12,0},{1,13},{5,9},{9,5},{13,1},{2,14},{6,10},... | collective-permute-start | bytes 147464 | tf_op jit(solution)/shard_map/ppermute | solution.py:499
  25.0 0.9 %collective-permute-start.4 = (f32[2,16,128]{2,1,0:T(8,128)S(1)}, f32[2,16,128]{2,1,0:T(8,128)S(1)}, u32[]{:S(2)}, u32[]{:S(2)}) collective-permute-start(f32[2,16,128]{2,1,0:T(8,128)S(1)} %get-tuple-element.45), channel_id=1, source_target_pairs={{0,8},{4,12},{8,0},{12,4},{1,9},{5,13},{9,1},{13,5},{2,10},{6,14},... | collective-permute-start | bytes 49160 | tf_op jit(solution)/shard_map/ppermute | solution.py:499
  25.9 1.4 %collective-permute-start.5 = (f32[2,16,128]{2,1,0:T(8,128)S(1)}, f32[2,16,128]{2,1,0:T(8,128)S(1)}, u32[]{:S(2)}, u32[]{:S(2)}) collective-permute-start(f32[2,16,128]{2,1,0:T(8,128)S(1)} %get-tuple-element.46), channel_id=1, source_target_pairs={{0,12},{4,8},{8,4},{12,0},{1,13},{5,9},{9,5},{13,1},{2,14},{6,10},... | collective-permute-start | bytes 49160 | tf_op jit(solution)/shard_map/ppermute | solution.py:499
  27.3 3.1 %collective-permute-done.4.refs_1_ = f32[2,16,128]{2,1,0:T(8,128)S(1)} collective-permute-done((f32[2,16,128]{2,1,0:T(8,128)S(1)}, f32[2,16,128]{2,1,0:T(8,128)S(1)}, u32[]{:S(2)}, u32[]{:S(2)}) %collective-permute-start.4) | collective-permute-done | bytes 16416 | tf_op jit(solution)/shard_map/ppermute | solution.py:499
  30.4 1.1 %collective-permute-done.5.refs_2_ = f32[2,16,128]{2,1,0:T(8,128)S(1)} collective-permute-done((f32[2,16,128]{2,1,0:T(8,128)S(1)}, f32[2,16,128]{2,1,0:T(8,128)S(1)}, u32[]{:S(2)}, u32[]{:S(2)}) %collective-permute-start.5) | collective-permute-done | bytes 16416 | tf_op jit(solution)/shard_map/ppermute | solution.py:499
  31.4 0.0 collective-permute-done.9.refs_5_
  31.4 0.0 collective-permute-done.10.refs_6_
  31.4 0.0 collective-permute-done.8.refs_4_
  31.5 0.8 %shard_map.43 = f32[16,4,1024]{2,1,0:T(4,128)} custom-call(f32[2,16,128]{2,1,0:T(8,128)S(1)} %get-tuple-element.44.refs_0_, f32[2,16,128]{2,1,0:T(8,128)S(1)} %collective-permute-done.4.refs_1_, f32[2,16,128]{2,1,0:T(8,128)S(1)} %collective-permute-done.5.refs_2_, f32[6,16,128]{2,1,0:T(8,128)S(1)} %get-tuple-element.55.refs_3_, ...), custom_call_target="tpu_custom_call" | custom-call | tf_op jit(solution)/shard_map/pallas_call | solution.py:39
  (1 shorter events, 0.0 us)
Async XLA Ops:
  1.2 7.1 %collective-permute-start = (f32[17,8,128]{2,1,0:T(8,128)S(1)}, f32[17,8,128]{2,1,0:T(8,128)S(1)}, u32[]{:S(2)}, u32[]{:S(2)}) collective-permute-start(f32[17,8,128]{2,1,0:T(8,128)S(1)} %get-tuple-element.33), channel_id=1, source_target_pairs={{4,0},{0,4},{12,8},{8,12},{5,1},{1,5},{13,9},{9,13},{6,2},{2,6},{1... | collective-permute-start | bytes 208904 | tf_op jit(solution)/shard_map/ppermute | solution.py:490
  4.3 7.5 %collective-permute-start.1 = (f32[17,8,128]{2,1,0:T(8,128)S(1)}, f32[17,8,128]{2,1,0:T(8,128)S(1)}, u32[]{:S(2)}, u32[]{:S(2)}) collective-permute-start(f32[17,8,128]{2,1,0:T(8,128)S(1)} %get-tuple-element.34), channel_id=1, source_target_pairs={{8,0},{12,4},{0,8},{4,12},{9,1},{13,5},{1,9},{5,13},{10,2},{14,6},... | collective-permute-start | bytes 208904 | tf_op jit(solution)/shard_map/ppermute | solution.py:490
  6.9 6.2 %collective-permute-start.2 = (f32[17,8,128]{2,1,0:T(8,128)S(1)}, f32[17,8,128]{2,1,0:T(8,128)S(1)}, u32[]{:S(2)}, u32[]{:S(2)}) collective-permute-start(f32[17,8,128]{2,1,0:T(8,128)S(1)} %get-tuple-element.35), channel_id=1, source_target_pairs={{12,0},{8,4},{4,8},{0,12},{13,1},{9,5},{5,9},{1,13},{14,2},{10,6},... | collective-permute-start | bytes 208904 | tf_op jit(solution)/shard_map/ppermute | solution.py:490
  13.1 2.2 %collective-permute-start.3 = (f32[65,8,128]{2,1,0:T(8,128)S(1)}, f32[65,8,128]{2,1,0:T(8,128)S(1)}, u32[]{:S(2)}, u32[]{:S(2)}) collective-permute-start(f32[65,8,128]{2,1,0:T(8,128)S(1)} %get-tuple-element.38), channel_id=1, source_target_pairs={{0,1},{1,0},{2,3},{3,2},{4,5},{5,4},{6,7},{7,6},{8,9},{9,8},{10,11... | collective-permute-start | bytes 798728 | tf_op jit(solution)/shard_map/ppermute | solution.py:517
  13.2 6.5 %collective-permute-start.6 = (f32[52,8,128]{2,1,0:T(8,128)S(1)}, f32[52,8,128]{2,1,0:T(8,128)S(1)}, u32[]{:S(2)}, u32[]{:S(2)}) collective-permute-start(f32[52,8,128]{2,1,0:T(8,128)S(1)} %get-tuple-element.47), channel_id=1, source_target_pairs={{0,16},{1,2},{2,1},{3,19},{4,20},{5,6},{6,5},{7,23},{8,24},{9,10},... | collective-permute-start | bytes 638984 | tf_op jit(solution)/shard_map/ppermute | solution.py:517
  14.8 4.9 %collective-permute-start.7 = (f32[13,8,128]{2,1,0:T(8,128)S(1)}, f32[13,8,128]{2,1,0:T(8,128)S(1)}, u32[]{:S(2)}, u32[]{:S(2)}) collective-permute-start(f32[13,8,128]{2,1,0:T(8,128)S(1)} %get-tuple-element.48), channel_id=1, source_target_pairs={{0,16},{1,2},{2,1},{3,19},{4,20},{5,6},{6,5},{7,23},{8,24},{9,10},... | collective-permute-start | bytes 159752 | tf_op jit(solution)/shard_map/ppermute | solution.py:517
  20.6 10.9 %collective-permute-start.8 = (f32[8,16,128]{2,1,0:T(8,128)S(1)}, f32[8,16,128]{2,1,0:T(8,128)S(1)}, u32[]{:S(2)}, u32[]{:S(2)}) collective-permute-start(f32[8,16,128]{2,1,0:T(8,128)S(1)} %get-tuple-element.56), channel_id=1, source_target_pairs={{0,4},{4,0},{8,12},{12,8},{1,5},{5,1},{9,13},{13,9},{2,6},{6,2},{1... | collective-permute-start | bytes 196616 | tf_op jit(solution)/shard_map/ppermute | solution.py:499
  21.4 10.0 %collective-permute-start.9 = (f32[6,16,128]{2,1,0:T(8,128)S(1)}, f32[6,16,128]{2,1,0:T(8,128)S(1)}, u32[]{:S(2)}, u32[]{:S(2)}) collective-permute-start(f32[6,16,128]{2,1,0:T(8,128)S(1)} %get-tuple-element.57), channel_id=1, source_target_pairs={{0,8},{4,12},{8,0},{12,4},{1,9},{5,13},{9,1},{13,5},{2,10},{6,14},... | collective-permute-start | bytes 147464 | tf_op jit(solution)/shard_map/ppermute | solution.py:499
  23.1 8.3 %collective-permute-start.10 = (f32[6,16,128]{2,1,0:T(8,128)S(1)}, f32[6,16,128]{2,1,0:T(8,128)S(1)}, u32[]{:S(2)}, u32[]{:S(2)}) collective-permute-start(f32[6,16,128]{2,1,0:T(8,128)S(1)} %get-tuple-element.58), channel_id=1, source_target_pairs={{0,12},{4,8},{8,4},{12,0},{1,13},{5,9},{9,5},{13,1},{2,14},{6,10},... | collective-permute-start | bytes 147464 | tf_op jit(solution)/shard_map/ppermute | solution.py:499
  25.0 5.4 %collective-permute-start.4 = (f32[2,16,128]{2,1,0:T(8,128)S(1)}, f32[2,16,128]{2,1,0:T(8,128)S(1)}, u32[]{:S(2)}, u32[]{:S(2)}) collective-permute-start(f32[2,16,128]{2,1,0:T(8,128)S(1)} %get-tuple-element.45), channel_id=1, source_target_pairs={{0,8},{4,12},{8,0},{12,4},{1,9},{5,13},{9,1},{13,5},{2,10},{6,14},... | collective-permute-start | bytes 49160 | tf_op jit(solution)/shard_map/ppermute | solution.py:499
  25.9 5.5 %collective-permute-start.5 = (f32[2,16,128]{2,1,0:T(8,128)S(1)}, f32[2,16,128]{2,1,0:T(8,128)S(1)}, u32[]{:S(2)}, u32[]{:S(2)}) collective-permute-start(f32[2,16,128]{2,1,0:T(8,128)S(1)} %get-tuple-element.46), channel_id=1, source_target_pairs={{0,12},{4,8},{8,4},{12,0},{1,13},{5,9},{9,5},{13,1},{2,14},{6,10},... | collective-permute-start | bytes 49160 | tf_op jit(solution)/shard_map/ppermute | solution.py:499

commit v8 on v7

--- a/solution.py
+++ b/solution.py
@@ -21,7 +21,6 @@
 reach = len(relax_weights) - 1
 lanes = 128
 sublanes = 8
-early_moves = (2, 3)
 vmem = pl.BlockSpec(memory_space=pltpu.VMEM)
 smem = pl.BlockSpec(memory_space=pltpu.SMEM)
 hbm = pl.BlockSpec(memory_space=pltpu.HBM)
@@ -74,6 +73,14 @@
     forwards = 1 - 2 * lax.rem(me, 2) if steps % 2 == 0 else 1
     turn = forwards * slot if steps % 2 == 0 and slot % 2 else -forwards * slot
     return lax.rem(me + turn + steps, steps)
+
+
+def finished_place(slot, count):
+    return (slot, 0) if slot < 3 else (2, count) if slot == 3 else (slot - 1, 0)
+
+
+def in_one(slot):
+    return slot == 1 or slot > 3
 
 
 def put(block, index, value):
@@ -170,12 +177,12 @@
     blocks, (near, far) = refs[:-3], refs[-2:]
     for step, block in enumerate(blocks):
         copy_piece(block, True, piece, near, step * piece)
-        if (step + 1) * piece <= far.shape[0]:
-            copy_piece(block, False, piece, far, step * piece)
+        if 0 < step < len(blocks) - 1:
+            copy_piece(block, False, piece, far, (step - 1) * piece)
 
 
 def halos(blocks, own, ready, piece):
-    outs = [(count * piece, sublanes, lanes) for count in (len(blocks) + 1, len(blocks))]
+    outs = [(count * piece, sublanes, lanes) for count in (len(blocks) + 1, len(blocks) - 1)]
     return call(functools.partial(halo_kernel, piece), outs, *blocks, own, ready)
 
 
@@ -233,7 +240,7 @@
     return keep_right + keep_left
 
 
-def kappa_kernel(tm, space, steps, diffusivity, velocity, *refs):
+def kappa_kernel(tm, space, steps, diffusivity, velocity, block, *refs):
     own, own_far, drift, held, semaphores, turned, speeds, semaphore = refs
     up = upwards(space)
     copy = pltpu.make_async_copy(velocity, speeds, semaphore)
@@ -242,7 +249,9 @@
 
     turn(held, turned)
     pick_block(turned, diffusivity.shape[1], own, lax.axis_index(tm), steps, up)
-    copy_piece(own, False, own_far.shape[0], own_far, 0)
+    piece = own_far.shape[0] // 2
+    copy_piece(own, False, piece, own_far, 0)
+    copy_piece(block, False, piece, own_far, piece)
     copy.wait()
     direction = (2 * up - 1).astype(jnp.float32)
     for j in range(3):
@@ -303,7 +312,7 @@
     made = 2 + levels
     if second_half:
         far, kappa_far, drift = refs[:3]
-        done = sum(ahead not in early_moves for ahead in range(1, steps))
+        done = sum(in_one(ahead) for ahead in range(steps))
         finished, refs = refs[3 + made : 3 + made + done], refs[3 + made + done :]
         kappa, inverse, *iterates = refs[:made]
         outs = refs[made:]
@@ -358,7 +367,17 @@
             if tile == tiles and not 1 <= row < extended - 1:
                 continue
             held = [
-                row_piece(blocks[b], near, far, b, row, tile, rows, tiles, depth)
+                row_piece(
+                    blocks[b],
+                    near,
+                    far if b else kappa_far,
+                    (b - 1 if b else 1) if second_half else b,
+                    row,
+                    tile,
+                    rows,
+                    tiles,
+                    depth,
+                )
                 for b in range(steps)
             ]
             values = []
@@ -419,12 +438,15 @@
                     iterates[level][field, row, tile, middle, :] = results[field]
 
     last_rows = rows_of(levels)
-    skipped = [0] * steps
+    early = (rows - reach) * tiles
+    places = [(ahead, 0) for ahead in range(steps)]
     if second_half:
-        whole = [ahead for ahead in range(1, steps) if ahead not in early_moves]
+        whole = [ahead for ahead in range(steps) if in_one(ahead)]
         for ahead, block in zip(whole, finished, strict=True):
-            skipped[ahead] = (rows - reach) * tiles
-            outs[ahead][pl.ds(0, block.shape[0])] = block[...]
+            places[ahead] = (ahead, early)
+            outs[ahead][pl.ds(0, early)] = block[...]
+    else:
+        places = [finished_place(ahead, early) for ahead in range(steps)]
 
     for row in range(*last_rows):
         for tile, results in sweep(row, levels):
@@ -437,13 +459,18 @@
                     if is_complex:
                         terms.append((-factor * sine(k * ahead, steps), results[field]))
                         field += 1
-                place = (row - last_rows[0]) * tiles + tile + skipped[ahead]
-                outs[ahead][place] = combine(terms)
-
-
-def unpack_kernel(tm, space, log_alpha, steps, early, *refs):
-    refs = list(refs)
-    heads = [refs.pop(0) if two else None for two in early]
+                which, start = places[ahead]
+                outs[which][start + (row - last_rows[0]) * tiles + tile] = combine(terms)
+
+
+def join_kernel(block, early, joined):
+    count = block.shape[0]
+    joined[pl.ds(0, count)] = block[...]
+    handed = joined.shape[0] - count
+    joined[pl.ds(count, handed)] = early[pl.ds(handed, handed)]
+
+
+def unpack_kernel(tm, space, log_alpha, steps, own_early, early, *refs):
     tails, (out, held, semaphores) = refs[:steps], refs[steps:]
     me, up = lax.axis_index(tm), upwards(space)
     depth, rows, columns = out.shape
@@ -455,11 +482,13 @@
     rising = up == 1
 
     def at_row(behind, row, tile):
-        if heads[behind] is None:
+        if in_one(behind):
             return tails[behind][row * tiles + tile]
-        if row < first:
-            return heads[behind][row * tiles + tile]
-        return tails[behind][(row - first) * tiles + tile]
+        if row >= first:
+            return tails[behind][(row - first) * tiles + tile]
+        if behind == 3:
+            return tails[1][(rows + row) * tiles + tile]
+        return (early if behind else own_early)[row * tiles + tile]
 
     copies = []
     for behind in range(steps):
@@ -491,13 +520,8 @@
     return result
 
 
-def scatter(blocks, steps):
-    result = list(blocks)
-    for d in reversed(range(1, steps)):
-        if blocks[d] is not None:
-            pairs = [(t, slot_time(t, d, steps)) for t in range(steps)]
-            result[d] = lax.ppermute(blocks[d], "tm", pairs)
-    return result
+def scatter(block, d, steps):
+    return lax.ppermute(block, "tm", [(t, slot_time(t, d, steps)) for t in range(steps)])
 
 
 def swap(value, first):
@@ -533,11 +557,12 @@
         functools.partial(kappa_kernel, "tm", "space", steps),
         [
             (rows * tiles * sheets + 1, sublanes, lanes),
-            (piece, sublanes, lanes),
+            (2 * piece, sublanes, lanes),
             (3, depth, lanes),
         ],
         diffusivity,
         velocity,
+        blocks[0],
         specs={0: hbm, 1: hbm},
         scratch=[
             *staging(diffusivity.shape),
@@ -553,12 +578,13 @@
     far = swap(far, 1)
     near = swap(near, 0)
     state = [*made, *iterates]
-    early = rows - reach
+    early = (rows - reach) * tiles
     solve = functools.partial(solve_kernel, "tm", "space", rows, tiles, steps)
     kept = [kappa, inverse, *margins]
+    counts = [early, early, 2 * early] + [early] * (steps - 4)
     held = call(
         functools.partial(solve, False),
-        state + [(early * tiles, depth, lanes)] * steps,
+        state + [(n, depth, lanes) for n in counts],
         *blocks,
         near,
         drift,
@@ -566,24 +592,27 @@
         aliases={steps + 2 + i: i for i in range(len(kept))},
     )
     state_now, finished = held[: len(state)], held[len(state) :]
-    in_two = [d == 0 or d in early_moves for d in range(steps)]
-    heads = scatter([finished[d] if in_two[d] else None for d in range(steps)], steps)
-    heads = [head for head in heads if head is not None]
+    moved = scatter(finished[2], 2, steps)
     held = call(
         functools.partial(solve, True),
-        state + [((reach if two else rows) * tiles, depth, lanes) for two in in_two],
+        state
+        + [((rows if in_one(d) else reach) * tiles, depth, lanes) for d in range(steps)],
         far,
         kappa_far,
         drift,
         *state_now,
-        *(finished[d] for d in range(steps) if not in_two[d]),
+        *(finished[finished_place(d, early)[0]] for d in range(steps) if in_one(d)),
         aliases={3 + i: i for i in range(len(state))},
     )
-    tails = scatter(held[len(state) :], steps)
+    tails = list(held[len(state) :])
+    (tails[1],) = call(join_kernel, [(rows * tiles + early, depth, lanes)], tails[1], moved)
+    for d in reversed(range(1, steps)):
+        tails[d] = scatter(tails[d], d, steps)
     (result,) = call(
-        functools.partial(unpack_kernel, "tm", "space", log_alpha, steps, tuple(in_two)),
+        functools.partial(unpack_kernel, "tm", "space", log_alpha, steps),
         [(depth, rows, columns)],
-        *heads,
+        finished[0],
+        moved,
         *tails,
         kept=False,
         scratch=[
@@ -707,7 +736,8 @@
     local_steps, depth, rows, columns = rhs.shape
     slots = rows * (depth // sublanes)
     tiled = columns % (steps * lanes) == 0 and depth % sublanes == 0
-    if local_steps == 1 and rows >= reach and tiled and 2 * reach * slots <= lanes:
+    paired = steps % 2 == 0 and steps >= 4
+    if local_steps == 1 and rows > reach and tiled and paired and 2 * reach * slots <= lanes:
         return fast_local(rhs, diffusivity, velocity)
     return general_local(rhs, diffusivity, velocity)
 

time: 32.4 us -> 30.8 us (0.951)
  waiting for transfers between devices: 12.5 us -> 11.3 us
  starting transfers between devices: 14.6 us -> 14.1 us
    ppermute x3, waiting for transfers between devices: 3.43 us -> 1.56 us  [swap(): return lax.ppermute(value, names, pairs)]
    ppermute x5 -> x4, waiting for transfers between devices: 4.19 us -> 4.9 us  [scatter(): lax.ppermute(block, 'tm', [(t, slot_time(t, d, steps)) for t in range(ste...]
    ppermute x5 -> x4, starting transfers between devices: 6.7 us -> 6.25 us  [scatter(): lax.ppermute(block, 'tm', [(t, slot_time(t, d, steps)) for t in range(ste...]
    pallas_call x7 -> x8, Pallas kernels: 5.13 us -> 5.12 us  [call(): pl.pallas_call(kernel, out_shape=[make(o, jnp.float32) for o in outs], in...]
  transfers between devices with their start and end apart: 11 -> 10, of which waited for: 5 -> 6; matrix products, arithmetic and copies ran while one was open for 0% -> 0% of each run, Pallas kernels for 7% -> 10%
where the time goes in v8:
time: 30.8 us; the launch traced here: 30.6 us
  starting transfers between devices  14.1 us (46%)
  waiting for transfers between devices  11.3 us (37%)
  Pallas kernels  5.12 us (17%)
    ppermute x4, starting transfers between devices, scatter(): lax.ppermute(block, 'tm', [(t, slot_time(t, d, steps)) for t in range(ste...  6.25 us
    ppermute x3, starting transfers between devices, gather(): result[d] = lax.ppermute(blocks[d], 'tm', pairs)  5.71 us
    pallas_call x8, Pallas kernels, call(): pl.pallas_call(kernel, out_shape=[make(o, jnp.float32) for o in outs], in...  5.12 us
    ppermute x4, waiting for transfers between devices, scatter(): lax.ppermute(block, 'tm', [(t, slot_time(t, d, steps)) for t in range(ste...  4.9 us
    ppermute x3, waiting for transfers between devices, gather(): result[d] = lax.ppermute(blocks[d], 'tm', pairs)  4.84 us
    ppermute x3, starting transfers between devices, swap(): return lax.ppermute(value, names, pairs)  2.16 us
    ppermute x3, waiting for transfers between devices, swap(): return lax.ppermute(value, names, pairs)  1.56 us
  transfers between devices with their start and end apart: 10, of which 6 were waited for; matrix products, arithmetic and copies ran while one was open for 0% of the time, Pallas kernels for 10%

profile of v8, /device:TPU:0, one launch (start us, length us, event | category | flops | bytes accessed | tf_op | source)
XLA Modules:
  0.0 30.6 jit_solution(3221490351467813160)
XLA Ops:
  0.0 1.2 %shard_map.37 = (f32[17,8,128]{2,1,0:T(8,128)S(1)}, f32[17,8,128]{2,1,0:T(8,128)S(1)}, f32[17,8,128]{2,1,0:T(8,128)S(1)}, f32[17,8,128]{2,1,0:T(8,128)S(1)}) custom-call(f32[16,4,1024]{2,1,0:T(4,128)} %bitcast.2), custom_call_target="tpu_custom_call" | custom-call | tf_op jit(solution)/shard_map/pallas_call | solution.py:38
  1.2 3.1 %collective-permute-start = (f32[17,8,128]{2,1,0:T(8,128)S(1)}, f32[17,8,128]{2,1,0:T(8,128)S(1)}, u32[]{:S(2)}, u32[]{:S(2)}) collective-permute-start(f32[17,8,128]{2,1,0:T(8,128)S(1)} %get-tuple-element.32), channel_id=1, source_target_pairs={{4,0},{0,4},{12,8},{8,12},{5,1},{1,5},{13,9},{9,13},{6,2},{2,6},{1... | collective-permute-start | bytes 208904 | tf_op jit(solution)/shard_map/ppermute | solution.py:519
  4.3 2.6 %collective-permute-start.1 = (f32[17,8,128]{2,1,0:T(8,128)S(1)}, f32[17,8,128]{2,1,0:T(8,128)S(1)}, u32[]{:S(2)}, u32[]{:S(2)}) collective-permute-start(f32[17,8,128]{2,1,0:T(8,128)S(1)} %get-tuple-element.33), channel_id=1, source_target_pairs={{8,0},{12,4},{0,8},{4,12},{9,1},{13,5},{1,9},{5,13},{10,2},{14,6},... | collective-permute-start | bytes 208904 | tf_op jit(solution)/shard_map/ppermute | solution.py:519
  6.9 0.0 collective-permute-start.2
  6.9 1.1 %shard_map.38 = (f32[17,8,128]{2,1,0:T(8,128)S(1)}, f32[26,8,128]{2,1,0:T(8,128)S(1)}, f32[3,16,128]{2,1,0:T(8,128)S(1)}) custom-call(f32[16,4,1024]{2,1,0:T(4,128)} %diffusivity.1, f32[3]{0:T(128)} %velocity.1, f32[17,8,128]{2,1,0:T(8,128)S(1)} %get-tuple-element.31.block.refs_0_), custom_call_target="tpu_custom_call" | custom-call | tf_op jit(solution)/shard_map/pallas_call | solution.py:38
  8.0 0.2 shard_map.39
  8.2 0.0 collective-permute-done.refs_1_
  8.3 3.6 %collective-permute-done.1.refs_2_ = f32[17,8,128]{2,1,0:T(8,128)S(1)} collective-permute-done((f32[17,8,128]{2,1,0:T(8,128)S(1)}, f32[17,8,128]{2,1,0:T(8,128)S(1)}, u32[]{:S(2)}, u32[]{:S(2)}) %collective-permute-start.1) | collective-permute-done | bytes 69664 | tf_op jit(solution)/shard_map/ppermute | solution.py:519
  11.8 1.3 %collective-permute-done.2.refs_3_ = f32[17,8,128]{2,1,0:T(8,128)S(1)} collective-permute-done((f32[17,8,128]{2,1,0:T(8,128)S(1)}, f32[17,8,128]{2,1,0:T(8,128)S(1)}, u32[]{:S(2)}, u32[]{:S(2)}) %collective-permute-start.2) | collective-permute-done | bytes 69664 | tf_op jit(solution)/shard_map/ppermute | solution.py:519
  13.1 0.1 collective-permute-start.3
  13.2 1.6 %collective-permute-start.5 = (f32[39,8,128]{2,1,0:T(8,128)S(1)}, f32[39,8,128]{2,1,0:T(8,128)S(1)}, u32[]{:S(2)}, u32[]{:S(2)}) collective-permute-start(f32[39,8,128]{2,1,0:T(8,128)S(1)} %get-tuple-element.45), channel_id=1, source_target_pairs={{0,16},{1,2},{2,1},{3,19},{4,20},{5,6},{6,5},{7,23},{8,24},{9,10},... | collective-permute-start | bytes 479240 | tf_op jit(solution)/shard_map/ppermute | solution.py:541
  14.8 0.5 %collective-permute-start.6 = (f32[26,8,128]{2,1,0:T(8,128)S(1)}, f32[26,8,128]{2,1,0:T(8,128)S(1)}, u32[]{:S(2)}, u32[]{:S(2)}) collective-permute-start(f32[26,8,128]{2,1,0:T(8,128)S(1)} %get-tuple-element.46), channel_id=1, source_target_pairs={{0,16},{1,2},{2,1},{3,19},{4,20},{5,6},{6,5},{7,23},{8,24},{9,10},... | collective-permute-start | bytes 319496 | tf_op jit(solution)/shard_map/ppermute | solution.py:541
  15.3 0.0 collective-permute-done.3.refs_4_
  15.3 1.0 %shard_map.41 = (f32[10,3,16,128]{3,2,1,0:T(8,128)S(1)}, f32[4,10,3,16,128]{4,3,2,1,0:T(8,128)S(1)}, f32[4,10,3,32,128]{4,3,2,1,0:T(8,128)S(1)}, f32[4,10,3,32,1...) custom-call(f32[17,8,128]{2,1,0:T(8,128)S(1)} %get-tuple-element.31., ...), custom_call_target="tpu_custom_call", output_to_operand_aliasing={{0}: (6, {}), {1}: (7, {}), {2}: (8, {}), {3}: (9, {}), {4}... | custom-call | tf_op jit(solution)/shard_map/pallas_call | solution.py:38
  16.3 1.9 %collective-permute-start.4 = (f32[4,16,128]{2,1,0:T(8,128)S(1)}, f32[4,16,128]{2,1,0:T(8,128)S(1)}, u32[]{:S(2)}, u32[]{:S(2)}) collective-permute-start(f32[4,16,128]{2,1,0:T(8,128)S(1)} %get-tuple-element.44), channel_id=1, source_target_pairs={{0,8},{4,12},{8,0},{12,4},{1,9},{5,13},{9,1},{13,5},{2,10},{6,14},... | collective-permute-start | bytes 98312 | tf_op jit(solution)/shard_map/ppermute | solution.py:524
  18.1 1.6 %collective-permute-done.6.refs_1_ = f32[26,8,128]{2,1,0:T(8,128)S(1)} collective-permute-done((f32[26,8,128]{2,1,0:T(8,128)S(1)}, f32[26,8,128]{2,1,0:T(8,128)S(1)}, u32[]{:S(2)}, u32[]{:S(2)}) %collective-permute-start.6) | collective-permute-done | bytes 106528 | tf_op jit(solution)/shard_map/ppermute | solution.py:541
  19.7 0.0 collective-permute-done.5.refs_0_
  19.7 0.8 %shard_map.42 = (f32[10,3,16,128]{3,2,1,0:T(8,128)S(1)}, f32[4,10,3,16,128]{4,3,2,1,0:T(8,128)S(1)}, f32[4,10,3,32,128]{4,3,2,1,0:T(8,128)S(1)}, f32[4,10,3,32,1...) custom-call(f32[39,8,128]{2,1,0:T(8,128)S(1)} %collective-permute-do, ...), custom_call_target="tpu_custom_call", output_to_operand_aliasing={{0}: (3, {}), {1}: (4, {}), {2}: (5, {}), {3}: (6, {}), {4}... | custom-call | tf_op jit(solution)/shard_map/pallas_call | solution.py:38
  20.5 1.0 %collective-permute-done.4.early = f32[4,16,128]{2,1,0:T(8,128)S(1)} collective-permute-done((f32[4,16,128]{2,1,0:T(8,128)S(1)}, f32[4,16,128]{2,1,0:T(8,128)S(1)}, u32[]{:S(2)}, u32[]{:S(2)}) %collective-permute-start.4) | collective-permute-done | bytes 32800 | tf_op jit(solution)/shard_map/ppermute | solution.py:524
  21.5 0.4 %collective-permute-start.7 = (f32[10,16,128]{2,1,0:T(8,128)S(1)}, f32[10,16,128]{2,1,0:T(8,128)S(1)}, u32[]{:S(2)}, u32[]{:S(2)}) collective-permute-start(f32[10,16,128]{2,1,0:T(8,128)S(1)} %shard_map.43), channel_id=1, source_target_pairs={{0,4},{4,0},{8,12},{12,8},{1,5},{5,1},{9,13},{13,9},{2,6},{6,2},{1... | collective-permute-start | bytes 245768 | tf_op jit(solution)/shard_map/ppermute | solution.py:524
  21.9 2.0 %collective-permute-start.8 = (f32[6,16,128]{2,1,0:T(8,128)S(1)}, f32[6,16,128]{2,1,0:T(8,128)S(1)}, u32[]{:S(2)}, u32[]{:S(2)}) collective-permute-start(f32[6,16,128]{2,1,0:T(8,128)S(1)} %get-tuple-element.55), channel_id=1, source_target_pairs={{0,8},{4,12},{8,0},{12,4},{1,9},{5,13},{9,1},{13,5},{2,10},{6,14},... | collective-permute-start | bytes 147464 | tf_op jit(solution)/shard_map/ppermute | solution.py:524
  24.0 1.9 %collective-permute-start.9 = (f32[6,16,128]{2,1,0:T(8,128)S(1)}, f32[6,16,128]{2,1,0:T(8,128)S(1)}, u32[]{:S(2)}, u32[]{:S(2)}) collective-permute-start(f32[6,16,128]{2,1,0:T(8,128)S(1)} %get-tuple-element.56), channel_id=1, source_target_pairs={{0,12},{4,8},{8,4},{12,0},{1,13},{5,9},{9,5},{13,1},{2,14},{6,10},... | collective-permute-start | bytes 147464 | tf_op jit(solution)/shard_map/ppermute | solution.py:524
  25.9 1.2 %collective-permute-done.8.refs_2_ = f32[6,16,128]{2,1,0:T(8,128)S(1)} collective-permute-done((f32[6,16,128]{2,1,0:T(8,128)S(1)}, f32[6,16,128]{2,1,0:T(8,128)S(1)}, u32[]{:S(2)}, u32[]{:S(2)}) %collective-permute-start.8) | collective-permute-done | bytes 49184 | tf_op jit(solution)/shard_map/ppermute | solution.py:524
  27.1 2.7 %collective-permute-done.9.refs_3_ = f32[6,16,128]{2,1,0:T(8,128)S(1)} collective-permute-done((f32[6,16,128]{2,1,0:T(8,128)S(1)}, f32[6,16,128]{2,1,0:T(8,128)S(1)}, u32[]{:S(2)}, u32[]{:S(2)}) %collective-permute-start.9) | collective-permute-done | bytes 49184 | tf_op jit(solution)/shard_map/ppermute | solution.py:524
  29.8 0.0 collective-permute-done.7.refs_1_
  29.8 0.8 %shard_map.44 = f32[16,4,1024]{2,1,0:T(4,128)} custom-call(f32[2,16,128]{2,1,0:T(8,128)S(1)} %get-tuple-element.43.own_early, f32[4,16,128]{2,1,0:T(8,128)S(1)} %collective-permute-done.4.early, f32[6,16,128]{2,1,0:T(8,128)S(1)} %get-tuple-element.53.refs_0_, f32[10,16,128]{2,1,0:T(8,128)S(1)} %collective-permute-done.7.refs_1_, ...), custom_call_target="tpu_custom_call" | custom-call | tf_op jit(solution)/shard_map/pallas_call | solution.py:38
  (2 shorter events, 0.0 us)
Async XLA Ops:
  1.2 7.1 %collective-permute-start = (f32[17,8,128]{2,1,0:T(8,128)S(1)}, f32[17,8,128]{2,1,0:T(8,128)S(1)}, u32[]{:S(2)}, u32[]{:S(2)}) collective-permute-start(f32[17,8,128]{2,1,0:T(8,128)S(1)} %get-tuple-element.32), channel_id=1, source_target_pairs={{4,0},{0,4},{12,8},{8,12},{5,1},{1,5},{13,9},{9,13},{6,2},{2,6},{1... | collective-permute-start | bytes 208904 | tf_op jit(solution)/shard_map/ppermute | solution.py:519
  4.3 7.5 %collective-permute-start.1 = (f32[17,8,128]{2,1,0:T(8,128)S(1)}, f32[17,8,128]{2,1,0:T(8,128)S(1)}, u32[]{:S(2)}, u32[]{:S(2)}) collective-permute-start(f32[17,8,128]{2,1,0:T(8,128)S(1)} %get-tuple-element.33), channel_id=1, source_target_pairs={{8,0},{12,4},{0,8},{4,12},{9,1},{13,5},{1,9},{5,13},{10,2},{14,6},... | collective-permute-start | bytes 208904 | tf_op jit(solution)/shard_map/ppermute | solution.py:519
  6.9 6.2 %collective-permute-start.2 = (f32[17,8,128]{2,1,0:T(8,128)S(1)}, f32[17,8,128]{2,1,0:T(8,128)S(1)}, u32[]{:S(2)}, u32[]{:S(2)}) collective-permute-start(f32[17,8,128]{2,1,0:T(8,128)S(1)} %get-tuple-element.34), channel_id=1, source_target_pairs={{12,0},{8,4},{4,8},{0,12},{13,1},{9,5},{5,9},{1,13},{14,2},{10,6},... | collective-permute-start | bytes 208904 | tf_op jit(solution)/shard_map/ppermute | solution.py:519
  13.1 2.2 %collective-permute-start.3 = (f32[65,8,128]{2,1,0:T(8,128)S(1)}, f32[65,8,128]{2,1,0:T(8,128)S(1)}, u32[]{:S(2)}, u32[]{:S(2)}) collective-permute-start(f32[65,8,128]{2,1,0:T(8,128)S(1)} %get-tuple-element.37), channel_id=1, source_target_pairs={{0,1},{1,0},{2,3},{3,2},{4,5},{5,4},{6,7},{7,6},{8,9},{9,8},{10,11... | collective-permute-start | bytes 798728 | tf_op jit(solution)/shard_map/ppermute | solution.py:541
  13.2 6.5 %collective-permute-start.5 = (f32[39,8,128]{2,1,0:T(8,128)S(1)}, f32[39,8,128]{2,1,0:T(8,128)S(1)}, u32[]{:S(2)}, u32[]{:S(2)}) collective-permute-start(f32[39,8,128]{2,1,0:T(8,128)S(1)} %get-tuple-element.45), channel_id=1, source_target_pairs={{0,16},{1,2},{2,1},{3,19},{4,20},{5,6},{6,5},{7,23},{8,24},{9,10},... | collective-permute-start | bytes 479240 | tf_op jit(solution)/shard_map/ppermute | solution.py:541
  14.8 4.9 %collective-permute-start.6 = (f32[26,8,128]{2,1,0:T(8,128)S(1)}, f32[26,8,128]{2,1,0:T(8,128)S(1)}, u32[]{:S(2)}, u32[]{:S(2)}) collective-permute-start(f32[26,8,128]{2,1,0:T(8,128)S(1)} %get-tuple-element.46), channel_id=1, source_target_pairs={{0,16},{1,2},{2,1},{3,19},{4,20},{5,6},{6,5},{7,23},{8,24},{9,10},... | collective-permute-start | bytes 319496 | tf_op jit(solution)/shard_map/ppermute | solution.py:541
  16.3 5.2 %collective-permute-start.4 = (f32[4,16,128]{2,1,0:T(8,128)S(1)}, f32[4,16,128]{2,1,0:T(8,128)S(1)}, u32[]{:S(2)}, u32[]{:S(2)}) collective-permute-start(f32[4,16,128]{2,1,0:T(8,128)S(1)} %get-tuple-element.44), channel_id=1, source_target_pairs={{0,8},{4,12},{8,0},{12,4},{1,9},{5,13},{9,1},{13,5},{2,10},{6,14},... | collective-permute-start | bytes 98312 | tf_op jit(solution)/shard_map/ppermute | solution.py:524
  21.5 8.3 %collective-permute-start.7 = (f32[10,16,128]{2,1,0:T(8,128)S(1)}, f32[10,16,128]{2,1,0:T(8,128)S(1)}, u32[]{:S(2)}, u32[]{:S(2)}) collective-permute-start(f32[10,16,128]{2,1,0:T(8,128)S(1)} %shard_map.43), channel_id=1, source_target_pairs={{0,4},{4,0},{8,12},{12,8},{1,5},{5,1},{9,13},{13,9},{2,6},{6,2},{1... | collective-permute-start | bytes 245768 | tf_op jit(solution)/shard_map/ppermute | solution.py:524
  21.9 5.2 %collective-permute-start.8 = (f32[6,16,128]{2,1,0:T(8,128)S(1)}, f32[6,16,128]{2,1,0:T(8,128)S(1)}, u32[]{:S(2)}, u32[]{:S(2)}) collective-permute-start(f32[6,16,128]{2,1,0:T(8,128)S(1)} %get-tuple-element.55), channel_id=1, source_target_pairs={{0,8},{4,12},{8,0},{12,4},{1,9},{5,13},{9,1},{13,5},{2,10},{6,14},... | collective-permute-start | bytes 147464 | tf_op jit(solution)/shard_map/ppermute | solution.py:524
  24.0 5.9 %collective-permute-start.9 = (f32[6,16,128]{2,1,0:T(8,128)S(1)}, f32[6,16,128]{2,1,0:T(8,128)S(1)}, u32[]{:S(2)}, u32[]{:S(2)}) collective-permute-start(f32[6,16,128]{2,1,0:T(8,128)S(1)} %get-tuple-element.56), channel_id=1, source_target_pairs={{0,12},{4,8},{8,4},{12,0},{1,13},{5,9},{9,5},{13,1},{2,14},{6,10},... | collective-permute-start | bytes 147464 | tf_op jit(solution)/shard_map/ppermute | solution.py:524

commit v9 on v8

--- a/solution.py
+++ b/solution.py
@@ -396,23 +396,25 @@
         scale, weight = relax_weights[level - 1], relax_weights[level]
         keep = (1.0 - weight) * scale / weight + (1.0 if level == 1 else 0.0)
         tilt = [scale * h for h in half]
-        centers = [
-            [old[field, row, tile, middle, :] for tile in range(wide)] for field in range(fields)
-        ]
-        shifted_down = [[pltpu.roll(c, 1, 1) for c in line] for line in centers]
-        shifted_up = [[pltpu.roll(c, lanes - 1, 1) for c in line] for line in centers]
+        rolled = {}
+
+        def around(field, tile):
+            if (field, tile) not in rolled:
+                center = old[field, row, tile, middle, :]
+                rolled[field, tile] = (
+                    center, pltpu.roll(center, 1, 1), pltpu.roll(center, lanes - 1, 1)
+                )
+            return rolled[field, tile]
+
         for tile in range(wide if with_halo else tiles):
             values = []
             scaled = scale * kappa[row, tile]
             below = [scaled + t for t in tilt]
             above = [scaled - t for t in tilt]
             for field in range(fields):
-                lower_x = jnp.where(
-                    at_first, shifted_down[field][(tile - 1) % wide], shifted_down[field][tile]
-                )
-                upper_x = jnp.where(
-                    at_last, shifted_up[field][(tile + 1) % wide], shifted_up[field][tile]
-                )
+                _, down, up = around(field, tile)
+                lower_x = jnp.where(at_first, around(field, (tile - 1) % wide)[1], down)
+                upper_x = jnp.where(at_last, around(field, (tile + 1) % wide)[2], up)
                 lower_z = old[field, row, tile, pl.ds(pad - 1, depth), :]
                 upper_z = old[field, row, tile, pl.ds(pad + 1, depth), :]
                 lower_y = old[field, row - 1, tile, middle, :]
@@ -425,7 +427,7 @@
             quotients = divide(values, row, tile)
             results = []
             for field in range(fields):
-                value = keep * centers[field][tile] + quotients[field]
+                value = keep * old[field, row, tile, middle, :] + quotients[field]
                 if level > 1:
                     value = value + iterates[0][field, row, tile, middle, :]
                 results.append(value)
@@ -530,7 +532,7 @@
     pairs = []
     for part in range(parts):
         for step in range(steps):
-            beside = (part ^ 1, step) if parts % 2 == 0 else (part, (step + 1) % steps)
+            beside = (part, step ^ 1)
             for slab in range(size):
                 partner = slab + 1 if (slab - first) % 2 == 0 else slab - 1
                 target = (part, step, partner) if 0 <= partner < size else (*beside, slab)

time: 30.8 us -> 30.8 us (level)
  no operation moved by 1% of the time
where the time goes in v9:
time: 30.8 us; the launch traced here: 30.6 us
  starting transfers between devices  14.1 us (46%)
  waiting for transfers between devices  11.3 us (37%)
  Pallas kernels  5.11 us (17%)
    ppermute x4, starting transfers between devices, scatter(): lax.ppermute(block, 'tm', [(t, slot_time(t, d, steps)) for t in range(ste...  6.25 us
    ppermute x3, starting transfers between devices, gather(): result[d] = lax.ppermute(blocks[d], 'tm', pairs)  5.71 us
    pallas_call x8, Pallas kernels, call(): pl.pallas_call(kernel, out_shape=[make(o, jnp.float32) for o in outs], in...  5.11 us
    ppermute x4, waiting for transfers between devices, scatter(): lax.ppermute(block, 'tm', [(t, slot_time(t, d, steps)) for t in range(ste...  4.91 us
    ppermute x3, waiting for transfers between devices, gather(): result[d] = lax.ppermute(blocks[d], 'tm', pairs)  4.84 us
    ppermute x3, starting transfers between devices, swap(): return lax.ppermute(value, names, pairs)  2.16 us
    ppermute x3, waiting for transfers between devices, swap(): return lax.ppermute(value, names, pairs)  1.56 us
  transfers between devices with their start and end apart: 10, of which 6 were waited for; matrix products, arithmetic and copies ran while one was open for 0% of the time, Pallas kernels for 10%

profile of v9, /device:TPU:0, one launch (start us, length us, event | category | flops | bytes accessed | tf_op | source)
XLA Modules:
  0.0 30.6 jit_solution(2530829026704978679)
XLA Ops:
  0.0 1.2 %shard_map.37 = (f32[17,8,128]{2,1,0:T(8,128)S(1)}, f32[17,8,128]{2,1,0:T(8,128)S(1)}, f32[17,8,128]{2,1,0:T(8,128)S(1)}, f32[17,8,128]{2,1,0:T(8,128)S(1)}) custom-call(f32[16,4,1024]{2,1,0:T(4,128)} %bitcast.2), custom_call_target="tpu_custom_call" | custom-call | tf_op jit(solution)/shard_map/pallas_call | solution.py:38
  1.2 3.1 %collective-permute-start = (f32[17,8,128]{2,1,0:T(8,128)S(1)}, f32[17,8,128]{2,1,0:T(8,128)S(1)}, u32[]{:S(2)}, u32[]{:S(2)}) collective-permute-start(f32[17,8,128]{2,1,0:T(8,128)S(1)} %get-tuple-element.32), channel_id=1, source_target_pairs={{4,0},{0,4},{12,8},{8,12},{5,1},{1,5},{13,9},{9,13},{6,2},{2,6},{1... | collective-permute-start | bytes 208904 | tf_op jit(solution)/shard_map/ppermute | solution.py:521
  4.3 2.6 %collective-permute-start.1 = (f32[17,8,128]{2,1,0:T(8,128)S(1)}, f32[17,8,128]{2,1,0:T(8,128)S(1)}, u32[]{:S(2)}, u32[]{:S(2)}) collective-permute-start(f32[17,8,128]{2,1,0:T(8,128)S(1)} %get-tuple-element.33), channel_id=1, source_target_pairs={{8,0},{12,4},{0,8},{4,12},{9,1},{13,5},{1,9},{5,13},{10,2},{14,6},... | collective-permute-start | bytes 208904 | tf_op jit(solution)/shard_map/ppermute | solution.py:521
  6.9 0.0 collective-permute-start.2
  6.9 1.1 %shard_map.38 = (f32[17,8,128]{2,1,0:T(8,128)S(1)}, f32[26,8,128]{2,1,0:T(8,128)S(1)}, f32[3,16,128]{2,1,0:T(8,128)S(1)}) custom-call(f32[16,4,1024]{2,1,0:T(4,128)} %diffusivity.1, f32[3]{0:T(128)} %velocity.1, f32[17,8,128]{2,1,0:T(8,128)S(1)} %get-tuple-element.31.block.refs_0_), custom_call_target="tpu_custom_call" | custom-call | tf_op jit(solution)/shard_map/pallas_call | solution.py:38
  8.0 0.2 shard_map.39
  8.2 0.0 collective-permute-done.refs_1_
  8.3 3.6 %collective-permute-done.1.refs_2_ = f32[17,8,128]{2,1,0:T(8,128)S(1)} collective-permute-done((f32[17,8,128]{2,1,0:T(8,128)S(1)}, f32[17,8,128]{2,1,0:T(8,128)S(1)}, u32[]{:S(2)}, u32[]{:S(2)}) %collective-permute-start.1) | collective-permute-done | bytes 69664 | tf_op jit(solution)/shard_map/ppermute | solution.py:521
  11.8 1.3 %collective-permute-done.2.refs_3_ = f32[17,8,128]{2,1,0:T(8,128)S(1)} collective-permute-done((f32[17,8,128]{2,1,0:T(8,128)S(1)}, f32[17,8,128]{2,1,0:T(8,128)S(1)}, u32[]{:S(2)}, u32[]{:S(2)}) %collective-permute-start.2) | collective-permute-done | bytes 69664 | tf_op jit(solution)/shard_map/ppermute | solution.py:521
  13.1 0.1 collective-permute-start.3
  13.2 0.9 %collective-permute-start.5 = (f32[39,8,128]{2,1,0:T(8,128)S(1)}, f32[39,8,128]{2,1,0:T(8,128)S(1)}, u32[]{:S(2)}, u32[]{:S(2)}) collective-permute-start(f32[39,8,128]{2,1,0:T(8,128)S(1)} %get-tuple-element.45), channel_id=1, source_target_pairs={{0,4},{1,2},{2,1},{3,7},{4,0},{5,6},{6,5},{7,3},{8,12},{9,10},{10,... | collective-permute-start | bytes 479240 | tf_op jit(solution)/shard_map/ppermute | solution.py:543
  14.1 1.2 %collective-permute-start.6 = (f32[26,8,128]{2,1,0:T(8,128)S(1)}, f32[26,8,128]{2,1,0:T(8,128)S(1)}, u32[]{:S(2)}, u32[]{:S(2)}) collective-permute-start(f32[26,8,128]{2,1,0:T(8,128)S(1)} %get-tuple-element.46), channel_id=1, source_target_pairs={{0,4},{1,2},{2,1},{3,7},{4,0},{5,6},{6,5},{7,3},{8,12},{9,10},{10,... | collective-permute-start | bytes 319496 | tf_op jit(solution)/shard_map/ppermute | solution.py:543
  15.3 0.0 collective-permute-done.3.refs_4_
  15.3 1.0 %shard_map.41 = (f32[10,3,16,128]{3,2,1,0:T(8,128)S(1)}, f32[4,10,3,16,128]{4,3,2,1,0:T(8,128)S(1)}, f32[4,10,3,32,128]{4,3,2,1,0:T(8,128)S(1)}, f32[4,10,3,32,1...) custom-call(f32[17,8,128]{2,1,0:T(8,128)S(1)} %get-tuple-element.31., ...), custom_call_target="tpu_custom_call", output_to_operand_aliasing={{0}: (6, {}), {1}: (7, {}), {2}: (8, {}), {3}: (9, {}), {4}... | custom-call | tf_op jit(solution)/shard_map/pallas_call | solution.py:38
  16.3 1.9 %collective-permute-start.4 = (f32[4,16,128]{2,1,0:T(8,128)S(1)}, f32[4,16,128]{2,1,0:T(8,128)S(1)}, u32[]{:S(2)}, u32[]{:S(2)}) collective-permute-start(f32[4,16,128]{2,1,0:T(8,128)S(1)} %get-tuple-element.44), channel_id=1, source_target_pairs={{0,8},{4,12},{8,0},{12,4},{1,9},{5,13},{9,1},{13,5},{2,10},{6,14},... | collective-permute-start | bytes 98312 | tf_op jit(solution)/shard_map/ppermute | solution.py:526
  18.1 1.6 %collective-permute-done.6.refs_1_ = f32[26,8,128]{2,1,0:T(8,128)S(1)} collective-permute-done((f32[26,8,128]{2,1,0:T(8,128)S(1)}, f32[26,8,128]{2,1,0:T(8,128)S(1)}, u32[]{:S(2)}, u32[]{:S(2)}) %collective-permute-start.6) | collective-permute-done | bytes 106528 | tf_op jit(solution)/shard_map/ppermute | solution.py:543
  19.7 0.0 collective-permute-done.5.refs_0_
  19.7 0.8 %shard_map.42 = (f32[10,3,16,128]{3,2,1,0:T(8,128)S(1)}, f32[4,10,3,16,128]{4,3,2,1,0:T(8,128)S(1)}, f32[4,10,3,32,128]{4,3,2,1,0:T(8,128)S(1)}, f32[4,10,3,32,1...) custom-call(f32[39,8,128]{2,1,0:T(8,128)S(1)} %collective-permute-do, ...), custom_call_target="tpu_custom_call", output_to_operand_aliasing={{0}: (3, {}), {1}: (4, {}), {2}: (5, {}), {3}: (6, {}), {4}... | custom-call | tf_op jit(solution)/shard_map/pallas_call | solution.py:38
  20.5 0.7 %collective-permute-done.4.early = f32[4,16,128]{2,1,0:T(8,128)S(1)} collective-permute-done((f32[4,16,128]{2,1,0:T(8,128)S(1)}, f32[4,16,128]{2,1,0:T(8,128)S(1)}, u32[]{:S(2)}, u32[]{:S(2)}) %collective-permute-start.4) | collective-permute-done | bytes 32800 | tf_op jit(solution)/shard_map/ppermute | solution.py:526
  21.2 1.0 %collective-permute-start.7 = (f32[10,16,128]{2,1,0:T(8,128)S(1)}, f32[10,16,128]{2,1,0:T(8,128)S(1)}, u32[]{:S(2)}, u32[]{:S(2)}) collective-permute-start(f32[10,16,128]{2,1,0:T(8,128)S(1)} %shard_map.43), channel_id=1, source_target_pairs={{0,4},{4,0},{8,12},{12,8},{1,5},{5,1},{9,13},{13,9},{2,6},{6,2},{1... | collective-permute-start | bytes 245768 | tf_op jit(solution)/shard_map/ppermute | solution.py:526
  22.2 1.8 %collective-permute-start.8 = (f32[6,16,128]{2,1,0:T(8,128)S(1)}, f32[6,16,128]{2,1,0:T(8,128)S(1)}, u32[]{:S(2)}, u32[]{:S(2)}) collective-permute-start(f32[6,16,128]{2,1,0:T(8,128)S(1)} %get-tuple-element.55), channel_id=1, source_target_pairs={{0,8},{4,12},{8,0},{12,4},{1,9},{5,13},{9,1},{13,5},{2,10},{6,14},... | collective-permute-start | bytes 147464 | tf_op jit(solution)/shard_map/ppermute | solution.py:526
  24.0 1.6 %collective-permute-start.9 = (f32[6,16,128]{2,1,0:T(8,128)S(1)}, f32[6,16,128]{2,1,0:T(8,128)S(1)}, u32[]{:S(2)}, u32[]{:S(2)}) collective-permute-start(f32[6,16,128]{2,1,0:T(8,128)S(1)} %get-tuple-element.56), channel_id=1, source_target_pairs={{0,12},{4,8},{8,4},{12,0},{1,13},{5,9},{9,5},{13,1},{2,14},{6,10},... | collective-permute-start | bytes 147464 | tf_op jit(solution)/shard_map/ppermute | solution.py:526
  25.6 1.6 %collective-permute-done.8.refs_2_ = f32[6,16,128]{2,1,0:T(8,128)S(1)} collective-permute-done((f32[6,16,128]{2,1,0:T(8,128)S(1)}, f32[6,16,128]{2,1,0:T(8,128)S(1)}, u32[]{:S(2)}, u32[]{:S(2)}) %collective-permute-start.8) | collective-permute-done | bytes 49184 | tf_op jit(solution)/shard_map/ppermute | solution.py:526
  27.2 2.6 %collective-permute-done.9.refs_3_ = f32[6,16,128]{2,1,0:T(8,128)S(1)} collective-permute-done((f32[6,16,128]{2,1,0:T(8,128)S(1)}, f32[6,16,128]{2,1,0:T(8,128)S(1)}, u32[]{:S(2)}, u32[]{:S(2)}) %collective-permute-start.9) | collective-permute-done | bytes 49184 | tf_op jit(solution)/shard_map/ppermute | solution.py:526
  29.8 0.0 collective-permute-done.7.refs_1_
  29.8 0.8 %shard_map.44 = f32[16,4,1024]{2,1,0:T(4,128)} custom-call(f32[2,16,128]{2,1,0:T(8,128)S(1)} %get-tuple-element.43.own_early, f32[4,16,128]{2,1,0:T(8,128)S(1)} %collective-permute-done.4.early, f32[6,16,128]{2,1,0:T(8,128)S(1)} %get-tuple-element.53.refs_0_, f32[10,16,128]{2,1,0:T(8,128)S(1)} %collective-permute-done.7.refs_1_, ...), custom_call_target="tpu_custom_call" | custom-call | tf_op jit(solution)/shard_map/pallas_call | solution.py:38
  (2 shorter events, 0.0 us)
Async XLA Ops:
  1.2 7.1 %collective-permute-start = (f32[17,8,128]{2,1,0:T(8,128)S(1)}, f32[17,8,128]{2,1,0:T(8,128)S(1)}, u32[]{:S(2)}, u32[]{:S(2)}) collective-permute-start(f32[17,8,128]{2,1,0:T(8,128)S(1)} %get-tuple-element.32), channel_id=1, source_target_pairs={{4,0},{0,4},{12,8},{8,12},{5,1},{1,5},{13,9},{9,13},{6,2},{2,6},{1... | collective-permute-start | bytes 208904 | tf_op jit(solution)/shard_map/ppermute | solution.py:521
  4.3 7.5 %collective-permute-start.1 = (f32[17,8,128]{2,1,0:T(8,128)S(1)}, f32[17,8,128]{2,1,0:T(8,128)S(1)}, u32[]{:S(2)}, u32[]{:S(2)}) collective-permute-start(f32[17,8,128]{2,1,0:T(8,128)S(1)} %get-tuple-element.33), channel_id=1, source_target_pairs={{8,0},{12,4},{0,8},{4,12},{9,1},{13,5},{1,9},{5,13},{10,2},{14,6},... | collective-permute-start | bytes 208904 | tf_op jit(solution)/shard_map/ppermute | solution.py:521
  6.9 6.2 %collective-permute-start.2 = (f32[17,8,128]{2,1,0:T(8,128)S(1)}, f32[17,8,128]{2,1,0:T(8,128)S(1)}, u32[]{:S(2)}, u32[]{:S(2)}) collective-permute-start(f32[17,8,128]{2,1,0:T(8,128)S(1)} %get-tuple-element.34), channel_id=1, source_target_pairs={{12,0},{8,4},{4,8},{0,12},{13,1},{9,5},{5,9},{1,13},{14,2},{10,6},... | collective-permute-start | bytes 208904 | tf_op jit(solution)/shard_map/ppermute | solution.py:521
  13.1 2.2 %collective-permute-start.3 = (f32[65,8,128]{2,1,0:T(8,128)S(1)}, f32[65,8,128]{2,1,0:T(8,128)S(1)}, u32[]{:S(2)}, u32[]{:S(2)}) collective-permute-start(f32[65,8,128]{2,1,0:T(8,128)S(1)} %get-tuple-element.37), channel_id=1, source_target_pairs={{0,1},{1,0},{2,3},{3,2},{4,5},{5,4},{6,7},{7,6},{8,9},{9,8},{10,11... | collective-permute-start | bytes 798728 | tf_op jit(solution)/shard_map/ppermute | solution.py:543
  13.2 6.5 %collective-permute-start.5 = (f32[39,8,128]{2,1,0:T(8,128)S(1)}, f32[39,8,128]{2,1,0:T(8,128)S(1)}, u32[]{:S(2)}, u32[]{:S(2)}) collective-permute-start(f32[39,8,128]{2,1,0:T(8,128)S(1)} %get-tuple-element.45), channel_id=1, source_target_pairs={{0,4},{1,2},{2,1},{3,7},{4,0},{5,6},{6,5},{7,3},{8,12},{9,10},{10,... | collective-permute-start | bytes 479240 | tf_op jit(solution)/shard_map/ppermute | solution.py:543
  14.1 5.6 %collective-permute-start.6 = (f32[26,8,128]{2,1,0:T(8,128)S(1)}, f32[26,8,128]{2,1,0:T(8,128)S(1)}, u32[]{:S(2)}, u32[]{:S(2)}) collective-permute-start(f32[26,8,128]{2,1,0:T(8,128)S(1)} %get-tuple-element.46), channel_id=1, source_target_pairs={{0,4},{1,2},{2,1},{3,7},{4,0},{5,6},{6,5},{7,3},{8,12},{9,10},{10,... | collective-permute-start | bytes 319496 | tf_op jit(solution)/shard_map/ppermute | solution.py:543
  16.3 4.9 %collective-permute-start.4 = (f32[4,16,128]{2,1,0:T(8,128)S(1)}, f32[4,16,128]{2,1,0:T(8,128)S(1)}, u32[]{:S(2)}, u32[]{:S(2)}) collective-permute-start(f32[4,16,128]{2,1,0:T(8,128)S(1)} %get-tuple-element.44), channel_id=1, source_target_pairs={{0,8},{4,12},{8,0},{12,4},{1,9},{5,13},{9,1},{13,5},{2,10},{6,14},... | collective-permute-start | bytes 98312 | tf_op jit(solution)/shard_map/ppermute | solution.py:526
  21.2 8.6 %collective-permute-start.7 = (f32[10,16,128]{2,1,0:T(8,128)S(1)}, f32[10,16,128]{2,1,0:T(8,128)S(1)}, u32[]{:S(2)}, u32[]{:S(2)}) collective-permute-start(f32[10,16,128]{2,1,0:T(8,128)S(1)} %shard_map.43), channel_id=1, source_target_pairs={{0,4},{4,0},{8,12},{12,8},{1,5},{5,1},{9,13},{13,9},{2,6},{6,2},{1... | collective-permute-start | bytes 245768 | tf_op jit(solution)/shard_map/ppermute | solution.py:526
  22.2 5.0 %collective-permute-start.8 = (f32[6,16,128]{2,1,0:T(8,128)S(1)}, f32[6,16,128]{2,1,0:T(8,128)S(1)}, u32[]{:S(2)}, u32[]{:S(2)}) collective-permute-start(f32[6,16,128]{2,1,0:T(8,128)S(1)} %get-tuple-element.55), channel_id=1, source_target_pairs={{0,8},{4,12},{8,0},{12,4},{1,9},{5,13},{9,1},{13,5},{2,10},{6,14},... | collective-permute-start | bytes 147464 | tf_op jit(solution)/shard_map/ppermute | solution.py:526
  24.0 5.9 %collective-permute-start.9 = (f32[6,16,128]{2,1,0:T(8,128)S(1)}, f32[6,16,128]{2,1,0:T(8,128)S(1)}, u32[]{:S(2)}, u32[]{:S(2)}) collective-permute-start(f32[6,16,128]{2,1,0:T(8,128)S(1)} %get-tuple-element.56), channel_id=1, source_target_pairs={{0,12},{4,8},{8,4},{12,0},{1,13},{5,9},{9,5},{13,1},{2,14},{6,10},... | collective-permute-start | bytes 147464 | tf_op jit(solution)/shard_map/ppermute | solution.py:526
